TPU v7x, 128 devices: a whole 4x4x4 slice. The times are simulated.
128 devices in a mesh: gx: 4 (over z), gy: 4 (over x), gz: 8 (over y, core).
Axes of the slice: x: 4, y: 4, z: 4, core: 2. Of those that a mesh axis runs over, the one named last changes fastest.
Arguments:
- pressure: float32 [128, 128, 1024], P('gx', 'gy', 'gz'), may hold values from -6 to 6
- saturation: float32 [2, 128, 128, 1024], P(None, 'gx', 'gy', 'gz'), may hold values from 0.05 to 0.45
- old_saturation: float32 [2, 128, 128, 1024], P(None, 'gx', 'gy', 'gz'), may hold values from 0.05 to 0.45
- permeability: float32 [128, 128, 1024], P('gx', 'gy', 'gz'), may hold values from 0.1 to 10
- storage: float32 [128, 128, 1024], P('gx', 'gy', 'gz'), may hold values from 0.3 to 3
- cell_mask: int32 [128, 128, 1024], P('gx', 'gy', 'gz'), may hold values from 0 to 1, as said below
- row_owner: int32 [128, 128, 8], P('gx', 'gy', 'gz'), may hold values from -1 to 127, as said below
- row_slot: int32 [128, 128, 8], P('gx', 'gy', 'gz'), may hold values from -1 to 639, as said below
Outputs:
- update: float32 [3, 81920, 128], P(None, ('gx', 'gy', 'gz'))
Inputs may be any that keep to these rules, and one draw needn't show every extreme that they name: `cell_mask`: A block row of 128 cells without an active cell has row_owner -1; every other block row has an owner. `row_owner`: -1 exactly for block rows without active cells; every owner holds exactly 640 block rows; at most 8 block rows of one device's tile go to one owner, and in every draw some tile sends exactly 8 to every owner. `row_slot`: -1 exactly where row_owner is -1; the places of one owner's block rows are 0 to 639, each taken once.
All inputs are finite; a program needn't handle non-finite values.
Results may differ from a plain program's by a relative error of at most 0.0003.
Values sent between devices are 32-bit elements; how exact they have to be, the bound alone decides.
No kernel may reach another device: no remote copies, remote signals or barrier semaphores. Data moves between devices by JAX's collectives and lax.ppermute only.
A program may use at most 128 MiB of HBM per device.

v0:
```python
import jax
import jax.numpy as jnp
from jax import lax
from jax.sharding import PartitionSpec as P

ITERS = 2
SWEEPS = 4
SLOTS = 640


VISCOSITY = (0.5, 2.0, 0.25)
COMPRESS = (0.5, 1.0, 2.0)


def padded_2(array, sides, width):
    for axis, dim in sides:
        size, length = (lax.axis_size(axis), array.shape[dim])
        up = [(i, (i + 1) % size) for i in range(size - 1)]
        down = [(j, i) for i, j in up]
        last = lax.slice_in_dim(array, length - width, length, axis=dim)
        leading = lax.slice_in_dim(array, 0, width, axis=dim)
        before = lax.ppermute(last, axis, up)
        after = lax.ppermute(leading, axis, down)
        array = jnp.concatenate([before, array, after], axis=dim)
    return array


def shifted(padded):
    return [
        padded[..., 2:, 1:-1, 1:-1],
        padded[..., :-2, 1:-1, 1:-1],
        padded[..., 1:-1, 2:, 1:-1],
        padded[..., 1:-1, :-2, 1:-1],
        padded[..., 1:-1, 1:-1, 2:],
        padded[..., 1:-1, 1:-1, :-2],
    ]


def phases_of(saturation):
    return jnp.stack([saturation[0], 1.0 - saturation[0] - saturation[1], saturation[1]])


def mobilities(saturation):
    phase_sat = phases_of(saturation)
    viscous = jnp.array(VISCOSITY, jnp.float32).reshape(3, 1, 1, 1)
    return phase_sat * phase_sat / viscous


def assemble(pressure, saturation, old_saturation, conduct, storage, active, mobility, padded):
    flux_sum = jnp.zeros_like(mobility)
    couple_list = []
    for neighbour in shifted(padded):
        transmit = 2.0 * conduct * neighbour[1] / jnp.maximum(conduct + neighbour[1], 0.5)
        upwind = jnp.where(pressure >= neighbour[0], mobility, neighbour[2:])
        weight = transmit * upwind
        couple_list.append(weight)
        flux_sum = flux_sum + weight * (pressure - neighbour[0])
    outflow = couple_list[0]
    for face_index in range(1, 6):
        outflow = outflow + couple_list[face_index]
    change = saturation - old_saturation
    phase_change = jnp.stack([change[0], -change[0] - change[1], change[1]])
    compress = jnp.array(COMPRESS, jnp.float32).reshape(3, 1, 1, 1)
    press_column = active * (storage * compress * phases_of(saturation) + outflow) + (1.0 - active)
    sat_scale = active * storage + (1.0 - active)
    right_side = -(active * storage * phase_change + flux_sum)
    return (right_side, press_column, sat_scale, couple_list)


def precondition(right_side, press_column, sat_scale, phase_terms, press_terms):
    press_total = jnp.sum(press_column, axis=0)
    sol_press = jnp.zeros_like(sat_scale)
    sol_water = jnp.zeros_like(sat_scale)
    sol_gas = jnp.zeros_like(sat_scale)
    for outer_index in range(ITERS):
        if outer_index == 0:
            residual = right_side
        else:
            applied = (
                press_column * sol_press
                + sat_scale * jnp.stack([sol_water, -sol_water - sol_gas, sol_gas])
                - phase_terms(sol_press)
            )
            residual = right_side - applied
        reduced = jnp.sum(residual, axis=0)
        correction = reduced / press_total
        for sweep_index in range(SWEEPS - 1):
            correction = (
                correction
                + (reduced - press_total * correction + press_terms(correction)) / press_total
            )
        second = residual - (press_column * correction - phase_terms(correction))
        lifted = jnp.sum(second, axis=0) / press_total
        sol_press = sol_press + correction + lifted
        sol_water = sol_water + (second[0] - press_column[0] * lifted) / sat_scale
        sol_gas = sol_gas + (second[2] - press_column[2] * lifted) / sat_scale
    return jnp.stack([sol_press, sol_water, sol_gas])


def neighbour_list(values):
    padded = padded_2(values, (("gx", 0), ("gy", 1), ("gz", 2)), 1)
    return shifted(padded)


def weighted_sum(weights, nearby):
    summed = weights[0] * nearby[0]
    for face_index in range(1, 6):
        summed = summed + weights[face_index] * nearby[face_index]
    return summed


def placement_rows(owner_rows, devices, capacity):
    matches = (owner_rows[:, None] == jnp.arange(devices, dtype=jnp.int32)[None, :]).astype(
        jnp.int32
    )
    earlier = jnp.cumsum(matches, axis=0) - matches
    within = jnp.sum(earlier * matches, axis=1)
    return jnp.where(owner_rows >= 0, owner_rows * capacity + within, devices * capacity)


def slot_sources(target, total_slots):
    row_count = target.shape[0]
    order = jnp.argsort(target, stable=True)
    sorted_target = target[order]
    wanted = jnp.arange(total_slots, dtype=jnp.int32)
    found = jnp.minimum(jnp.searchsorted(sorted_target, wanted), row_count - 1)
    present = sorted_target[found] == wanted
    return (order[found], present)


def pack_rows(values, sources, present):
    picked = values[:, sources]
    return jnp.where(present[None, :, None], picked, 0.0)


def slot_order(places):
    order = jnp.argsort(places, stable=True)
    return order[places.shape[0] - SLOTS :]


def to_slots(values, order):
    return values[:, order]


def move_rows(values, places, devices, capacity):
    field_count, total_slots, line_len = values.shape
    got_values, got_places = (
        lax.all_to_all(
            values.reshape(field_count, devices, capacity, line_len),
            ("gx", "gy", "gz"),
            split_axis=1,
            concat_axis=1,
            tiled=True,
        ),
        lax.all_to_all(
            places.reshape(1, devices, capacity),
            ("gx", "gy", "gz"),
            split_axis=1,
            concat_axis=1,
            tiled=True,
        ),
    )
    return (got_values.reshape(field_count, total_slots, line_len), got_places.reshape(total_slots))


def body(
    pressure, saturation, old_saturation, permeability, storage, cell_mask, row_owner, row_slot
):
    active = cell_mask.astype(jnp.float32)
    conduct = permeability * active
    mobility = mobilities(saturation)
    fields = jnp.concatenate([pressure[None], conduct[None], mobility], axis=0)
    padded = padded_2(fields, (("gx", 1), ("gy", 2), ("gz", 3)), 1)
    right_side, press_column, sat_scale, couple = assemble(
        pressure, saturation, old_saturation, conduct, storage, active, mobility, padded
    )
    press_couple = [jnp.sum(weight, axis=0) for weight in couple]
    span_first, span_second, line_len = pressure.shape
    row_count = span_first * span_second
    devices = lax.axis_size(("gx", "gy", "gz"))
    capacity = row_count // devices
    total_slots = devices * capacity
    owner_rows = row_owner.reshape(row_count)
    slot_rows = row_slot.reshape(row_count)
    target = placement_rows(owner_rows, devices, capacity)
    sources, present = slot_sources(target, total_slots)
    places_out = jnp.where(present, slot_rows[sources], -1)

    def tile_phase(values):
        return weighted_sum(couple, neighbour_list(values))

    def tile_press(values):
        return weighted_sum(press_couple, neighbour_list(values))

    solution = precondition(right_side, press_column, sat_scale, tile_phase, tile_press)
    send_buffer = pack_rows(solution.reshape(3, row_count, line_len), sources, present)
    got_values, got_places = move_rows(send_buffer, places_out, devices, capacity)
    return to_slots(got_values, slot_order(got_places))


def solution(mesh):
    placed = (
        P("gx", "gy", "gz"),
        P(None, "gx", "gy", "gz"),
        P(None, "gx", "gy", "gz"),
        P("gx", "gy", "gz"),
        P("gx", "gy", "gz"),
        P("gx", "gy", "gz"),
        P("gx", "gy", "gz"),
        P("gx", "gy", "gz"),
    )
    return jax.shard_map(
        body,
        mesh=mesh,
        in_specs=placed,
        out_specs=P(None, ("gx", "gy", "gz"), None),
        check_vma=False,
    )
```

profile of v0, /device:TPU:0, one launch (start us, length us, event | category | flops | bytes accessed | tf_op | source)
XLA Modules:
  0.0 533.8 jit_solution(4998828787328166570)
XLA Ops:
  5.5 4.6 collective-permute-start.1
  13.6 4.6 collective-permute-start.3
  48.0 10.0 %pad_maximum_fusion = (f32[5,34,34,129]{3,2,1,0:T(8,128)S(1)}, f32[5,34,34,129]{3,2,1,0:T(8,128)S(1)}) fusion(f32[5,34,34,1]{3,2,1,0:T(8,128)} %copy.164, f32[5,34,1,128]{3,2,1,0:T(1,128)S(1)} %collective-permute-done.2, f32[5,1,32,128]{3,2,1,0:T(8,128)S(1)} %collective-permute-done, f32[3,32,32,128]{3,2,1,0:T(8,128)S(1)} %multiply_multiply_fusion, ...), kind=kLoop, calls=%fused_computation.13 | loop fusion | flops 10438680 | bytes 8970560 | tf_op jit(solution)/shard_map/concatenate | solution.py:24
  75.3 4.9 collective-permute-start.7
  83.0 4.9 collective-permute-start.9
  106.4 4.8 collective-permute-start.13
  113.9 4.8 collective-permute-start.15
  138.4 4.8 collective-permute-start.19
  146.0 4.8 collective-permute-start.21
  170.4 4.8 collective-permute-start.25
  178.1 4.8 collective-permute-start.27
  199.7 6.2 %fusion.128 = (f32[32,32,128]{2,1,0:T(8,128)S(1)}, f32[3,32,32,128]{3,2,1,0:T(8,128)S(1)}) fusion(f32[3,32,32,128]{3,2,1,0:T(8,128)S(1)} %copy-done.4, f32[32,32,128]{2,1,0:T(8,128)S(1)} %get-tuple-element.205, f32[3,32,32,128]{3,2,1,0:T(8,128)S(1)} %copy-done.2, f32[32,32,128]{2,1,0:T(8,128)S(1)} %get-tuple-element.204, f32[3,32,32,128]{3,2,1,0:T(8,128)} %copy-done.10, ...), kind=kLoop, calls=%fused_computation.401 | loop fusion | flops 6160384 | bytes 18350080 | tf_op jit(solution)/shard_map/reduce_sum | solution.py:93
  208.8 4.6 collective-permute-start.31
  216.2 4.6 collective-permute-start.33
  240.4 6.8 %fusion.16 = f32[32,32,128]{2,1,0:T(8,128)S(1)} fusion(f32[3,32,32,128]{3,2,1,0:T(8,128)S(1)} %copy-done.5, f32[3,32,32,128]{3,2,1,0:T(8,128)S(1)} %copy-done.2, f32[3,32,32,128]{3,2,1,0:T(8,128)} %copy-done.10, f32[3,32,32,128]{3,2,1,0:T(8,128)S(1)} %copy-done.8, f32[3,32,32,128]{3,2,1,0:T(8,128)} %copy-done.11, f32[3,32,32,128]{3,2,1,0:T(8,128)} %copy-done.12, ...), kind=kLoop, calls=%fused_computation.57 | loop fusion | flops 7733248 | bytes 18874368 | tf_op jit(solution)/shard_map/reduce_sum | solution.py:85
  250.2 4.6 collective-permute-start.37
  258.5 4.6 collective-permute-start.39
  279.7 4.6 fusion.55
  285.7 4.7 collective-permute-start.43
  297.1 4.6 collective-permute-start.45
  316.7 50.7 %while.24 = (s32[]{:T(128)}, u32[1024]{0:T(1024)S(1)}, u32[1024]{0:T(1024)S(1)}, s32[1024]{0:T(1024)S(1)}, s32[]{:T(128)}, /*index=5*/s32[]{:T(128)}, s32[]{}) while((s32[]{:T(128)}, u32[1024]{0:T(1024)S(1)}, u32[1024]{0:T(1024)S(1)}, s32[1024]{0:T(1024)S(1)}, s32[]{:T(128)}, /*index=5*/s32[]{:T(128)}, s32[]{}) %tuple.128), condition=%wide.region_5.6_spmd.clone, body=%wide.region_4.5_spmd.clone.sunk | while | flops 19460 | bytes 63597 | solution.py:126
  369.8 5.0 fusion.41
  376.9 4.6 collective-permute-start.49
  388.4 4.5 collective-permute-start.51
  417.0 5.0 fusion.27
  424.2 4.5 collective-permute-start.55
  429.4 16.9 %all-to-all-start.1 = ((s32[1,128,8]{2,0,1:T(1,128)}), s32[1,128,8]{2,0,1:T(1,128)S(1)}, u32[]{:S(2)}, u32[]{:S(2)}) async-start(s32[1,128,8]{2,0,1:T(1,128)} %bitcast.34), calls=%async_computation.1 | async-start | bytes 131072 | tf_op jit(solution)/shard_map/all_to_all | solution.py:155
  448.8 4.5 collective-permute-start.57
  472.0 6.5 %fusion.124 = (f32[32,32,128]{2,1,0:T(8,128)S(1)}, f32[3,32,32,128]{3,2,1,0:T(8,128)S(1)}) fusion(f32[3,32,32,128]{3,2,1,0:T(8,128)S(1)} %copy-done.6, f32[32,32,128]{2,1,0:T(8,128)S(1)} %get-tuple-element.201, f32[3,32,32,128]{3,2,1,0:T(8,128)S(1)} %copy-done.2, f32[32,32,128]{2,1,0:T(8,128)S(1)} %get-tuple-element.200, f32[3,32,32,128]{3,2,1,0:T(8,128)} %copy-done.10, ...), kind=kLoop, calls=%fused_computation.400 | loop fusion | flops 13238272 | bytes 24117248 | tf_op jit(solution)/shard_map/reduce_sum | solution.py:93
  480.6 7.9 %gather_fusion.4 = f32[1024,3,128]{2,1,0:T(4,128)} fusion(f32[3,1024,128]{2,0,1:T(4,128)S(1)} %pad_maximum_fusion.2, s32[1024]{0:T(1024)S(1)} %broadcast_clamp_fusion.1), kind=kCustom, calls=%fused_computation.4 | custom fusion | bytes 3149824 | tf_op jit(solution)/shard_map/gather | solution.py:132
  491.5 11.1 %all-to-all-start = ((f32[3,128,8,128]{3,2,0,1:T(8,128)}), f32[3,128,8,128]{3,2,0,1:T(8,128)S(1)}, u32[]{:S(2)}, u32[]{:S(2)}) async-start(f32[3,128,8,128]{3,2,0,1:T(8,128)} %copy_select_fusion), calls=%async_computation | async-start | bytes 3145728 | tf_op jit(solution)/shard_map/all_to_all | solution.py:148
  507.9 19.5 %all-to-all-done = f32[3,128,8,128]{3,2,0,1:T(8,128)S(1)} async-done(((f32[3,128,8,128]{3,2,0,1:T(8,128)}), f32[3,128,8,128]{3,2,0,1:T(8,128)S(1)}, u32[]{:S(2)}, u32[]{:S(2)}) %all-to-all-start) | async-done | bytes 1572896 | tf_op jit(solution)/shard_map/all_to_all | solution.py:148
  (473 shorter events, 338.1 us)
Async XLA Ops:
  5.5 6.6 %collective-permute-start.1 = (f32[5,1,32,128]{3,2,1,0:T(8,128)S(1)}, f32[5,1,32,128]{3,2,1,0:T(8,128)S(1)}, u32[]{:S(2)}, u32[]{:S(2)}) collective-permute-start(f32[5,1,32,128]{3,2,1,0:T(8,128)S(1)} %get-tuple-element.160), channel_id=1, source_target_pairs={{0,32},{32,64},{64,96},{1,33},{33,65},{65,97},{2,34},{34,66},{66,9... | collective-permute-start | bytes 245768 | tf_op jit(solution)/shard_map/ppermute | solution.py:22
  12.3 7.9 %collective-permute-start.2 = (f32[5,34,1,128]{3,2,1,0:T(1,128)S(1)}, f32[5,34,1,128]{3,2,1,0:T(1,128)S(1)}, u32[]{:S(2)}, u32[]{:S(2)}) collective-permute-start(f32[5,34,1,128]{3,2,1,0:T(1,128)S(1)} %get-tuple-element.156), channel_id=1, source_target_pairs={{8,0},{16,8},{24,16},{9,1},{17,9},{25,17},{10,2},{18,10},{26,18},{... | collective-permute-start | bytes 261128 | tf_op jit(solution)/shard_map/ppermute | solution.py:23
  13.6 6.6 %collective-permute-start.3 = (f32[5,34,1,128]{3,2,1,0:T(1,128)S(1)}, f32[5,34,1,128]{3,2,1,0:T(1,128)S(1)}, u32[]{:S(2)}, u32[]{:S(2)}) collective-permute-start(f32[5,34,1,128]{3,2,1,0:T(1,128)S(1)} %get-tuple-element.155), channel_id=1, source_target_pairs={{0,8},{8,16},{16,24},{1,9},{9,17},{17,25},{2,10},{10,18},{18,26},{... | collective-permute-start | bytes 261128 | tf_op jit(solution)/shard_map/ppermute | solution.py:22
  29.0 12.0 %collective-permute-start.4 = (f32[5,34,34,1]{2,3,1,0:T(1,128)}, f32[5,34,34,1]{2,3,1,0:T(1,128)}, u32[]{:S(2)}, u32[]{:S(2)}) collective-permute-start(f32[5,34,34,1]{2,3,1,0:T(1,128)} %copy.225), channel_id=1, source_target_pairs={{1,0},{2,1},{3,2},{4,3},{5,4},{6,5},{7,6},{9,8},{10,9},{11,10},{12... | collective-permute-start | bytes 69368 | tf_op jit(solution)/shard_map/ppermute | solution.py:23
  33.8 10.8 %collective-permute-start.5 = (f32[5,34,34,1]{2,3,1,0:T(1,128)}, f32[5,34,34,1]{2,3,1,0:T(1,128)}, u32[]{:S(2)}, u32[]{:S(2)}) collective-permute-start(f32[5,34,34,1]{2,3,1,0:T(1,128)} %copy.226), channel_id=1, source_target_pairs={{0,1},{1,2},{2,3},{3,4},{4,5},{5,6},{6,7},{8,9},{9,10},{10,11},{11... | collective-permute-start | bytes 69368 | tf_op jit(solution)/shard_map/ppermute | solution.py:22
  176.8 7.3 %collective-permute-start.26 = (f32[34,1,128]{2,1,0:T(1,128)S(1)}, f32[34,1,128]{2,1,0:T(1,128)S(1)}, u32[]{:S(2)}, u32[]{:S(2)}) collective-permute-start(f32[34,1,128]{2,1,0:T(1,128)S(1)} %get-tuple-element.217), channel_id=1, source_target_pairs={{8,0},{16,8},{24,16},{9,1},{17,9},{25,17},{10,2},{18,10},{26,18},{... | collective-permute-start | bytes 52232 | tf_op jit(solution)/shard_map/ppermute | solution.py:23
  187.0 7.9 %collective-permute-start.28 = (f32[34,34,1]{1,2,0:T(1,128)S(1)}, f32[34,34,1]{1,2,0:T(1,128)S(1)}, u32[]{:S(2)}, u32[]{:S(2)}) collective-permute-start(f32[34,34,1]{1,2,0:T(1,128)S(1)} %copy.233), channel_id=1, source_target_pairs={{1,0},{2,1},{3,2},{4,3},{5,4},{6,5},{7,6},{9,8},{10,9},{11,10},{12... | collective-permute-start | bytes 13880 | tf_op jit(solution)/shard_map/ppermute | solution.py:23
  188.6 7.5 %collective-permute-start.29 = (f32[34,34,1]{1,2,0:T(1,128)S(1)}, f32[34,34,1]{1,2,0:T(1,128)S(1)}, u32[]{:S(2)}, u32[]{:S(2)}) collective-permute-start(f32[34,34,1]{1,2,0:T(1,128)S(1)} %copy.234), channel_id=1, source_target_pairs={{0,1},{1,2},{2,3},{3,4},{4,5},{5,6},{6,7},{8,9},{9,10},{10,11},{11... | collective-permute-start | bytes 13880 | tf_op jit(solution)/shard_map/ppermute | solution.py:22
  214.9 8.1 %collective-permute-start.32 = (f32[34,1,128]{2,1,0:T(1,128)S(1)}, f32[34,1,128]{2,1,0:T(1,128)S(1)}, u32[]{:S(2)}, u32[]{:S(2)}) collective-permute-start(f32[34,1,128]{2,1,0:T(1,128)S(1)} %get-tuple-element.215), channel_id=1, source_target_pairs={{8,0},{16,8},{24,16},{9,1},{17,9},{25,17},{10,2},{18,10},{26,18},{... | collective-permute-start | bytes 52232 | tf_op jit(solution)/shard_map/ppermute | solution.py:23
  216.2 6.8 %collective-permute-start.33 = (f32[34,1,128]{2,1,0:T(1,128)S(1)}, f32[34,1,128]{2,1,0:T(1,128)S(1)}, u32[]{:S(2)}, u32[]{:S(2)}) collective-permute-start(f32[34,1,128]{2,1,0:T(1,128)S(1)} %get-tuple-element.214), channel_id=1, source_target_pairs={{0,8},{8,16},{16,24},{1,9},{9,17},{17,25},{2,10},{10,18},{18,26},{... | collective-permute-start | bytes 52232 | tf_op jit(solution)/shard_map/ppermute | solution.py:22
  225.8 9.7 %collective-permute-start.34 = (f32[34,34,1]{1,2,0:T(1,128)S(1)}, f32[34,34,1]{1,2,0:T(1,128)S(1)}, u32[]{:S(2)}, u32[]{:S(2)}) collective-permute-start(f32[34,34,1]{1,2,0:T(1,128)S(1)} %copy.235), channel_id=1, source_target_pairs={{1,0},{2,1},{3,2},{4,3},{5,4},{6,5},{7,6},{9,8},{10,9},{11,10},{12... | collective-permute-start | bytes 13880 | tf_op jit(solution)/shard_map/ppermute | solution.py:23
  228.5 8.2 %collective-permute-start.35 = (f32[34,34,1]{1,2,0:T(1,128)S(1)}, f32[34,34,1]{1,2,0:T(1,128)S(1)}, u32[]{:S(2)}, u32[]{:S(2)}) collective-permute-start(f32[34,34,1]{1,2,0:T(1,128)S(1)} %copy.236), channel_id=1, source_target_pairs={{0,1},{1,2},{2,3},{3,4},{4,5},{5,6},{6,7},{8,9},{9,10},{10,11},{11... | collective-permute-start | bytes 13880 | tf_op jit(solution)/shard_map/ppermute | solution.py:22
  257.2 9.1 %collective-permute-start.38 = (f32[34,1,128]{2,1,0:T(1,128)S(1)}, f32[34,1,128]{2,1,0:T(1,128)S(1)}, u32[]{:S(2)}, u32[]{:S(2)}) collective-permute-start(f32[34,1,128]{2,1,0:T(1,128)S(1)} %get-tuple-element.213), channel_id=1, source_target_pairs={{8,0},{16,8},{24,16},{9,1},{17,9},{25,17},{10,2},{18,10},{26,18},{... | collective-permute-start | bytes 52232 | tf_op jit(solution)/shard_map/ppermute | solution.py:23
  258.5 7.8 %collective-permute-start.39 = (f32[34,1,128]{2,1,0:T(1,128)S(1)}, f32[34,1,128]{2,1,0:T(1,128)S(1)}, u32[]{:S(2)}, u32[]{:S(2)}) collective-permute-start(f32[34,1,128]{2,1,0:T(1,128)S(1)} %get-tuple-element.212), channel_id=1, source_target_pairs={{0,8},{8,16},{16,24},{1,9},{9,17},{17,25},{2,10},{10,18},{18,26},{... | collective-permute-start | bytes 52232 | tf_op jit(solution)/shard_map/ppermute | solution.py:22
  270.1 7.2 %collective-permute-start.41 = (f32[34,34,1]{1,2,0:T(1,128)S(1)}, f32[34,34,1]{1,2,0:T(1,128)S(1)}, u32[]{:S(2)}, u32[]{:S(2)}) collective-permute-start(f32[34,34,1]{1,2,0:T(1,128)S(1)} %copy.238), channel_id=1, source_target_pairs={{0,1},{1,2},{2,3},{3,4},{4,5},{5,6},{6,7},{8,9},{9,10},{10,11},{11... | collective-permute-start | bytes 13880 | tf_op jit(solution)/shard_map/ppermute | solution.py:22
  284.4 10.4 %collective-permute-start.42 = (f32[1,32,128]{2,1,0:T(8,128)S(1)}, f32[1,32,128]{2,1,0:T(8,128)S(1)}, u32[]{:S(2)}, u32[]{:S(2)}) collective-permute-start(f32[1,32,128]{2,1,0:T(8,128)S(1)} %get-tuple-element.235), channel_id=1, source_target_pairs={{32,0},{64,32},{96,64},{33,1},{65,33},{97,65},{34,2},{66,34},{98,6... | collective-permute-start | bytes 49160 | tf_op jit(solution)/shard_map/ppermute | solution.py:23
  285.7 9.1 %collective-permute-start.43 = (f32[1,32,128]{2,1,0:T(8,128)S(1)}, f32[1,32,128]{2,1,0:T(8,128)S(1)}, u32[]{:S(2)}, u32[]{:S(2)}) collective-permute-start(f32[1,32,128]{2,1,0:T(8,128)S(1)} %get-tuple-element.234), channel_id=1, source_target_pairs={{0,32},{32,64},{64,96},{1,33},{33,65},{65,97},{2,34},{34,66},{66,9... | collective-permute-start | bytes 49160 | tf_op jit(solution)/shard_map/ppermute | solution.py:22
  295.8 10.4 %collective-permute-start.44 = (f32[34,1,128]{2,1,0:T(1,128)S(1)}, f32[34,1,128]{2,1,0:T(1,128)S(1)}, u32[]{:S(2)}, u32[]{:S(2)}) collective-permute-start(f32[34,1,128]{2,1,0:T(1,128)S(1)} %get-tuple-element.211), channel_id=1, source_target_pairs={{8,0},{16,8},{24,16},{9,1},{17,9},{25,17},{10,2},{18,10},{26,18},{... | collective-permute-start | bytes 52232 | tf_op jit(solution)/shard_map/ppermute | solution.py:23
  297.1 9.1 %collective-permute-start.45 = (f32[34,1,128]{2,1,0:T(1,128)S(1)}, f32[34,1,128]{2,1,0:T(1,128)S(1)}, u32[]{:S(2)}, u32[]{:S(2)}) collective-permute-start(f32[34,1,128]{2,1,0:T(1,128)S(1)} %get-tuple-element.210), channel_id=1, source_target_pairs={{0,8},{8,16},{16,24},{1,9},{9,17},{17,25},{2,10},{10,18},{18,26},{... | collective-permute-start | bytes 52232 | tf_op jit(solution)/shard_map/ppermute | solution.py:22
  310.1 57.3 %collective-permute-start.47 = (f32[34,34,1]{1,2,0:T(1,128)S(1)}, f32[34,34,1]{1,2,0:T(1,128)S(1)}, u32[]{:S(2)}, u32[]{:S(2)}) collective-permute-start(f32[34,34,1]{1,2,0:T(1,128)S(1)} %copy.240), channel_id=1, source_target_pairs={{0,1},{1,2},{2,3},{3,4},{4,5},{5,6},{6,7},{8,9},{9,10},{10,11},{11... | collective-permute-start | bytes 13880 | tf_op jit(solution)/shard_map/ppermute | solution.py:22
  315.4 53.2 %collective-permute-start.46 = (f32[34,34,1]{1,2,0:T(1,128)S(1)}, f32[34,34,1]{1,2,0:T(1,128)S(1)}, u32[]{:S(2)}, u32[]{:S(2)}) collective-permute-start(f32[34,34,1]{1,2,0:T(1,128)S(1)} %copy.239), channel_id=1, source_target_pairs={{1,0},{2,1},{3,2},{4,3},{5,4},{6,5},{7,6},{9,8},{10,9},{11,10},{12... | collective-permute-start | bytes 13880 | tf_op jit(solution)/shard_map/ppermute | solution.py:23
  375.6 10.4 %collective-permute-start.48 = (f32[1,32,128]{2,1,0:T(8,128)S(1)}, f32[1,32,128]{2,1,0:T(8,128)S(1)}, u32[]{:S(2)}, u32[]{:S(2)}) collective-permute-start(f32[1,32,128]{2,1,0:T(8,128)S(1)} %get-tuple-element.233), channel_id=1, source_target_pairs={{32,0},{64,32},{96,64},{33,1},{65,33},{97,65},{34,2},{66,34},{98,6... | collective-permute-start | bytes 49160 | tf_op jit(solution)/shard_map/ppermute | solution.py:23
  376.9 9.2 %collective-permute-start.49 = (f32[1,32,128]{2,1,0:T(8,128)S(1)}, f32[1,32,128]{2,1,0:T(8,128)S(1)}, u32[]{:S(2)}, u32[]{:S(2)}) collective-permute-start(f32[1,32,128]{2,1,0:T(8,128)S(1)} %get-tuple-element.232), channel_id=1, source_target_pairs={{0,32},{32,64},{64,96},{1,33},{33,65},{65,97},{2,34},{34,66},{66,9... | collective-permute-start | bytes 49160 | tf_op jit(solution)/shard_map/ppermute | solution.py:22
  398.2 16.3 %collective-permute-start.53 = (f32[34,34,1]{1,2,0:T(1,128)S(1)}, f32[34,34,1]{1,2,0:T(1,128)S(1)}, u32[]{:S(2)}, u32[]{:S(2)}) collective-permute-start(f32[34,34,1]{1,2,0:T(1,128)S(1)} %copy.242), channel_id=1, source_target_pairs={{0,1},{1,2},{2,3},{3,4},{4,5},{5,6},{6,7},{8,9},{9,10},{10,11},{11... | collective-permute-start | bytes 13880 | tf_op jit(solution)/shard_map/ppermute | solution.py:22
  403.3 12.5 %collective-permute-start.52 = (f32[34,34,1]{1,2,0:T(1,128)S(1)}, f32[34,34,1]{1,2,0:T(1,128)S(1)}, u32[]{:S(2)}, u32[]{:S(2)}) collective-permute-start(f32[34,34,1]{1,2,0:T(1,128)S(1)} %copy.241), channel_id=1, source_target_pairs={{1,0},{2,1},{3,2},{4,3},{5,4},{6,5},{7,6},{9,8},{10,9},{11,10},{12... | collective-permute-start | bytes 13880 | tf_op jit(solution)/shard_map/ppermute | solution.py:23
  422.7 23.6 %collective-permute-start.54 = (f32[1,32,128]{2,1,0:T(8,128)S(1)}, f32[1,32,128]{2,1,0:T(8,128)S(1)}, u32[]{:S(2)}, u32[]{:S(2)}) collective-permute-start(f32[1,32,128]{2,1,0:T(8,128)S(1)} %get-tuple-element.231), channel_id=1, source_target_pairs={{32,0},{64,32},{96,64},{33,1},{65,33},{97,65},{34,2},{66,34},{98,6... | collective-permute-start | bytes 49160 | tf_op jit(solution)/shard_map/ppermute | solution.py:23
  424.2 22.2 %collective-permute-start.55 = (f32[1,32,128]{2,1,0:T(8,128)S(1)}, f32[1,32,128]{2,1,0:T(8,128)S(1)}, u32[]{:S(2)}, u32[]{:S(2)}) collective-permute-start(f32[1,32,128]{2,1,0:T(8,128)S(1)} %get-tuple-element.230), channel_id=1, source_target_pairs={{0,32},{32,64},{64,96},{1,33},{33,65},{65,97},{2,34},{34,66},{66,9... | collective-permute-start | bytes 49160 | tf_op jit(solution)/shard_map/ppermute | solution.py:22
  429.4 62.2 %all-to-all-start.1 = ((s32[1,128,8]{2,0,1:T(1,128)}), s32[1,128,8]{2,0,1:T(1,128)S(1)}, u32[]{:S(2)}, u32[]{:S(2)}) async-start(s32[1,128,8]{2,0,1:T(1,128)} %bitcast.34), calls=%async_computation.1 | async-start | bytes 131072 | tf_op jit(solution)/shard_map/all_to_all | solution.py:155
  447.5 7.1 %collective-permute-start.56 = (f32[34,1,128]{2,1,0:T(1,128)S(1)}, f32[34,1,128]{2,1,0:T(1,128)S(1)}, u32[]{:S(2)}, u32[]{:S(2)}) collective-permute-start(f32[34,1,128]{2,1,0:T(1,128)S(1)} %get-tuple-element.207), channel_id=1, source_target_pairs={{8,0},{16,8},{24,16},{9,1},{17,9},{25,17},{10,2},{18,10},{26,18},{... | collective-permute-start | bytes 52232 | tf_op jit(solution)/shard_map/ppermute | solution.py:23
  457.6 9.6 %collective-permute-start.58 = (f32[34,34,1]{1,2,0:T(1,128)S(1)}, f32[34,34,1]{1,2,0:T(1,128)S(1)}, u32[]{:S(2)}, u32[]{:S(2)}) collective-permute-start(f32[34,34,1]{1,2,0:T(1,128)S(1)} %copy.243), channel_id=1, source_target_pairs={{1,0},{2,1},{3,2},{4,3},{5,4},{6,5},{7,6},{9,8},{10,9},{11,10},{12... | collective-permute-start | bytes 13880 | tf_op jit(solution)/shard_map/ppermute | solution.py:23
  460.3 8.1 %collective-permute-start.59 = (f32[34,34,1]{1,2,0:T(1,128)S(1)}, f32[34,34,1]{1,2,0:T(1,128)S(1)}, u32[]{:S(2)}, u32[]{:S(2)}) collective-permute-start(f32[34,34,1]{1,2,0:T(1,128)S(1)} %copy.244), channel_id=1, source_target_pairs={{0,1},{1,2},{2,3},{3,4},{4,5},{5,6},{6,7},{8,9},{9,10},{10,11},{11... | collective-permute-start | bytes 13880 | tf_op jit(solution)/shard_map/ppermute | solution.py:22
  491.5 35.8 %all-to-all-start = ((f32[3,128,8,128]{3,2,0,1:T(8,128)}), f32[3,128,8,128]{3,2,0,1:T(8,128)S(1)}, u32[]{:S(2)}, u32[]{:S(2)}) async-start(f32[3,128,8,128]{3,2,0,1:T(8,128)} %copy_select_fusion), calls=%async_computation | async-start | bytes 3145728 | tf_op jit(solution)/shard_map/all_to_all | solution.py:148
  (104 other events, 552.2 us)
where the time goes:
time: 541 us; the launch traced here: 534 us
  starting transfers between devices  192 us (35%)
  local copies, waits for them, and re-layouts  179 us (33%)
  other arithmetic  120 us (22%)
  waiting for transfers between devices  40.4 us (7%)
    ppermute x30, starting transfers between devices, padded_2(): before = lax.ppermute(last, axis, up)  125 us
    gather x11, local copies, waits for them, and re-layouts, slot_sources(): found = jnp.minimum(jnp.searchsorted(sorted_target, wanted), row_count - 1)  49.8 us
    unnamed x169, local copies, waits for them, and re-layouts  39.6 us
    ppermute x30, starting transfers between devices, padded_2(): after = lax.ppermute(leading, axis, down)  39.3 us
    concatenate x27, other arithmetic, padded_2(): array = jnp.concatenate([before, array, after], axis=dim)  28.8 us
    add x6, other arithmetic, precondition(): correction + (reduced - press_total * correction + press_terms(correction...  27.7 us
    all_to_all x1, waiting for transfers between devices, move_rows(): lax.all_to_all(values.reshape(field_count, devices, capacity, line_len),...  19.5 us
    all_to_all x1, starting transfers between devices, move_rows(): lax.all_to_all(places.reshape(1, devices, capacity), ('gx', 'gy', 'gz'),...  16.9 us
  transfers between devices with their start and end apart: 62, of which 18 were waited for; matrix products, arithmetic and copies ran while one was open for 30% of the time, Pallas kernels for 0%

commit v1 on v0

v1 whole, which is shorter than its diff:
```python
import jax
import jax.numpy as jnp
from jax import lax
from jax.experimental import pallas as pl
from jax.experimental.pallas import tpu as pltpu
from jax.sharding import PartitionSpec as P

AXES = ("gx", "gy", "gz")
F32 = jnp.float32
T = 32
L = 128
H = 10
OJ = 12
EI = T + 2 * H
EJ = 56
SWEEPS = 9
SLOTS = 640
ZG = 10
ZS = 12
VMEM_LIMIT = 60 * 1024 * 1024


def strip_offsets():
    offsets, at = {}, 0
    for side in (0, 1):
        for dist in range(1, H):
            offsets[side, dist] = at
            at += H - dist
    return offsets


STRIPS = strip_offsets()


def plane_of(side, dist):
    return H - dist if side == 0 else dist - 1


def prep_kernel(p, sat, perm, sto, mask, own, xm, xp, ym, yp):
    def rows(q, carry):
        for u in range(4):
            i = q * 4 + u
            act = mask[i].astype(F32)
            s_w, s_g = sat[0, i], sat[1, i]
            s_o = 1.0 - s_w - s_g
            m_w, m_o, m_g = s_w * s_w * 2.0, s_o * s_o * 0.5, s_g * s_g * 4.0
            lam = m_w + m_o + m_g
            cond = perm[i] * act
            diag = act * (sto[i] * (0.5 * s_w + s_o + 2.0 * s_g)) + 3.0 * (1.0 - act)
            a_w, a_g = m_w / lam, m_g / lam
            for f, v in enumerate((cond, lam, diag, a_w, a_g)):
                own[f, i] = v
            for f, v in enumerate((p[i], cond, lam, diag)):
                ym[f * 8 + q, 10 * u : 10 * u + 10] = v[:H]
                yp[f * 8 + q, 10 * u : 10 * u + 10] = v[T - H :]
            for f, v in enumerate((a_w, a_g)):
                ym[32 + f, pl.ds(i, 1)] = v[:1]
                yp[32 + f, pl.ds(i, 1)] = v[T - 1 :]
        return carry

    lax.fori_loop(0, 8, rows, 0)
    for f in range(4):
        for t in range(H):
            xm[f * H + t] = p[t] if f == 0 else own[f - 1, t]
            xp[f * H + t] = p[T - H + t] if f == 0 else own[f - 1, T - H + t]
    for f in range(2):
        xm[4 * H + f] = own[3 + f, 0]
        xp[4 * H + f] = own[3 + f, T - 1]


def strip_kernel(x_lo, x_hi, cm, cp):
    for f in range(4):
        for side, src in ((0, x_lo), (1, x_hi)):
            for dist in range(1, H):
                n, at = H - dist, STRIPS[side, dist]
                t = f * H + plane_of(side, dist)
                cm[f, at : at + n] = src[t, :n]
                cp[f, at : at + n] = src[t, T - n :]


def lanes_of(rows):
    return lax.broadcasted_iota(jnp.int32, (rows, L), 1)


def build_kernel(edge, p, own, x_lo, x_hi, y_lo, y_hi, c_lo, c_hi, ext, aext, zm, zp):
    def cells(q, carry):
        for u in range(4):
            i = q * 4 + u
            for f in range(4):
                lo = y_lo[f * 8 + q, 10 * u : 10 * u + 10]
                hi = y_hi[f * 8 + q, 10 * u : 10 * u + 10]
                if f == 1:
                    lo, hi = lo * edge[2], hi * edge[3]
                ext[f, H + i, OJ - H : OJ] = lo
                ext[f, H + i, OJ : OJ + T] = p[i] if f == 0 else own[f - 1, i]
                ext[f, H + i, OJ + T : OJ + T + H] = hi
            for f in range(2):
                aext[f, 1 + i, OJ - 1 : OJ] = y_lo[32 + f, pl.ds(i, 1)]
                aext[f, 1 + i, OJ : OJ + T] = own[3 + f, i]
                aext[f, 1 + i, OJ + T : OJ + T + 1] = y_hi[32 + f, pl.ds(i, 1)]
        return carry

    lax.fori_loop(0, 8, cells, 0)
    for f in range(4):
        for side, src in ((0, x_lo), (1, x_hi)):
            for dist in range(1, H + 1):
                t = plane_of(side, dist)
                i = t if side == 0 else H + T + t
                v = src[f * H + t]
                if f == 1:
                    v = v * edge[side]
                ext[f, i, OJ : OJ + T] = v
                n = H - dist
                if n:
                    at = STRIPS[side, dist]
                    lo, hi = c_lo[f, at : at + n], c_hi[f, at : at + n]
                    if f == 1:
                        lo, hi = lo * (edge[side] * edge[2]), hi * (edge[side] * edge[3])
                    ext[f, i, OJ - n : OJ] = lo
                    ext[f, i, OJ + T : OJ + T + n] = hi
    for f in range(2):
        aext[f, 0, OJ : OJ + T] = x_lo[4 * H + f]
        aext[f, T + 1, OJ : OJ + T] = x_hi[4 * H + f]
    lane = lanes_of(EJ)

    def pack(s, carry):
        f, q = s // 5, s % 5
        low = jnp.zeros((EJ, L), F32)
        high = low
        for g in range(ZG):
            r = ext[f, 1 + q * ZG + g]
            if g:
                r = pltpu.roll(r, ZS * g, 1)
            low = jnp.where((lane >= ZS * g) & (lane < ZS * g + H), r, low)
            first = (ZS * g - H) % L
            high = jnp.where((lane >= first) & (lane < first + H), r, high)
        zm[s] = low
        zp[s] = high
        return carry

    lax.fori_loop(0, 20, pack, 0)

    def pack_share(f, carry):
        low = jnp.zeros((EJ, L), F32)
        high = low
        for g in range(T):
            r = aext[f, 1 + g]
            if g:
                r = pltpu.roll(r, g, 1)
            low = jnp.where(lane == g, r, low)
            high = jnp.where(lane == (g + L - 1) % L, r, high)
        zm[20 + f] = low
        zp[20 + f] = high
        return carry

    lax.fori_loop(0, 2, pack_share, 0)


def face(p, c, m, pn, cn, mn):
    trans = 2.0 * c * cn / jnp.maximum(c + cn, 0.5)
    there = trans * jnp.where(p >= pn, m, mn)
    back = trans * jnp.where(pn >= p, mn, m)
    step = pn - p
    return there, back, there * step, back * step


def solve_kernel(
    edge, dst, ext, aext, z_lo, z_hi, sat, old, sto, mask, places, send,
    wide, mat, base, one, two, total, rows, stage, sem,
):
    lane = lanes_of(EJ)
    at_end, at_start = lane == L - 1, lane == 0

    def spread(s, carry):
        f, q = s // 5, s % 5
        right, left = z_hi[s], z_lo[s]
        scale = jnp.where(lane < L // 2, edge[5], edge[4])
        scale = jnp.where(f == 1, scale, 1.0)
        for g in range(ZG):
            r, l = right, left
            if g:
                r, l = pltpu.roll(r, L - ZS * g, 1), pltpu.roll(l, L - ZS * g, 1)
            wide[f, 1 + q * ZG + g] = jnp.where(lane < L // 2, r, l) * scale
        return carry

    lax.fori_loop(0, 20, spread, 0)

    def pair(ref, *index):
        return ref[(0,) + index], ref[(1,) + index]

    def ring_next(a, w, end):
        ra, rw = pltpu.roll(a, L - 1, 1), pltpu.roll(w, L - 1, 1)
        return jnp.where(end, rw, ra), jnp.where(end, ra, rw)

    def ring_prev(a, w, start):
        ra, rw = pltpu.roll(a, 1, 1), pltpu.roll(w, 1, 1)
        return jnp.where(start, rw, ra), jnp.where(start, ra, rw)

    def up(v):
        return pltpu.roll(v, v.shape[0] - 1, 0)

    def down(v):
        return pltpu.roll(v, 1, 0)

    def both(f, i):
        return ext[f, i], wide[f, i]

    def x_face(i):
        here = [both(f, i) for f in range(3)]
        nxt = [both(f, i + 1) for f in range(3)]
        return [
            face(*(h[t] for h in here), *(n[t] for n in nxt)) for t in (0, 1)
        ]

    def assemble(i, carry):
        fields = [both(f, i) for f in range(3)]
        cross = x_face(i)
        nz = [ring_next(*v, at_end) for v in fields]
        z_faces = [face(*(v[t] for v in fields), *(n[t] for n in nz)) for t in (0, 1)]
        z_back = ring_prev(z_faces[0][1], z_faces[1][1], at_start)
        z_flow = ring_prev(z_faces[0][3], z_faces[1][3], at_start)
        out = []
        for t in (0, 1):
            mine = [v[t] for v in fields]
            y_there, y_back, y_flow, y_bflow = face(*mine, *(up(v) for v in mine))
            y_back, y_bflow = down(y_back), down(y_bflow)
            x_there, x_back, x_flow, x_bflow = cross[t]
            z_there, _, z_out, _ = z_faces[t]
            whole = both(3, i)[t] + (x_there + carry[2 * t]) + (y_there + y_back) + (z_there + z_back[t])
            flow = (x_flow - carry[2 * t + 1]) + (y_flow - y_bflow) + (z_out - z_flow[t])
            inv = 1.0 / whole
            weights = (x_there, carry[2 * t], y_there, y_back, z_there, z_back[t])
            for k, w in enumerate(weights):
                mat[k, t, i] = w * inv
            base[t, i] = flow * inv
            if t == 0:
                total[i] = whole
            out += [x_back, x_bflow]
        return tuple(out)

    first = x_face(0)
    lax.fori_loop(
        1, EI - 1, assemble, (first[0][1], first[0][3], first[1][1], first[1][3])
    )

    def sweep(src, target, depth):
        rows_at = slice(0, EJ) if depth > 3 else slice(8, 48)
        count = rows_at.stop - rows_at.start
        end, start = at_end[:count], at_start[:count]

        def plane(i, carry):
            ya, yw = src[0, i, rows_at], src[1, i, rows_at]
            zn = ring_next(ya, yw, end)
            zb = ring_prev(ya, yw, start)
            for t, y in ((0, ya), (1, yw)):
                if t == 1 and depth == 0:
                    continue
                acc = base[t, i, rows_at] + mat[0, t, i, rows_at] * src[t, i + 1, rows_at]
                acc = acc + mat[1, t, i, rows_at] * src[t, i - 1, rows_at]
                acc = acc + mat[2, t, i, rows_at] * up(y)
                acc = acc + mat[3, t, i, rows_at] * down(y)
                acc = acc + mat[4, t, i, rows_at] * zn[t]
                target[t, i, rows_at] = acc + mat[5, t, i, rows_at] * zb[t]
            return carry

        lax.fori_loop(H - depth, H + T + depth, plane, 0)

    src = base
    for k in range(1, SWEEPS + 1):
        target = one if k % 2 else two
        sweep(src, target, SWEEPS - k)
        src = target

    mid = slice(8, 48)
    end, start = at_end[:40], at_start[:40]

    def finish(i, carry):
        e = i + H
        pa, pw = ext[0, e, mid], wide[0, e, mid]
        sa, sw8 = two[0, e, mid], two[1, e, mid]
        p_near = (
            ext[0, e + 1, mid], ext[0, e - 1, mid], up(pa), down(pa),
            ring_next(pa, pw, end)[0], ring_prev(pa, pw, start)[0],
        )
        s_near = (
            two[0, e + 1, mid], two[0, e - 1, mid], up(sa), down(sa),
            ring_next(sa, sw8, end)[0], ring_prev(sa, sw8, start)[0],
        )
        share = []
        for f in range(2):
            a = aext[f, i + 1, mid]
            right = pltpu.roll(z_hi[20 + f, mid], L - 1 - i, 1)
            left = pltpu.roll(z_lo[20 + f, mid], (L + 1 - i) % L, 1)
            share.append((
                a,
                (
                    aext[f, i + 2, mid], aext[f, i, mid], up(a), down(a),
                    jnp.where(end, right, pltpu.roll(a, L - 1, 1)),
                    jnp.where(start, left, pltpu.roll(a, 1, 1)),
                ),
            ))
        sums = [jnp.zeros((40, L), F32) for _ in range(4)]
        for k in range(6):
            weight = mat[k, 0, e, mid]
            upstream = pa >= p_near[k]
            drive = s_near[k] - (pa - p_near[k])
            for f in range(2):
                w = weight * jnp.where(upstream, share[f][0], share[f][1][k])
                sums[2 * f] = sums[2 * f] + w
                sums[2 * f + 1] = sums[2 * f + 1] + w * drive
        scale = total[e, mid]
        sums = [(v * scale)[4:36] for v in sums]
        x_p = one[0, e, OJ : OJ + T]
        act = mask[i].astype(F32)
        held = act * sto[i]
        sat_scale = held + (1.0 - act)
        stage[0, i] = x_p
        for f, compress in ((0, 0.5), (1, 2.0)):
            column = held * compress * sat[f, i] + sums[2 * f] + (1.0 - act)
            change = held * (sat[f, i] - old[f, i])
            stage[1 + f, i] = (sums[2 * f + 1] - change - column * x_p) / sat_scale
        return carry

    lax.fori_loop(0, T, finish, 0)

    devices = places.shape[0]
    capacity = T * T // devices
    chunk = 3 * capacity + 1

    def place(i, carry):
        for j in range(T):
            d = dst[i * T + j]
            for f in range(3):
                rows[pl.ds(d + f * capacity, 1)] = stage[f, i, j : j + 1]
        return carry

    lax.fori_loop(0, T, place, 0)

    def tail(d, carry):
        rows[pl.ds(d * chunk + 3 * capacity, 1)] = places[pl.ds(d, 1)]
        return carry

    lax.fori_loop(0, devices, tail, 0)
    copy = pltpu.make_async_copy(rows.at[: devices * chunk], send, sem)
    copy.start()
    copy.wait()


def index_kernel(owner, slot, dst, place, count):
    devices = count.shape[0]
    capacity = T * T // devices
    chunk = 3 * capacity + 1

    def clear(d, carry):
        count[d] = 0
        return carry

    def blank(d, carry):
        place[d] = -1
        return carry

    lax.fori_loop(0, devices, clear, 0)
    lax.fori_loop(0, T * T, blank, 0, unroll=8)

    def row(r, carry):
        o = owner[r]

        @pl.when(o >= 0)
        def _():
            n = count[o]
            count[o] = n + 1
            place[o * capacity + n] = slot[r]
            dst[r] = o * chunk + n

        @pl.when(o < 0)
        def _():
            dst[r] = devices * chunk

        return carry

    lax.fori_loop(0, T * T, row, 0)


def unpack_kernel(got, update, held, number, table, where, sem):
    devices = where.shape[0]
    capacity = T * T // devices
    chunk = 3 * capacity + 1

    def collect(d, carry):
        number[pl.ds(d, 1)] = got[pl.ds(d * chunk + 3 * capacity, 1)]
        return carry

    lax.fori_loop(0, devices, collect, 0, unroll=8)
    slots = number[...].astype(jnp.int32)
    table[...] = jnp.where(slots < 0, SLOTS, slots)
    copy = pltpu.make_async_copy(table, where, sem)
    copy.start()
    copy.wait()

    def scatter(d, carry):
        for k in range(capacity):
            s = where[d, k]
            for f in range(3):
                held[f, pl.ds(s, 1)] = got[pl.ds(d * chunk + f * capacity + k, 1)]
        return carry

    lax.fori_loop(0, devices, scatter, 0)
    copy = pltpu.make_async_copy(held.at[:, :SLOTS], update, sem)
    copy.start()
    copy.wait()


def spec(space):
    return pl.BlockSpec(memory_space=space)


def shape(*dims):
    return jax.ShapeDtypeStruct(dims, F32)


def call(kernel, name, out_shape, smem, count, out_spaces=None, scratch=()):
    many = isinstance(out_shape, (tuple, list))
    spaces = out_spaces or ([pltpu.VMEM] * len(out_shape) if many else pltpu.VMEM)
    return pl.pallas_call(
        kernel,
        name=name,
        out_shape=out_shape,
        in_specs=[spec(pltpu.SMEM)] * smem + [spec(pltpu.VMEM)] * count,
        out_specs=[spec(s) for s in spaces] if many else spec(spaces),
        scratch_shapes=list(scratch),
        compiler_params=pltpu.CompilerParams(vmem_limit_bytes=VMEM_LIMIT),
    )


def ring(axis, step):
    size = lax.axis_size(axis)
    return [(i, (i + step) % size) for i in range(size)]


def swap(low, high, axis):
    return lax.ppermute(high, axis, ring(axis, 1)), lax.ppermute(low, axis, ring(axis, -1))


def body(
    pressure, saturation, old_saturation, permeability, storage, cell_mask, row_owner, row_slot
):
    devices = lax.axis_size(AXES)
    capacity = T * T // devices
    chunk = 3 * capacity + 1
    inside = []
    for axis in AXES:
        at = lax.axis_index(axis)
        inside += [at > 0, at < lax.axis_size(axis) - 1]
    edge = jnp.stack(inside).astype(F32)

    own, xm, xp, ym, yp = call(
        prep_kernel,
        "prep",
        (
            shape(5, T, T, L),
            shape(4 * H + 2, T, L),
            shape(4 * H + 2, T, L),
            shape(34, 40, L),
            shape(34, 40, L),
        ),
        0,
        5,
    )(pressure, saturation, permeability, storage, cell_mask)
    x_lo, x_hi = swap(xm, xp, "gx")
    y_lo, y_hi = swap(ym, yp, "gy")

    ints = jax.ShapeDtypeStruct((T * T,), jnp.int32)
    dst, place = call(
        index_kernel,
        "index",
        (ints, ints),
        2,
        0,
        [pltpu.SMEM] * 2,
        [pltpu.SMEM((devices,), jnp.int32)],
    )(row_owner.reshape(T * T), row_slot.reshape(T * T))
    places = jnp.pad(
        place.reshape(devices, capacity).astype(F32), ((0, 0), (0, L - capacity))
    )

    cm, cp = call(strip_kernel, "strip", (shape(4, 96, L), shape(4, 96, L)), 0, 2)(x_lo, x_hi)
    c_lo, c_hi = swap(cm, cp, "gy")
    ext, aext, zm, zp = call(
        build_kernel,
        "build",
        (shape(4, EI, EJ, L), shape(2, T + 2, EJ, L), shape(22, EJ, L), shape(22, EJ, L)),
        1,
        8,
    )(edge, pressure, own, x_lo, x_hi, y_lo, y_hi, c_lo, c_hi)
    z_lo, z_hi = swap(zm, zp, "gz")
    grid = (EI, EJ, L)
    send = call(
        solve_kernel,
        "solve",
        shape(devices * chunk, L),
        2,
        9,
        pl.ANY,
        [
            pltpu.VMEM((4,) + grid, F32),
            pltpu.VMEM((6, 2) + grid, F32),
            pltpu.VMEM((2,) + grid, F32),
            pltpu.VMEM((2,) + grid, F32),
            pltpu.VMEM((2,) + grid, F32),
            pltpu.VMEM(grid, F32),
            pltpu.VMEM((devices * chunk + 2 * capacity + 8, L), F32),
            pltpu.VMEM((3, T, T, L), F32),
            pltpu.SemaphoreType.DMA(()),
        ],
    )(edge, dst, ext, aext, z_lo, z_hi, saturation, old_saturation, storage, cell_mask, places)
    got = lax.all_to_all(
        send.reshape(devices, chunk, 1, L), AXES, split_axis=0, concat_axis=0, tiled=True
    )
    return call(
        unpack_kernel,
        "unpack",
        shape(3, SLOTS, L),
        0,
        1,
        pl.ANY,
        [
            pltpu.VMEM((3, SLOTS + 8, L), F32),
            pltpu.VMEM((devices, L), F32),
            pltpu.VMEM((devices, L), jnp.int32),
            pltpu.SMEM((devices, L), jnp.int32),
            pltpu.SemaphoreType.DMA(()),
        ],
    )(got.reshape(devices * chunk, L))


def solution(mesh):
    cells = P("gx", "gy", "gz")
    pair = P(None, "gx", "gy", "gz")
    return jax.shard_map(
        body,
        mesh=mesh,
        in_specs=(cells, pair, pair, cells, cells, cells, cells, cells),
        out_specs=P(None, AXES, None),
        check_vma=False,
    )
```

time: 541 us -> 179 us (0.33); the launches traced: 534 us -> 179 us
  starting transfers between devices: 192 us -> 13.6 us
  local copies, waits for them, and re-layouts: 179 us -> 6.22 us
  other arithmetic: 120 us -> 2.59 us
  Pallas kernels: 0 us -> 107 us
  blocking collectives: 0 us -> 33.2 us
  waiting for transfers between devices: 40.4 us -> 15.9 us
    ppermute x60 -> x8, starting transfers between devices: 164 us -> 13.6 us  [the longest x4 8.57 us: swap(): lax.ppermute(low, axis, ring(axis, -1))]
    pallas_call x0 -> x6, Pallas kernels: none -> 107 us  [the longest x1 67.5 us: body(): call(solve_kernel, 'solve', shape(devices * chunk, L), 2, 9, pl.ANY, [plt...]
    gather x21 -> x0, local copies, waits for them, and re-layouts: 80.5 us -> none  [the longest x11 49.8 us: slot_sources(): found = jnp.minimum(jnp.searchsorted(sorted_target, wanted), row_count - 1)]
    unnamed x169 -> x21, local copies, waits for them, and re-layouts: 39.6 us -> 4.08 us
    all_to_all x0 -> x1, blocking collectives: none -> 33.2 us  [body(): lax.all_to_all(send.reshape(devices, chunk, 1, L), AXES, split_axis=0, co...]
    reduce_sum x9 -> x0, other arithmetic: 33 us -> none  [the longest x2 12.7 us: precondition(): lifted = jnp.sum(second, axis=0) / press_total]
    concatenate x28 -> x0, other arithmetic: 28.8 us -> none  [the longest x27 28.8 us: padded_2(): array = jnp.concatenate([before, array, after], axis=dim)]
    ppermute x26 -> x0, local copies, waits for them, and re-layouts: 28.8 us -> none  [the longest x13 14.5 us: padded_2(): after = lax.ppermute(leading, axis, down)]
  transfers between devices with their start and end apart: 62 -> 8, of which waited for: 18 -> 2; matrix products, arithmetic and copies ran while one was open for 30% -> 3% of each run, Pallas kernels for 0% -> 10%
where the time goes in v1:
time: 179 us
  Pallas kernels  107 us (60%)
  blocking collectives  33.2 us (19%)
  waiting for transfers between devices  15.9 us (9%)
  starting transfers between devices  13.6 us (8%)
  local copies, waits for them, and re-layouts  6.22 us (3%)
  other arithmetic  2.59 us (1%)
    pallas_call x1, Pallas kernels, body(): call(solve_kernel, 'solve', shape(devices * chunk, L), 2, 9, pl.ANY, [plt...  67.5 us
    all_to_all x1, blocking collectives, body(): lax.all_to_all(send.reshape(devices, chunk, 1, L), AXES, split_axis=0, co...  33.2 us
    pallas_call x1, Pallas kernels, body(): call(index_kernel, 'index', (ints, ints), 2, 0, [pltpu.SMEM] * 2, [pltpu....  16.5 us
    ppermute x4, waiting for transfers between devices, swap(): lax.ppermute(high, axis, ring(axis, 1))  15.9 us
    pallas_call x1, Pallas kernels, body(): call(build_kernel, 'build', (shape(4, EI, EJ, L), shape(2, T + 2, EJ, L),...  10.2 us
    ppermute x4, starting transfers between devices, swap(): lax.ppermute(low, axis, ring(axis, -1))  8.57 us
    pallas_call x1, Pallas kernels, body(): call(unpack_kernel, 'unpack', shape(3, SLOTS, L), 0, 1, pl.ANY, [pltpu.VM...  5.9 us
    ppermute x4, starting transfers between devices, swap(): lax.ppermute(high, axis, ring(axis, 1))  5.01 us
  transfers between devices with their start and end apart: 8, of which 2 were waited for; matrix products, arithmetic and copies ran while one was open for 3% of the time, Pallas kernels for 10%

profile of v1, /device:TPU:0, one launch (start us, length us, event | category | flops | bytes accessed | tf_op | source)
XLA Modules:
  0.0 178.5 jit_solution(6987284162704165514)
XLA Ops:
  0.0 4.7 %prep.1 = (f32[5,32,32,128]{3,2,1,0:T(8,128)}, f32[42,32,128]{2,1,0:T(8,128)}, f32[42,32,128]{2,1,0:T(8,128)}, f32[34,40,128]{2,1,0:T(8,128)}, f32[34,40,128]{2,1,0:T(8,128)}) custom-call(f32[32,32,128]{2,1,0:T(8,128)} %p.3, f32[2,32,32,128]{3,2,1,0:T(8,128)} %sat.3, f32[32,32,128]{2,1,0:T(8,128)} %perm.1, f32[32,32,128]{2,1,0:T(8,128)} %sto.3, ...), custom_call_target="tpu_custom_call" | custom-call | tf_op jit(solution)/shard_map/prep/pallas_call | solution.py:456
  4.7 2.0 %collective-permute-start = (f32[42,32,128]{2,1,0:T(8,128)}, f32[42,32,128]{2,1,0:T(8,128)S(1)}, u32[]{:S(2)}, u32[]{:S(2)}) collective-permute-start(f32[42,32,128]{2,1,0:T(8,128)} %get-tuple-element.20), channel_id=1, source_target_pairs={{0,32},{32,64},{64,96},{96,0},{1,33},{33,65},{65,97},{97,1},{2,34}... | collective-permute-start | bytes 2064392 | tf_op jit(solution)/shard_map/ppermute | solution.py:441
  6.8 2.1 %collective-permute-start.1 = (f32[42,32,128]{2,1,0:T(8,128)}, f32[42,32,128]{2,1,0:T(8,128)S(1)}, u32[]{:S(2)}, u32[]{:S(2)}) collective-permute-start(f32[42,32,128]{2,1,0:T(8,128)} %get-tuple-element.21), channel_id=1, source_target_pairs={{0,96},{32,0},{64,32},{96,64},{1,97},{33,1},{65,33},{97,65},{2,98}... | collective-permute-start | bytes 2064392 | tf_op jit(solution)/shard_map/ppermute | solution.py:441
  8.9 1.5 collective-permute-start.2
  10.4 1.7 collective-permute-start.3
  12.1 12.4 %collective-permute-done.x_lo = f32[42,32,128]{2,1,0:T(8,128)S(1)} collective-permute-done((f32[42,32,128]{2,1,0:T(8,128)}, f32[42,32,128]{2,1,0:T(8,128)S(1)}, u32[]{:S(2)}, u32[]{:S(2)}) %collective-permute-start) | collective-permute-done | bytes 688160 | tf_op jit(solution)/shard_map/ppermute | solution.py:441
  24.5 0.8 copy-done
  25.4 0.9 copy-done.1
  26.2 2.2 %strip.1 = (f32[4,96,128]{2,1,0:T(8,128)}, f32[4,96,128]{2,1,0:T(8,128)}) custom-call(f32[42,32,128]{2,1,0:T(8,128)} %copy-done, f32[42,32,128]{2,1,0:T(8,128)} %copy-done.1), custom_call_target="tpu_custom_call" | custom-call | tf_op jit(solution)/shard_map/strip/pallas_call | solution.py:486
  28.4 1.5 collective-permute-start.4
  29.9 1.7 collective-permute-start.5
  31.6 0.1 stack.27
  31.7 0.6 convert_element_type.11.edge
  32.4 3.5 %collective-permute-done.4.c_lo = f32[4,96,128]{2,1,0:T(8,128)S(1)} collective-permute-done((f32[4,96,128]{2,1,0:T(8,128)}, f32[4,96,128]{2,1,0:T(8,128)S(1)}, u32[]{:S(2)}, u32[]{:S(2)}) %collective-permute-start.4) | collective-permute-done | bytes 196640 | tf_op jit(solution)/shard_map/ppermute | solution.py:441
  35.9 0.7 copy-done.6
  36.6 0.1 copy-done.7
  36.6 10.2 %build.1 = (f32[4,52,56,128]{3,2,1,0:T(8,128)}, f32[2,34,56,128]{3,2,1,0:T(8,128)}, f32[22,56,128]{2,1,0:T(8,128)}, f32[22,56,128]{2,1,0:T(8,128)}) custom-call(f32[6]{0:T(128)} %convert_element_type.11.edge, f32[32,32,128]{2,1,0:T(8,128)} %p.3, f32[5,32,32,128]{3,2,1,0:T(8,128)} %get-tuple-element.19.own, f32[42,32,128]{2,1,0:T(8,128)} %copy-done, ...), custom_call_target="tpu_custom_call" | custom-call | tf_op jit(solution)/shard_map/build/pallas_call | solution.py:488
  46.8 3.0 %collective-permute-start.7 = (f32[22,56,128]{2,1,0:T(8,128)}, f32[22,56,128]{2,1,0:T(8,128)S(1)}, u32[]{:S(2)}, u32[]{:S(2)}) collective-permute-start(f32[22,56,128]{2,1,0:T(8,128)} %get-tuple-element.29), channel_id=1, source_target_pairs={{0,7},{1,0},{2,1},{3,2},{4,3},{5,4},{6,5},{7,6},{8,15},{9,8},{10,9... | collective-permute-start | bytes 1892360 | tf_op jit(solution)/shard_map/ppermute | solution.py:441
  49.7 0.6 broadcast.8
  50.3 0.7 reduce.6
  51.0 0.7 reshape.14.owner
  51.7 0.7 reduce.7
  52.3 0.7 reshape.15.slot
  53.0 16.5 %index.1 = (s32[1024]{0:T(1024)}, s32[1024]{0:T(1024)}) custom-call(s32[1024]{0:T(1024)} %reshape.14.owner, s32[1024]{0:T(1024)} %reshape.15.slot), custom_call_target="tpu_custom_call" | custom-call | tf_op jit(solution)/shard_map/index/pallas_call | solution.py:473
  69.5 0.7 convert_element_type.12
  70.1 0.1 convert_element_type.13
  70.2 0.6 pad.4.places
  70.9 0.8 copy-done.4
  71.7 0.3 copy-done.5
  71.9 67.5 %solve.1 = f32[3200,128]{1,0:T(8,128)} custom-call(f32[6]{0:T(128)} %convert_element_type.11.edge, s32[1024]{0:T(1024)} %get-tuple-element.18.dst, f32[4,52,56,128]{3,2,1,0:T(8,128)} %get-tuple-element.26.ext, f32[2,34,56,128]{3,2,1,0:T(8,128)} %get-tuple-element.27.aext, f32[22,56,128]{2,1,0:T(8,128)} %copy-done.4, f32[22,56,128]{2,1,0:T(8,128)} %copy-done.5, ...), custom_call_target="tpu_custom_call" | custom-call | tf_op jit(solution)/shard_map/solve/pallas_call | solution.py:497
  139.4 33.2 %all_to_all.5 = f32[128,25,1,128]{3,2,1,0:T(1,128)} all-to-all(f32[128,25,1,128]{3,2,1,0:T(1,128)} %bitcast.10), channel_id=1, replica_groups=mesh['gx'=4,'gy'=4,'gz'=8] {'gx','gy','gz'}, dimensions={0} | all-to-all | bytes 3276800 | tf_op jit(solution)/shard_map/all_to_all | solution.py:516
  172.6 5.9 %unpack.1 = f32[3,640,128]{2,1,0:T(8,128)} custom-call(f32[3200,128]{1,0:T(8,128)} %bitcast.11), custom_call_target="tpu_custom_call" | custom-call | tf_op jit(solution)/shard_map/unpack/pallas_call | solution.py:519
  (21 shorter events, 0.0 us)
Async XLA Ops:
  4.7 19.8 %collective-permute-start = (f32[42,32,128]{2,1,0:T(8,128)}, f32[42,32,128]{2,1,0:T(8,128)S(1)}, u32[]{:S(2)}, u32[]{:S(2)}) collective-permute-start(f32[42,32,128]{2,1,0:T(8,128)} %get-tuple-element.20), channel_id=1, source_target_pairs={{0,32},{32,64},{64,96},{96,0},{1,33},{33,65},{65,97},{97,1},{2,34}... | collective-permute-start | bytes 2064392 | tf_op jit(solution)/shard_map/ppermute | solution.py:441
  6.8 17.8 %collective-permute-start.1 = (f32[42,32,128]{2,1,0:T(8,128)}, f32[42,32,128]{2,1,0:T(8,128)S(1)}, u32[]{:S(2)}, u32[]{:S(2)}) collective-permute-start(f32[42,32,128]{2,1,0:T(8,128)} %get-tuple-element.21), channel_id=1, source_target_pairs={{0,96},{32,0},{64,32},{96,64},{1,97},{33,1},{65,33},{97,65},{2,98}... | collective-permute-start | bytes 2064392 | tf_op jit(solution)/shard_map/ppermute | solution.py:441
  8.9 23.5 %collective-permute-start.2 = (f32[34,40,128]{2,1,0:T(8,128)}, f32[34,40,128]{2,1,0:T(8,128)S(1)}, u32[]{:S(2)}, u32[]{:S(2)}) collective-permute-start(f32[34,40,128]{2,1,0:T(8,128)} %get-tuple-element.22), channel_id=1, source_target_pairs={{0,8},{8,16},{16,24},{24,0},{1,9},{9,17},{17,25},{25,1},{2,10},{10... | collective-permute-start | bytes 2088968 | tf_op jit(solution)/shard_map/ppermute | solution.py:441
  10.4 22.0 %collective-permute-start.3 = (f32[34,40,128]{2,1,0:T(8,128)}, f32[34,40,128]{2,1,0:T(8,128)S(1)}, u32[]{:S(2)}, u32[]{:S(2)}) collective-permute-start(f32[34,40,128]{2,1,0:T(8,128)} %get-tuple-element.23), channel_id=1, source_target_pairs={{0,24},{8,0},{16,8},{24,16},{1,25},{9,1},{17,9},{25,17},{2,26},{10... | collective-permute-start | bytes 2088968 | tf_op jit(solution)/shard_map/ppermute | solution.py:441
  24.5 0.8 copy-start
  25.4 0.9 copy-start.1
  28.4 7.5 %collective-permute-start.4 = (f32[4,96,128]{2,1,0:T(8,128)}, f32[4,96,128]{2,1,0:T(8,128)S(1)}, u32[]{:S(2)}, u32[]{:S(2)}) collective-permute-start(f32[4,96,128]{2,1,0:T(8,128)} %get-tuple-element.24), channel_id=1, source_target_pairs={{0,8},{8,16},{16,24},{24,0},{1,9},{9,17},{17,25},{25,1},{2,10},{10... | collective-permute-start | bytes 589832 | tf_op jit(solution)/shard_map/ppermute | solution.py:441
  29.9 6.0 %collective-permute-start.5 = (f32[4,96,128]{2,1,0:T(8,128)}, f32[4,96,128]{2,1,0:T(8,128)S(1)}, u32[]{:S(2)}, u32[]{:S(2)}) collective-permute-start(f32[4,96,128]{2,1,0:T(8,128)} %get-tuple-element.25), channel_id=1, source_target_pairs={{0,24},{8,0},{16,8},{24,16},{1,25},{9,1},{17,9},{25,17},{2,26},{10... | collective-permute-start | bytes 589832 | tf_op jit(solution)/shard_map/ppermute | solution.py:441
  32.3 3.6 %copy-start.2 = (f32[34,40,128]{2,1,0:T(8,128)}, f32[34,40,128]{2,1,0:T(8,128)S(1)}, u32[]{:S(2)}) copy-start(f32[34,40,128]{2,1,0:T(8,128)S(1)} %collective-permute-done.2.y_lo) | copy-start | bytes 2088964
  32.3 3.6 %copy-start.3 = (f32[34,40,128]{2,1,0:T(8,128)}, f32[34,40,128]{2,1,0:T(8,128)S(1)}, u32[]{:S(2)}) copy-start(f32[34,40,128]{2,1,0:T(8,128)S(1)} %collective-permute-done.3.y_hi) | copy-start | bytes 2088964
  35.9 0.7 copy-start.6
  35.9 0.7 copy-start.7
  36.6 13.7 %copy-start.8 = (s32[32,32,1]{1,2,0:T(1,128)S(1)}, s32[32,32,1]{1,2,0:T(1,128)}, u32[]{:S(2)}) copy-start(s32[32,32,1]{1,2,0:T(1,128)} %param.14) | copy-start | bytes 12292
  36.6 15.0 %copy-start.9 = (s32[32,32,1]{1,2,0:T(1,128)S(1)}, s32[32,32,1]{1,2,0:T(1,128)}, u32[]{:S(2)}) copy-start(s32[32,32,1]{1,2,0:T(1,128)} %param.15) | copy-start | bytes 12292
  46.8 24.1 %collective-permute-start.6 = (f32[22,56,128]{2,1,0:T(8,128)}, f32[22,56,128]{2,1,0:T(8,128)S(1)}, u32[]{:S(2)}, u32[]{:S(2)}) collective-permute-start(f32[22,56,128]{2,1,0:T(8,128)} %get-tuple-element.28), channel_id=1, source_target_pairs={{0,1},{1,2},{2,3},{3,4},{4,5},{5,6},{6,7},{7,0},{8,9},{9,10},{10,1... | collective-permute-start | bytes 1892360 | tf_op jit(solution)/shard_map/ppermute | solution.py:441
  46.8 24.1 %collective-permute-start.7 = (f32[22,56,128]{2,1,0:T(8,128)}, f32[22,56,128]{2,1,0:T(8,128)S(1)}, u32[]{:S(2)}, u32[]{:S(2)}) collective-permute-start(f32[22,56,128]{2,1,0:T(8,128)} %get-tuple-element.29), channel_id=1, source_target_pairs={{0,7},{1,0},{2,1},{3,2},{4,3},{5,4},{6,5},{7,6},{8,15},{9,8},{10,9... | collective-permute-start | bytes 1892360 | tf_op jit(solution)/shard_map/ppermute | solution.py:441
  70.9 0.8 copy-start.4
  70.9 1.1 copy-start.5

commit v2 on v1

--- a/solution.py
+++ b/solution.py
@@ -16,8 +16,10 @@
 SWEEPS = 9
 SLOTS = 640
 ZG = 10
+NQ = 5
+SOLVE_MIB = 42
+PAD = 8
 ZS = 12
-VMEM_LIMIT = 60 * 1024 * 1024
 
 
 def strip_offsets():
@@ -68,7 +70,8 @@
         xp[4 * H + f] = own[3 + f, T - 1]
 
 
-def strip_kernel(x_lo, x_hi, cm, cp):
+def strip_kernel(dst, x_lo, x_hi, places, cm, cp):
+    del dst, places
     for f in range(4):
         for side, src in ((0, x_lo), (1, x_hi)):
             for dist in range(1, H):
@@ -80,6 +83,18 @@
 
 def lanes_of(rows):
     return lax.broadcasted_iota(jnp.int32, (rows, L), 1)
+
+
+def up(v):
+    return pltpu.roll(v, v.shape[0] - 1, 0)
+
+
+def down(v):
+    return pltpu.roll(v, 1, 0)
+
+
+def turn(v, by):
+    return pltpu.roll(v, by % L if isinstance(by, int) else lax.rem(by + 2 * L, L), 1)
 
 
 def build_kernel(edge, p, own, x_lo, x_hi, y_lo, y_hi, c_lo, c_hi, ext, aext, zm, zp):
@@ -124,13 +139,15 @@
     lane = lanes_of(EJ)
 
     def pack(s, carry):
-        f, q = s // 5, s % 5
+        f, q = s // NQ, s % NQ
         low = jnp.zeros((EJ, L), F32)
         high = low
         for g in range(ZG):
-            r = ext[f, 1 + q * ZG + g]
+            i = 1 + q + NQ * g
+            r = ext[f, i, :EJ]
             if g:
-                r = pltpu.roll(r, ZS * g, 1)
+                r = turn(r, ZS * g)
+                ext[f, i, :EJ] = r
             low = jnp.where((lane >= ZS * g) & (lane < ZS * g + H), r, low)
             first = (ZS * g - H) % L
             high = jnp.where((lane >= first) & (lane < first + H), r, high)
@@ -138,19 +155,23 @@
         zp[s] = high
         return carry
 
-    lax.fori_loop(0, 20, pack, 0)
+    lax.fori_loop(0, 4 * NQ, pack, 0)
+    for f in range(3):
+        ext[f, EI - 1, :EJ] = turn(ext[f, EI - 1, :EJ], ZS * ZG)
 
     def pack_share(f, carry):
         low = jnp.zeros((EJ, L), F32)
         high = low
-        for g in range(T):
-            r = aext[f, 1 + g]
-            if g:
-                r = pltpu.roll(r, g, 1)
-            low = jnp.where(lane == g, r, low)
-            high = jnp.where(lane == (g + L - 1) % L, r, high)
-        zm[20 + f] = low
-        zp[20 + f] = high
+        for i in range(T + 2):
+            v = aext[f, i]
+            if 1 <= i <= T:
+                spot = 2 * (i - 1)
+                r = turn(v, spot) if spot else v
+                low = jnp.where(lane == spot, r, low)
+                high = jnp.where(lane == (spot + L - 1) % L, r, high)
+            aext[f, i] = turn(v, ZS * ((i + H - 2) // NQ))
+        zm[4 * NQ + f] = low
+        zp[4 * NQ + f] = high
         return carry
 
     lax.fori_loop(0, 2, pack_share, 0)
@@ -165,163 +186,241 @@
 
 
 def solve_kernel(
-    edge, dst, ext, aext, z_lo, z_hi, sat, old, sto, mask, places, send,
-    wide, mat, base, one, two, total, rows, stage, sem,
+    edge, dst, ext, aext, z_lo, z_hi, z_first, z_last, sat, old, sto, mask, places, send,
+    side, rim, back, mat, zmat, base, one, two, zbase, zone, ztwo, border, total, share, spare, rows, stage, sem,
 ):
     lane = lanes_of(EJ)
-    at_end, at_start = lane == L - 1, lane == 0
-
-    def spread(s, carry):
-        f, q = s // 5, s % 5
-        right, left = z_hi[s], z_lo[s]
-        scale = jnp.where(lane < L // 2, edge[5], edge[4])
-        scale = jnp.where(f == 1, scale, 1.0)
-        for g in range(ZG):
-            r, l = right, left
-            if g:
-                r, l = pltpu.roll(r, L - ZS * g, 1), pltpu.roll(l, L - ZS * g, 1)
-            wide[f, 1 + q * ZG + g] = jnp.where(lane < L // 2, r, l) * scale
-        return carry
-
-    lax.fori_loop(0, 20, spread, 0)
-
-    def pair(ref, *index):
-        return ref[(0,) + index], ref[(1,) + index]
-
-    def ring_next(a, w, end):
-        ra, rw = pltpu.roll(a, L - 1, 1), pltpu.roll(w, L - 1, 1)
-        return jnp.where(end, rw, ra), jnp.where(end, ra, rw)
-
-    def ring_prev(a, w, start):
-        ra, rw = pltpu.roll(a, 1, 1), pltpu.roll(w, 1, 1)
-        return jnp.where(start, rw, ra), jnp.where(start, ra, rw)
-
-    def up(v):
-        return pltpu.roll(v, v.shape[0] - 1, 0)
-
-    def down(v):
-        return pltpu.roll(v, 1, 0)
-
-    def both(f, i):
-        return ext[f, i], wide[f, i]
-
-    def x_face(i):
-        here = [both(f, i) for f in range(3)]
-        nxt = [both(f, i + 1) for f in range(3)]
-        return [
-            face(*(h[t] for h in here), *(n[t] for n in nxt)) for t in (0, 1)
+    part = lax.rem(lane, ZS)
+    first_lane = part == 0
+    last_lane = (part == ZS - 1) & (lane < ZS * (ZG - 1)) | (lane == L - 1)
+    body_rows = slice(PAD, PAD + EJ)
+
+    def wrap(ref, t):
+        ref[t, 0] = turn(ref[t, NQ], ZS)
+        ref[t, NQ + 1] = turn(ref[t, 1], -ZS)
+
+    def join(q, carry):
+        for f in range(4):
+            right, left = z_hi[f * NQ + q], z_lo[f * NQ + q]
+            if f == 1:
+                right, left = right * edge[5], left * edge[4]
+            if f < 3:
+                right = jnp.where(last_lane, z_last[f * NQ + q], right)
+                left = jnp.where(first_lane, z_first[f * NQ + q], left)
+                rim[f, q] = jnp.where(first_lane, z_hi[f * NQ + q], z_lo[f * NQ + q])
+                if f == 1:
+                    rim[f, q] = jnp.where(first_lane, right, left)
+            side[f, 0, 1 + q] = right
+            side[f, 1, 1 + q] = left
+        return carry
+
+    lax.fori_loop(0, NQ, join, 0)
+    for f in range(3):
+        for t in (0, 1):
+            wrap(side.at[f], t)
+
+    def combine(diag, x, x_carry, y, z, z_back, z_bflow):
+        y_back, y_bflow = down(y[1]), down(y[3])
+        whole = diag + (x[0] + x_carry[0]) + (y[0] + y_back) + (z[0] + z_back)
+        flow = (x[2] - x_carry[1]) + (y[2] - y_bflow) + (z[2] - z_bflow)
+        inv = 1.0 / whole
+        weights = [w * inv for w in (x[0], x_carry[0], y[0], y_back, z[0], z_back)]
+        return whole, flow * inv, weights
+
+    for t in (0, 1):
+
+        def packed(q, carry, t=t):
+            here = [side[f, t, q] for f in range(3)]
+            x = face(*here, *(side[f, t, q + 1] for f in range(3)))
+            y = face(*here, *(up(v) for v in here))
+            z = face(*here, *(turn(v, -1) for v in here))
+            if t == 1:
+                back[0, q - 1] = z[1]
+                back[1, q - 1] = z[3]
+            _, start, weights = combine(
+                side[3, t, q], x, carry, y, z, turn(z[1], 1), turn(z[3], 1)
+            )
+            for k, w in enumerate(weights):
+                zmat[k, t, q - 1] = w
+            zbase[t, q, body_rows] = start
+            return x[1], x[3]
+
+        x = face(*(side[f, t, 0] for f in range(3)), *(side[f, t, 1] for f in range(3)))
+        lax.fori_loop(1, NQ + 1, packed, (x[1], x[3]))
+
+    def spots(g, lanes):
+        return lanes == ZS * g, lanes == lax.rem(ZS * g + L - 1, L)
+
+    def ghosts(ref, q, value, rows_at, marks):
+        pltpu.store(ref.at[0, 1 + q, rows_at], value, mask=marks[1])
+        pltpu.store(ref.at[1, 1 + q, rows_at], value, mask=marks[0])
+
+    all_rows = slice(0, EJ)
+
+    def assemble(g, carry):
+        marks = spots(g, lane)
+        for q in range(NQ):
+            i = 1 + NQ * g + q
+            here = [ext[f, i, all_rows] for f in range(3)]
+            ahead = [ext[f, i + 1, all_rows] for f in range(3)]
+            if q == NQ - 1:
+                ahead = [turn(v, -ZS) for v in ahead]
+            x = face(*here, *ahead)
+            y = face(*here, *(ext[f, i, 1 : EJ + 1] for f in range(3)))
+            z = face(
+                *here,
+                *(turn(jnp.where(marks[0], rim[f, q], v), -1) for f, v in enumerate(here)),
+            )
+            z_back, z_bflow = (
+                turn(jnp.where(marks[1], back[k, q], z[n]), 1) for k, n in ((0, 1), (1, 3))
+            )
+            whole, start, weights = combine(ext[3, i, all_rows], x, carry, y, z, z_back, z_bflow)
+            for k, w in enumerate(weights):
+                mat[k, i] = w
+            total[i] = whole
+            base[i, body_rows] = start
+            ghosts(zbase, q, start, body_rows, marks)
+            carry = x[1], x[3]
+        return tuple(turn(v, ZS) for v in carry)
+
+    x = face(*(ext[f, 0, all_rows] for f in range(3)), *(ext[f, 1, all_rows] for f in range(3)))
+    lax.fori_loop(0, ZG, assemble, (x[1], x[3]))
+
+    def prepare(zsrc):
+        for t in (0, 1):
+            wrap(zsrc, t)
+
+        def plane(q, carry):
+            border[q] = jnp.where(
+                first_lane, zsrc[0, 1 + q, body_rows], zsrc[1, 1 + q, body_rows]
+            )
+            return carry
+
+        lax.fori_loop(0, NQ, plane, 0)
+
+    def sweep(src, zsrc, target, ztarget, depth):
+        low, high = (0, EJ) if depth > 3 else (8, 48)
+        at = slice(low, high)
+        y_at = slice(PAD + low, PAD + high)
+        y_up, y_down = (slice(y_at.start + k, y_at.stop + k) for k in (1, -1))
+        lanes = lane[at]
+        prepare(zsrc)
+
+        def halo(q, carry):
+            for t in (0, 1):
+                y = zsrc[t, q, y_at]
+                acc = zbase[t, q, y_at] + zmat[0, t, q - 1, at] * zsrc[t, q + 1, y_at]
+                acc = acc + zmat[1, t, q - 1, at] * zsrc[t, q - 1, y_at]
+                acc = acc + zmat[2, t, q - 1, at] * zsrc[t, q, y_up]
+                acc = acc + zmat[3, t, q - 1, at] * zsrc[t, q, y_down]
+                acc = acc + zmat[4, t, q - 1, at] * turn(y, -1)
+                ztarget[t, q, y_at] = acc + zmat[5, t, q - 1, at] * turn(y, 1)
+            return carry
+
+        lax.fori_loop(1, NQ + 1, halo, 0)
+
+        def planes(g, carry):
+            marks = spots(g, lanes)
+            for q in range(NQ):
+                i = 1 + NQ * g + q
+                y, near = src[i, y_at], border[q, at]
+                ahead, behind = src[i + 1, y_at], src[i - 1, y_at]
+                if q == 0:
+                    behind = turn(behind, ZS)
+                if q == NQ - 1:
+                    ahead = turn(ahead, -ZS)
+                acc = base[i, y_at] + mat[0, i, at] * ahead
+                acc = acc + mat[1, i, at] * behind
+                acc = acc + mat[2, i, at] * src[i, y_up]
+                acc = acc + mat[3, i, at] * src[i, y_down]
+                acc = acc + mat[4, i, at] * turn(jnp.where(marks[0], near, y), -1)
+                acc = acc + mat[5, i, at] * turn(jnp.where(marks[1], near, y), 1)
+                target[i, y_at] = acc
+                ghosts(ztarget, q, acc, y_at, marks)
+            return carry
+
+        lax.fori_loop(*((0, ZG) if depth > 4 else (1, ZG - 1)), planes, 0)
+
+    src, zsrc = base, zbase
+    for k in range(1, SWEEPS):
+        target, ztarget = (one, zone) if k % 2 else (two, ztwo)
+        sweep(src, zsrc, target, ztarget, SWEEPS - k)
+        src, zsrc = target, ztarget
+    prepare(zsrc)
+
+    mid, mid_up, mid_down = slice(8, 48), slice(9, 49), slice(7, 47)
+    y_mid, y_up, y_down = (slice(PAD + k, PAD + 40 + k) for k in (8, 9, 7))
+    lanes = lane[mid]
+    even = lax.rem(lanes, 2) == 0
+    for f in range(2):
+        share[f] = jnp.where(even, z_hi[4 * NQ + f, mid], z_lo[4 * NQ + f, mid])
+
+    def near_of(ref, lead, i, at, at_up, at_down, edge_plane, q, marks):
+        here, ahead, behind = (ref[lead + (i + k, at)] for k in (0, 1, -1))
+        if q == 0:
+            behind = turn(behind, ZS)
+        if q == NQ - 1:
+            ahead = turn(ahead, -ZS)
+        return here, (
+            ahead,
+            behind,
+            ref[lead + (i, at_up)],
+            ref[lead + (i, at_down)],
+            turn(jnp.where(marks[0], edge_plane, here), -1),
+            turn(jnp.where(marks[1], edge_plane, here), 1),
+        )
+
+    def finish(g, q, marks):
+        e = 1 + NQ * g + q
+        i = e - H
+        pa, p_near = near_of(ext, (0,), e, mid, mid_up, mid_down, rim[0, q, mid], q, marks)
+        _, s_near = near_of(src, (), e, y_mid, y_up, y_down, border[q, mid], q, marks)
+        shares = [
+            near_of(
+                aext, (f,), i + 1, mid, mid_up, mid_down,
+                turn(share[f], ZS * g - 2 * i), q, marks,
+            )
+            for f in range(2)
         ]
-
-    def assemble(i, carry):
-        fields = [both(f, i) for f in range(3)]
-        cross = x_face(i)
-        nz = [ring_next(*v, at_end) for v in fields]
-        z_faces = [face(*(v[t] for v in fields), *(n[t] for n in nz)) for t in (0, 1)]
-        z_back = ring_prev(z_faces[0][1], z_faces[1][1], at_start)
-        z_flow = ring_prev(z_faces[0][3], z_faces[1][3], at_start)
-        out = []
-        for t in (0, 1):
-            mine = [v[t] for v in fields]
-            y_there, y_back, y_flow, y_bflow = face(*mine, *(up(v) for v in mine))
-            y_back, y_bflow = down(y_back), down(y_bflow)
-            x_there, x_back, x_flow, x_bflow = cross[t]
-            z_there, _, z_out, _ = z_faces[t]
-            whole = both(3, i)[t] + (x_there + carry[2 * t]) + (y_there + y_back) + (z_there + z_back[t])
-            flow = (x_flow - carry[2 * t + 1]) + (y_flow - y_bflow) + (z_out - z_flow[t])
-            inv = 1.0 / whole
-            weights = (x_there, carry[2 * t], y_there, y_back, z_there, z_back[t])
-            for k, w in enumerate(weights):
-                mat[k, t, i] = w * inv
-            base[t, i] = flow * inv
-            if t == 0:
-                total[i] = whole
-            out += [x_back, x_bflow]
-        return tuple(out)
-
-    first = x_face(0)
-    lax.fori_loop(
-        1, EI - 1, assemble, (first[0][1], first[0][3], first[1][1], first[1][3])
-    )
-
-    def sweep(src, target, depth):
-        rows_at = slice(0, EJ) if depth > 3 else slice(8, 48)
-        count = rows_at.stop - rows_at.start
-        end, start = at_end[:count], at_start[:count]
-
-        def plane(i, carry):
-            ya, yw = src[0, i, rows_at], src[1, i, rows_at]
-            zn = ring_next(ya, yw, end)
-            zb = ring_prev(ya, yw, start)
-            for t, y in ((0, ya), (1, yw)):
-                if t == 1 and depth == 0:
-                    continue
-                acc = base[t, i, rows_at] + mat[0, t, i, rows_at] * src[t, i + 1, rows_at]
-                acc = acc + mat[1, t, i, rows_at] * src[t, i - 1, rows_at]
-                acc = acc + mat[2, t, i, rows_at] * up(y)
-                acc = acc + mat[3, t, i, rows_at] * down(y)
-                acc = acc + mat[4, t, i, rows_at] * zn[t]
-                target[t, i, rows_at] = acc + mat[5, t, i, rows_at] * zb[t]
-            return carry
-
-        lax.fori_loop(H - depth, H + T + depth, plane, 0)
-
-    src = base
-    for k in range(1, SWEEPS + 1):
-        target = one if k % 2 else two
-        sweep(src, target, SWEEPS - k)
-        src = target
-
-    mid = slice(8, 48)
-    end, start = at_end[:40], at_start[:40]
-
-    def finish(i, carry):
-        e = i + H
-        pa, pw = ext[0, e, mid], wide[0, e, mid]
-        sa, sw8 = two[0, e, mid], two[1, e, mid]
-        p_near = (
-            ext[0, e + 1, mid], ext[0, e - 1, mid], up(pa), down(pa),
-            ring_next(pa, pw, end)[0], ring_prev(pa, pw, start)[0],
-        )
-        s_near = (
-            two[0, e + 1, mid], two[0, e - 1, mid], up(sa), down(sa),
-            ring_next(sa, sw8, end)[0], ring_prev(sa, sw8, start)[0],
-        )
-        share = []
+        x_p = base[e, y_mid]
+        for k in range(6):
+            x_p = x_p + mat[k, e, mid] * s_near[k]
+        column = [jnp.zeros((40, L), F32) for _ in range(2)]
+        drive = [jnp.zeros((40, L), F32) for _ in range(2)]
+        for k in range(6):
+            weight = mat[k, e, mid]
+            upstream = pa >= p_near[k]
+            step = s_near[k] - (pa - p_near[k])
+            for f, (a, a_near) in enumerate(shares):
+                w = weight * jnp.where(upstream, a, a_near[k])
+                column[f] = column[f] + w
+                drive[f] = drive[f] + w * step
+        scale = total[e, mid]
+        shift = -ZS * g
+        spare[0] = turn(x_p, shift)
         for f in range(2):
-            a = aext[f, i + 1, mid]
-            right = pltpu.roll(z_hi[20 + f, mid], L - 1 - i, 1)
-            left = pltpu.roll(z_lo[20 + f, mid], (L + 1 - i) % L, 1)
-            share.append((
-                a,
-                (
-                    aext[f, i + 2, mid], aext[f, i, mid], up(a), down(a),
-                    jnp.where(end, right, pltpu.roll(a, L - 1, 1)),
-                    jnp.where(start, left, pltpu.roll(a, 1, 1)),
-                ),
-            ))
-        sums = [jnp.zeros((40, L), F32) for _ in range(4)]
-        for k in range(6):
-            weight = mat[k, 0, e, mid]
-            upstream = pa >= p_near[k]
-            drive = s_near[k] - (pa - p_near[k])
-            for f in range(2):
-                w = weight * jnp.where(upstream, share[f][0], share[f][1][k])
-                sums[2 * f] = sums[2 * f] + w
-                sums[2 * f + 1] = sums[2 * f + 1] + w * drive
-        scale = total[e, mid]
-        sums = [(v * scale)[4:36] for v in sums]
-        x_p = one[0, e, OJ : OJ + T]
+            spare[1 + f] = turn((drive[f] - column[f] * x_p) * scale, shift)
+        x_p = spare[0, 4:36]
         act = mask[i].astype(F32)
         held = act * sto[i]
-        sat_scale = held + (1.0 - act)
+        idle = 1.0 - act
+        inverse = 1.0 / (held + idle)
         stage[0, i] = x_p
         for f, compress in ((0, 0.5), (1, 2.0)):
-            column = held * compress * sat[f, i] + sums[2 * f] + (1.0 - act)
-            change = held * (sat[f, i] - old[f, i])
-            stage[1 + f, i] = (sums[2 * f + 1] - change - column * x_p) / sat_scale
-        return carry
-
-    lax.fori_loop(0, T, finish, 0)
+            s_now = sat[f, i]
+            local = (held * (compress * s_now) + idle) * x_p
+            change = held * (s_now - old[f, i])
+            stage[1 + f, i] = (spare[1 + f, 4:36] - change - local) * inverse
+
+    def group(g, carry):
+        marks = spots(g, lanes)
+        for q in range(NQ):
+            finish(g, q, marks)
+        return carry
+
+    lax.fori_loop(2, 8, group, 0)
+    finish(jnp.int32(1), NQ - 1, spots(1, lanes))
+    finish(jnp.int32(8), 0, spots(8, lanes))
 
     devices = places.shape[0]
     capacity = T * T // devices
@@ -340,7 +439,7 @@
         rows[pl.ds(d * chunk + 3 * capacity, 1)] = places[pl.ds(d, 1)]
         return carry
 
-    lax.fori_loop(0, devices, tail, 0)
+    lax.fori_loop(0, devices, tail, 0, unroll=8)
     copy = pltpu.make_async_copy(rows.at[: devices * chunk], send, sem)
     copy.start()
     copy.wait()
@@ -418,7 +517,7 @@
     return jax.ShapeDtypeStruct(dims, F32)
 
 
-def call(kernel, name, out_shape, smem, count, out_spaces=None, scratch=()):
+def call(kernel, name, out_shape, smem, count, out_spaces=None, scratch=(), limit=16):
     many = isinstance(out_shape, (tuple, list))
     spaces = out_spaces or ([pltpu.VMEM] * len(out_shape) if many else pltpu.VMEM)
     return pl.pallas_call(
@@ -428,7 +527,7 @@
         in_specs=[spec(pltpu.SMEM)] * smem + [spec(pltpu.VMEM)] * count,
         out_specs=[spec(s) for s in spaces] if many else spec(spaces),
         scratch_shapes=list(scratch),
-        compiler_params=pltpu.CompilerParams(vmem_limit_bytes=VMEM_LIMIT),
+        compiler_params=pltpu.CompilerParams(vmem_limit_bytes=limit << 20),
     )
 
 
@@ -483,36 +582,49 @@
         place.reshape(devices, capacity).astype(F32), ((0, 0), (0, L - capacity))
     )
 
-    cm, cp = call(strip_kernel, "strip", (shape(4, 96, L), shape(4, 96, L)), 0, 2)(x_lo, x_hi)
+    cm, cp = call(strip_kernel, "strip", (shape(4, 96, L), shape(4, 96, L)), 1, 3)(
+        dst, x_lo, x_hi, places
+    )
     c_lo, c_hi = swap(cm, cp, "gy")
     ext, aext, zm, zp = call(
         build_kernel,
         "build",
-        (shape(4, EI, EJ, L), shape(2, T + 2, EJ, L), shape(22, EJ, L), shape(22, EJ, L)),
+        (shape(4, EI, EJ + 8, L), shape(2, T + 2, EJ, L), shape(22, EJ, L), shape(22, EJ, L)),
         1,
         8,
+        limit=24,
     )(edge, pressure, own, x_lo, x_hi, y_lo, y_hi, c_lo, c_hi)
     z_lo, z_hi = swap(zm, zp, "gz")
-    grid = (EI, EJ, L)
     send = call(
         solve_kernel,
         "solve",
         shape(devices * chunk, L),
         2,
-        9,
+        11,
         pl.ANY,
         [
-            pltpu.VMEM((4,) + grid, F32),
-            pltpu.VMEM((6, 2) + grid, F32),
-            pltpu.VMEM((2,) + grid, F32),
-            pltpu.VMEM((2,) + grid, F32),
-            pltpu.VMEM((2,) + grid, F32),
-            pltpu.VMEM(grid, F32),
+            pltpu.VMEM((4, 2, NQ + 2, EJ, L), F32),
+            pltpu.VMEM((3, NQ, EJ, L), F32),
+            pltpu.VMEM((2, NQ, EJ, L), F32),
+            pltpu.VMEM((6, EI, EJ, L), F32),
+            pltpu.VMEM((6, 2, NQ, EJ, L), F32),
+        ]
+        + [pltpu.VMEM((EI, EJ + 2 * PAD, L), F32)] * 3
+        + [pltpu.VMEM((2, NQ + 2, EJ + 2 * PAD, L), F32)] * 3
+        + [
+            pltpu.VMEM((NQ, EJ, L), F32),
+            pltpu.VMEM((EI, EJ, L), F32),
+            pltpu.VMEM((2, 40, L), F32),
+            pltpu.VMEM((3, 40, L), F32),
             pltpu.VMEM((devices * chunk + 2 * capacity + 8, L), F32),
             pltpu.VMEM((3, T, T, L), F32),
             pltpu.SemaphoreType.DMA(()),
         ],
-    )(edge, dst, ext, aext, z_lo, z_hi, saturation, old_saturation, storage, cell_mask, places)
+        SOLVE_MIB,
+    )(
+        edge, dst, ext, aext, z_lo, z_hi, zm, zp,
+        saturation, old_saturation, storage, cell_mask, places,
+    )
     got = lax.all_to_all(
         send.reshape(devices, chunk, 1, L), AXES, split_axis=0, concat_axis=0, tiled=True
     )

time: 179 us -> 141 us (0.79)
  Pallas kernels: 107 us -> 67 us
  local copies, waits for them, and re-layouts: 6.22 us -> 13 us
  waiting for transfers between devices: 15.9 us -> 10.6 us
    pallas_call x3, Pallas kernels: 79.8 us -> 44.1 us  [the longest x1 37 us: body(): call(solve_kernel, 'solve', shape(devices * chunk, L), 2, 11, pl.ANY, [pl...]
    unnamed x21 -> x35, local copies, waits for them, and re-layouts: 4.08 us -> 12 us
    ppermute x4, waiting for transfers between devices: 15.9 us -> 10.6 us  [swap(): lax.ppermute(high, axis, ring(axis, 1))]
    pallas_call x1, Pallas kernels: 4.73 us -> 2.02 us  [body(): call(prep_kernel, 'prep', (shape(5, T, T, L), shape(4 * H + 2, T, L), sha...]
  transfers between devices with their start and end apart: 8 -> 8, of which waited for: 2 -> 2; matrix products, arithmetic and copies ran while one was open for 3% -> 2% of each run, Pallas kernels for 10% -> 13%
where the time goes in v2:
time: 141 us
  Pallas kernels  67 us (48%)
  blocking collectives  34.2 us (24%)
  starting transfers between devices  13.6 us (10%)
  local copies, waits for them, and re-layouts  13 us (9%)
  waiting for transfers between devices  10.6 us (8%)
  other arithmetic  2.04 us (1%)
    pallas_call x1, Pallas kernels, body(): call(solve_kernel, 'solve', shape(devices * chunk, L), 2, 11, pl.ANY, [pl...  37 us
    all_to_all x1, blocking collectives, body(): lax.all_to_all(send.reshape(devices, chunk, 1, L), AXES, split_axis=0, co...  34.2 us
    pallas_call x1, Pallas kernels, body(): call(index_kernel, 'index', (ints, ints), 2, 0, [pltpu.SMEM] * 2, [pltpu....  16.4 us
    unnamed x35, local copies, waits for them, and re-layouts  12 us
    ppermute x4, waiting for transfers between devices, swap(): lax.ppermute(high, axis, ring(axis, 1))  10.6 us
    ppermute x4, starting transfers between devices, swap(): lax.ppermute(low, axis, ring(axis, -1))  9.78 us
    pallas_call x1, Pallas kernels, body(): call(build_kernel, 'build', (shape(4, EI, EJ + 8, L), shape(2, T + 2, EJ,...  5.7 us
    pallas_call x1, Pallas kernels, body(): call(unpack_kernel, 'unpack', shape(3, SLOTS, L), 0, 1, pl.ANY, [pltpu.VM...  4.47 us
  transfers between devices with their start and end apart: 8, of which 2 were waited for; matrix products, arithmetic and copies ran while one was open for 2% of the time, Pallas kernels for 13%

profile of v2, /device:TPU:0, one launch (start us, length us, event | category | flops | bytes accessed | tf_op | source)
XLA Modules:
  0.0 140.6 jit_solution(15656703281634309737)
XLA Ops:
  0.0 1.2 copy-done.1
  1.2 1.0 copy-done.5
  2.3 1.0 copy-done.7
  3.3 1.0 copy-done.9
  4.4 1.0 copy-done.12
  5.4 2.0 %prep.1 = (f32[5,32,32,128]{3,2,1,0:T(8,128)S(1)}, f32[42,32,128]{2,1,0:T(8,128)}, f32[42,32,128]{2,1,0:T(8,128)}, f32[34,40,128]{2,1,0:T(8,128)}, f32[34,40,128]{2,1,0:T(8,128)}) custom-call(f32[32,32,128]{2,1,0:T(8,128)S(1)} %copy-done.5, f32[2,32,32,128]{3,2,1,0:T(8,128)S(1)} %copy-done.1, f32[32,32,128]{2,1,0:T(8,128)S(1)} %copy-done.12, ...), custom_call_target="tpu_custom_call" | custom-call | tf_op jit(solution)/shard_map/prep/pallas_call | solution.py:555
  7.4 1.5 %copy-done.3 = f32[5,32,32,128]{3,2,1,0:T(8,128)} copy-done((f32[5,32,32,128]{3,2,1,0:T(8,128)}, f32[5,32,32,128]{3,2,1,0:T(8,128)S(1)}, u32[]{:S(2)}) %copy-start.3) | copy-done | bytes 2621464
  8.9 2.0 %collective-permute-start = (f32[42,32,128]{2,1,0:T(8,128)}, f32[42,32,128]{2,1,0:T(8,128)S(1)}, u32[]{:S(2)}, u32[]{:S(2)}) collective-permute-start(f32[42,32,128]{2,1,0:T(8,128)} %get-tuple-element.20), channel_id=1, source_target_pairs={{0,32},{32,64},{64,96},{96,0},{1,33},{33,65},{65,97},{97,1},{2,34}... | collective-permute-start | bytes 2064392 | tf_op jit(solution)/shard_map/ppermute | solution.py:540
  10.9 2.1 %collective-permute-start.1 = (f32[42,32,128]{2,1,0:T(8,128)}, f32[42,32,128]{2,1,0:T(8,128)S(1)}, u32[]{:S(2)}, u32[]{:S(2)}) collective-permute-start(f32[42,32,128]{2,1,0:T(8,128)} %get-tuple-element.21), channel_id=1, source_target_pairs={{0,96},{32,0},{64,32},{96,64},{1,97},{33,1},{65,33},{97,65},{2,98}... | collective-permute-start | bytes 2064392 | tf_op jit(solution)/shard_map/ppermute | solution.py:540
  13.1 1.5 %collective-permute-start.2 = (f32[34,40,128]{2,1,0:T(8,128)}, f32[34,40,128]{2,1,0:T(8,128)S(1)}, u32[]{:S(2)}, u32[]{:S(2)}) collective-permute-start(f32[34,40,128]{2,1,0:T(8,128)} %get-tuple-element.22), channel_id=1, source_target_pairs={{0,8},{8,16},{16,24},{24,0},{1,9},{9,17},{17,25},{25,1},{2,10},{10... | collective-permute-start | bytes 2088968 | tf_op jit(solution)/shard_map/ppermute | solution.py:540
  14.6 1.7 %collective-permute-start.3 = (f32[34,40,128]{2,1,0:T(8,128)}, f32[34,40,128]{2,1,0:T(8,128)S(1)}, u32[]{:S(2)}, u32[]{:S(2)}) collective-permute-start(f32[34,40,128]{2,1,0:T(8,128)} %get-tuple-element.23), channel_id=1, source_target_pairs={{0,24},{8,0},{16,8},{24,16},{1,25},{9,1},{17,9},{25,17},{2,26},{10... | collective-permute-start | bytes 2088968 | tf_op jit(solution)/shard_map/ppermute | solution.py:540
  16.3 0.5 broadcast.8
  16.8 0.7 reduce.6
  17.5 0.1 reshape.14.owner
  17.6 0.7 reduce.7
  18.3 0.1 reshape.15.slot
  18.4 16.4 %index.1 = (s32[1024]{0:T(1024)S(1)}, s32[1024]{0:T(1024)S(1)}) custom-call(s32[1024]{0:T(1024)S(1)} %reshape.14.owner, s32[1024]{0:T(1024)S(1)} %reshape.15.slot), custom_call_target="tpu_custom_call" | custom-call | tf_op jit(solution)/shard_map/index/pallas_call | solution.py:572
  34.8 0.1 convert_element_type.13
  34.9 1.4 strip.1
  36.3 0.3 collective-permute-start.4
  36.6 3.0 %collective-permute-start.5 = (f32[4,96,128]{2,1,0:T(8,128)}, f32[4,96,128]{2,1,0:T(8,128)}, u32[]{:S(2)}, u32[]{:S(2)}) collective-permute-start(f32[4,96,128]{2,1,0:T(8,128)} %get-tuple-element.26), channel_id=1, source_target_pairs={{0,24},{8,0},{16,8},{24,16},{1,25},{9,1},{17,9},{25,17},{2,26},{10... | collective-permute-start | bytes 589832 | tf_op jit(solution)/shard_map/ppermute | solution.py:540
  39.6 0.7 stack.27
  40.3 0.7 convert_element_type.11.edge
  40.9 2.6 %collective-permute-done.4.c_lo = f32[4,96,128]{2,1,0:T(8,128)S(1)} collective-permute-done((f32[4,96,128]{2,1,0:T(8,128)}, f32[4,96,128]{2,1,0:T(8,128)S(1)}, u32[]{:S(2)}, u32[]{:S(2)}) %collective-permute-start.4) | collective-permute-done | bytes 196640 | tf_op jit(solution)/shard_map/ppermute | solution.py:540
  43.6 1.7 %copy-done.4 = f32[5,32,32,128]{3,2,1,0:T(8,128)S(1)} copy-done((f32[5,32,32,128]{3,2,1,0:T(8,128)S(1)}, f32[5,32,32,128]{3,2,1,0:T(8,128)}, u32[]{:S(2)}) %copy-start.4) | copy-done | bytes 2621464
  45.3 5.7 %build.1 = (f32[4,52,64,128]{3,2,1,0:T(8,128)S(1)}, f32[2,34,56,128]{3,2,1,0:T(8,128)S(1)}, f32[22,56,128]{2,1,0:T(8,128)S(1)}, f32[22,56,128]{2,1,0:T(8,128)S(1)}) custom-call(f32[6]{0:T(128)S(1)} %convert_element_type.11.edge, f32[32,32,128]{2,1,0:T(8,128)S(1)} %copy-done.6, f32[5,32,32,128]{3,2,1,0:T(8,128)S(1)} %copy-done.4, ...), custom_call_target="tpu_custom_call" | custom-call | tf_op jit(solution)/shard_map/build/pallas_call | solution.py:589
  51.0 2.8 %copy-done = f32[4,52,64,128]{3,2,1,0:T(8,128)} copy-done((f32[4,52,64,128]{3,2,1,0:T(8,128)}, f32[4,52,64,128]{3,2,1,0:T(8,128)S(1)}, u32[]{:S(2)}) %copy-start) | copy-done | bytes 6815768
  53.9 3.0 %collective-permute-start.7 = (f32[22,56,128]{2,1,0:T(8,128)S(1)}, f32[22,56,128]{2,1,0:T(8,128)S(1)}, u32[]{:S(2)}, u32[]{:S(2)}) collective-permute-start(f32[22,56,128]{2,1,0:T(8,128)S(1)} %get-tuple-element.30.z_first), channel_id=1, source_target_pairs={{0,7},{1,0},{2,1},{3,2},{4,3},{5,4},{6,5},{7,6},{8,15},{9,8},{10,9... | collective-permute-start | bytes 1892360 | tf_op jit(solution)/shard_map/ppermute | solution.py:540
  56.8 8.0 %collective-permute-done.6.z_lo = f32[22,56,128]{2,1,0:T(8,128)S(1)} collective-permute-done((f32[22,56,128]{2,1,0:T(8,128)S(1)}, f32[22,56,128]{2,1,0:T(8,128)S(1)}, u32[]{:S(2)}, u32[]{:S(2)}) %collective-permute-start.6) | collective-permute-done | bytes 630816 | tf_op jit(solution)/shard_map/ppermute | solution.py:540
  64.9 37.0 %solve.1 = f32[3200,128]{1,0:T(8,128)S(1)} custom-call(f32[6]{0:T(128)S(1)} %convert_element_type.11.edge, s32[1024]{0:T(1024)S(1)} %copy-done.14, f32[4,52,64,128]{3,2,1,0:T(8,128)} %copy-done, f32[2,34,56,128]{3,2,1,0:T(8,128)S(1)} %get-tuple-element.28.aext, f32[22,56,128]{2,1,0:T(8,128)S(1)} %collective-permute-done.6.z_lo, ...), custom_call_target="tpu_custom_call" | custom-call | tf_op jit(solution)/shard_map/solve/pallas_call | solution.py:598
  101.8 34.2 %all_to_all.5 = f32[128,25,1,128]{3,2,1,0:T(1,128)S(1)} all-to-all(f32[128,25,1,128]{3,2,1,0:T(1,128)S(1)} %bitcast.10), channel_id=1, replica_groups=mesh['gx'=4,'gy'=4,'gz'=8] {'gx','gy','gz'}, dimensions={0} | all-to-all | bytes 3276800 | tf_op jit(solution)/shard_map/all_to_all | solution.py:628
  136.1 4.5 %unpack.1 = f32[3,640,128]{2,1,0:T(8,128)} custom-call(f32[3200,128]{1,0:T(8,128)S(1)} %bitcast.11), custom_call_target="tpu_custom_call" | custom-call | tf_op jit(solution)/shard_map/unpack/pallas_call | solution.py:631
  (35 shorter events, 0.1 us)
Async XLA Ops:
  0.0 1.2 copy-start.1
  1.2 1.0 copy-start.5
  2.3 1.0 copy-start.7
  3.3 1.0 copy-start.9
  4.4 1.0 copy-start.12
  5.4 11.4 %copy-start.15 = (s32[32,32,1]{1,2,0:T(1,128)S(1)}, s32[32,32,1]{1,2,0:T(1,128)}, u32[]{:S(2)}) copy-start(s32[32,32,1]{1,2,0:T(1,128)} %param.14) | copy-start | bytes 12292
  5.4 12.2 %copy-start.16 = (s32[32,32,1]{1,2,0:T(1,128)S(1)}, s32[32,32,1]{1,2,0:T(1,128)}, u32[]{:S(2)}) copy-start(s32[32,32,1]{1,2,0:T(1,128)} %param.15) | copy-start | bytes 12292
  5.4 38.2 %copy-start.6 = (f32[32,32,128]{2,1,0:T(8,128)S(1)}, f32[32,32,128]{2,1,0:T(8,128)}, u32[]{:S(2)}) copy-start(f32[32,32,128]{2,1,0:T(8,128)} %p.3) | copy-start | bytes 1572868
  7.4 1.5 %copy-start.3 = (f32[5,32,32,128]{3,2,1,0:T(8,128)}, f32[5,32,32,128]{3,2,1,0:T(8,128)S(1)}, u32[]{:S(2)}) copy-start(f32[5,32,32,128]{3,2,1,0:T(8,128)S(1)} %get-tuple-element.19.own) | copy-start | bytes 7864324
  8.9 26.0 %collective-permute-start = (f32[42,32,128]{2,1,0:T(8,128)}, f32[42,32,128]{2,1,0:T(8,128)S(1)}, u32[]{:S(2)}, u32[]{:S(2)}) collective-permute-start(f32[42,32,128]{2,1,0:T(8,128)} %get-tuple-element.20), channel_id=1, source_target_pairs={{0,32},{32,64},{64,96},{96,0},{1,33},{33,65},{65,97},{97,1},{2,34}... | collective-permute-start | bytes 2064392 | tf_op jit(solution)/shard_map/ppermute | solution.py:540
  10.9 24.0 %collective-permute-start.1 = (f32[42,32,128]{2,1,0:T(8,128)}, f32[42,32,128]{2,1,0:T(8,128)S(1)}, u32[]{:S(2)}, u32[]{:S(2)}) collective-permute-start(f32[42,32,128]{2,1,0:T(8,128)} %get-tuple-element.21), channel_id=1, source_target_pairs={{0,96},{32,0},{64,32},{96,64},{1,97},{33,1},{65,33},{97,65},{2,98}... | collective-permute-start | bytes 2064392 | tf_op jit(solution)/shard_map/ppermute | solution.py:540
  13.1 27.9 %collective-permute-start.2 = (f32[34,40,128]{2,1,0:T(8,128)}, f32[34,40,128]{2,1,0:T(8,128)S(1)}, u32[]{:S(2)}, u32[]{:S(2)}) collective-permute-start(f32[34,40,128]{2,1,0:T(8,128)} %get-tuple-element.22), channel_id=1, source_target_pairs={{0,8},{8,16},{16,24},{24,0},{1,9},{9,17},{17,25},{25,1},{2,10},{10... | collective-permute-start | bytes 2088968 | tf_op jit(solution)/shard_map/ppermute | solution.py:540
  14.6 26.4 %collective-permute-start.3 = (f32[34,40,128]{2,1,0:T(8,128)}, f32[34,40,128]{2,1,0:T(8,128)S(1)}, u32[]{:S(2)}, u32[]{:S(2)}) collective-permute-start(f32[34,40,128]{2,1,0:T(8,128)} %get-tuple-element.23), channel_id=1, source_target_pairs={{0,24},{8,0},{16,8},{24,16},{1,25},{9,1},{17,9},{25,17},{2,26},{10... | collective-permute-start | bytes 2088968 | tf_op jit(solution)/shard_map/ppermute | solution.py:540
  34.8 1.6 %copy-start.13 = (s32[1024]{0:T(1024)}, s32[1024]{0:T(1024)S(1)}, u32[]{:S(2)}) copy-start(s32[1024]{0:T(1024)S(1)} %get-tuple-element.18.dst) | copy-start | bytes 12292
  36.3 7.2 %collective-permute-start.4 = (f32[4,96,128]{2,1,0:T(8,128)}, f32[4,96,128]{2,1,0:T(8,128)S(1)}, u32[]{:S(2)}, u32[]{:S(2)}) collective-permute-start(f32[4,96,128]{2,1,0:T(8,128)} %get-tuple-element.25), channel_id=1, source_target_pairs={{0,8},{8,16},{16,24},{24,0},{1,9},{9,17},{17,25},{25,1},{2,10},{10... | collective-permute-start | bytes 589832 | tf_op jit(solution)/shard_map/ppermute | solution.py:540
  36.6 6.9 %collective-permute-start.5 = (f32[4,96,128]{2,1,0:T(8,128)}, f32[4,96,128]{2,1,0:T(8,128)}, u32[]{:S(2)}, u32[]{:S(2)}) collective-permute-start(f32[4,96,128]{2,1,0:T(8,128)} %get-tuple-element.26), channel_id=1, source_target_pairs={{0,24},{8,0},{16,8},{24,16},{1,25},{9,1},{17,9},{25,17},{2,26},{10... | collective-permute-start | bytes 589832 | tf_op jit(solution)/shard_map/ppermute | solution.py:540
  43.6 1.7 %copy-start.4 = (f32[5,32,32,128]{3,2,1,0:T(8,128)S(1)}, f32[5,32,32,128]{3,2,1,0:T(8,128)}, u32[]{:S(2)}) copy-start(f32[5,32,32,128]{3,2,1,0:T(8,128)} %copy-done.3) | copy-start | bytes 7864324
  45.3 19.5 %copy-start.2 = (f32[2,32,32,128]{3,2,1,0:T(8,128)S(1)}, f32[2,32,32,128]{3,2,1,0:T(8,128)}, u32[]{:S(2)}) copy-start(f32[2,32,32,128]{3,2,1,0:T(8,128)} %sat.3) | copy-start | bytes 3145732
  45.3 19.5 %copy-start.8 = (f32[32,32,128]{2,1,0:T(8,128)S(1)}, f32[32,32,128]{2,1,0:T(8,128)}, u32[]{:S(2)}) copy-start(f32[32,32,128]{2,1,0:T(8,128)} %sto.3) | copy-start | bytes 1572868
  45.3 19.5 %copy-start.10 = (s32[32,32,128]{2,1,0:T(8,128)S(1)}, s32[32,32,128]{2,1,0:T(8,128)}, u32[]{:S(2)}) copy-start(s32[32,32,128]{2,1,0:T(8,128)} %mask.3) | copy-start | bytes 1572868
  45.3 19.5 %copy-start.11 = (f32[2,32,32,128]{3,2,1,0:T(8,128)S(1)}, f32[2,32,32,128]{3,2,1,0:T(8,128)}, u32[]{:S(2)}) copy-start(f32[2,32,32,128]{3,2,1,0:T(8,128)} %old.1) | copy-start | bytes 3145732
  45.3 19.5 %copy-start.14 = (s32[1024]{0:T(1024)S(1)}, s32[1024]{0:T(1024)}, u32[]{:S(2)}) copy-start(s32[1024]{0:T(1024)} %copy-done.13) | copy-start | bytes 12292
  51.0 2.8 %copy-start = (f32[4,52,64,128]{3,2,1,0:T(8,128)}, f32[4,52,64,128]{3,2,1,0:T(8,128)S(1)}, u32[]{:S(2)}) copy-start(f32[4,52,64,128]{3,2,1,0:T(8,128)S(1)} %get-tuple-element.27.ext) | copy-start | bytes 20447236
  53.9 11.0 %collective-permute-start.6 = (f32[22,56,128]{2,1,0:T(8,128)S(1)}, f32[22,56,128]{2,1,0:T(8,128)S(1)}, u32[]{:S(2)}, u32[]{:S(2)}) collective-permute-start(f32[22,56,128]{2,1,0:T(8,128)S(1)} %get-tuple-element.29.z_last), channel_id=1, source_target_pairs={{0,1},{1,2},{2,3},{3,4},{4,5},{5,6},{6,7},{7,0},{8,9},{9,10},{10,1... | collective-permute-start | bytes 1892360 | tf_op jit(solution)/shard_map/ppermute | solution.py:540
  53.9 11.0 %collective-permute-start.7 = (f32[22,56,128]{2,1,0:T(8,128)S(1)}, f32[22,56,128]{2,1,0:T(8,128)S(1)}, u32[]{:S(2)}, u32[]{:S(2)}) collective-permute-start(f32[22,56,128]{2,1,0:T(8,128)S(1)} %get-tuple-element.30.z_first), channel_id=1, source_target_pairs={{0,7},{1,0},{2,1},{3,2},{4,3},{5,4},{6,5},{7,6},{8,15},{9,8},{10,9... | collective-permute-start | bytes 1892360 | tf_op jit(solution)/shard_map/ppermute | solution.py:540

commit v3 on v2

--- a/solution.py
+++ b/solution.py
@@ -17,7 +17,7 @@
 SLOTS = 640
 ZG = 10
 NQ = 5
-SOLVE_MIB = 42
+SOLVE_MIB = 34
 PAD = 8
 ZS = 12
 
@@ -187,7 +187,7 @@
 
 def solve_kernel(
     edge, dst, ext, aext, z_lo, z_hi, z_first, z_last, sat, old, sto, mask, places, send,
-    side, rim, back, mat, zmat, base, one, two, zbase, zone, ztwo, border, total, share, spare, rows, stage, sem,
+    side, rim, back, mat, zmat, base, one, two, zbase, zone, ztwo, border, total, share, rows, stage, sem,
 ):
     lane = lanes_of(EJ)
     part = lax.rem(lane, ZS)
@@ -299,11 +299,11 @@
         lax.fori_loop(0, NQ, plane, 0)
 
     def sweep(src, zsrc, target, ztarget, depth):
-        low, high = (0, EJ) if depth > 3 else (8, 48)
+        low, high = (4, 52) if depth > 4 else (8, 48)
         at = slice(low, high)
         y_at = slice(PAD + low, PAD + high)
         y_up, y_down = (slice(y_at.start + k, y_at.stop + k) for k in (1, -1))
-        lanes = lane[at]
+        lanes = lanes_of(high - low)
         prepare(zsrc)
 
         def halo(q, carry):
@@ -348,9 +348,9 @@
         src, zsrc = target, ztarget
     prepare(zsrc)
 
-    mid, mid_up, mid_down = slice(8, 48), slice(9, 49), slice(7, 47)
-    y_mid, y_up, y_down = (slice(PAD + k, PAD + 40 + k) for k in (8, 9, 7))
-    lanes = lane[mid]
+    mid, mid_up, mid_down = (slice(k, k + T) for k in (OJ, OJ + 1, OJ - 1))
+    y_mid, y_up, y_down = (slice(PAD + k, PAD + k + T) for k in (OJ, OJ + 1, OJ - 1))
+    lanes = lanes_of(T)
     even = lax.rem(lanes, 2) == 0
     for f in range(2):
         share[f] = jnp.where(even, z_hi[4 * NQ + f, mid], z_lo[4 * NQ + f, mid])
@@ -385,8 +385,8 @@
         x_p = base[e, y_mid]
         for k in range(6):
             x_p = x_p + mat[k, e, mid] * s_near[k]
-        column = [jnp.zeros((40, L), F32) for _ in range(2)]
-        drive = [jnp.zeros((40, L), F32) for _ in range(2)]
+        column = [jnp.zeros((T, L), F32) for _ in range(2)]
+        drive = [jnp.zeros((T, L), F32) for _ in range(2)]
         for k in range(6):
             weight = mat[k, e, mid]
             upstream = pa >= p_near[k]
@@ -397,10 +397,8 @@
                 drive[f] = drive[f] + w * step
         scale = total[e, mid]
         shift = -ZS * g
-        spare[0] = turn(x_p, shift)
-        for f in range(2):
-            spare[1 + f] = turn((drive[f] - column[f] * x_p) * scale, shift)
-        x_p = spare[0, 4:36]
+        coupled = [turn((drive[f] - column[f] * x_p) * scale, shift) for f in range(2)]
+        x_p = turn(x_p, shift)
         act = mask[i].astype(F32)
         held = act * sto[i]
         idle = 1.0 - act
@@ -410,7 +408,7 @@
             s_now = sat[f, i]
             local = (held * (compress * s_now) + idle) * x_p
             change = held * (s_now - old[f, i])
-            stage[1 + f, i] = (spare[1 + f, 4:36] - change - local) * inverse
+            stage[1 + f, i] = (coupled[f] - change - local) * inverse
 
     def group(g, carry):
         marks = spots(g, lanes)
@@ -445,39 +443,38 @@
     copy.wait()
 
 
-def index_kernel(owner, slot, dst, place, count):
-    devices = count.shape[0]
+def index_kernel(owner, slot, dst, places):
+    devices = places.shape[0]
     capacity = T * T // devices
     chunk = 3 * capacity + 1
-
-    def clear(d, carry):
-        count[d] = 0
-        return carry
-
-    def blank(d, carry):
-        place[d] = -1
-        return carry
-
-    lax.fori_loop(0, devices, clear, 0)
-    lax.fori_loop(0, T * T, blank, 0, unroll=8)
-
-    def row(r, carry):
-        o = owner[r]
-
-        @pl.when(o >= 0)
-        def _():
-            n = count[o]
-            count[o] = n + 1
-            place[o * capacity + n] = slot[r]
-            dst[r] = o * chunk + n
-
-        @pl.when(o < 0)
-        def _():
-            dst[r] = devices * chunk
-
-        return carry
-
-    lax.fori_loop(0, T * T, row, 0)
+    bf16 = jnp.bfloat16
+    who = lax.broadcasted_iota(jnp.int32, (devices, L), 0)
+    spot = lax.broadcasted_iota(jnp.int32, (L, L), 0)
+    earlier = (spot < lax.broadcasted_iota(jnp.int32, (L, L), 1)).astype(F32).astype(bf16)
+    count = jnp.zeros((devices, 1), F32)
+    coarse = jnp.zeros((devices, L), F32)
+    fine = coarse
+    for c in range(T * T // L):
+        own = owner[c : c + 1]
+        hit = (who == own).astype(F32)
+        ahead = jnp.dot(hit.astype(bf16), earlier, preferred_element_type=F32) + count
+        count = count + jnp.sum(hit, axis=1, keepdims=True)
+        rank = jnp.sum(hit * ahead, axis=0, keepdims=True).astype(jnp.int32)
+        dst[c : c + 1] = jnp.where(own >= 0, own * chunk + rank, devices * chunk)
+        place = slot[c : c + 1]
+        high = lax.div(place, 32)
+        here = spot == rank
+        for part, value in enumerate((high, place - 32 * high)):
+            row = jnp.where(here, value.astype(F32), 0.0).astype(bf16)
+            found = lax.dot_general(
+                hit.astype(bf16), row, (((1,), (1,)), ((), ())), preferred_element_type=F32
+            )
+            if part == 0:
+                coarse = coarse + found
+            else:
+                fine = fine + found
+    lane = lax.broadcasted_iota(jnp.int32, (devices, L), 1).astype(F32)
+    places[...] = jnp.where(lane < count, 32.0 * coarse + fine, -1.0)
 
 
 def unpack_kernel(got, update, held, number, table, where, sem):
@@ -564,23 +561,16 @@
         ),
         0,
         5,
+        limit=60,
     )(pressure, saturation, permeability, storage, cell_mask)
     x_lo, x_hi = swap(xm, xp, "gx")
     y_lo, y_hi = swap(ym, yp, "gy")
 
-    ints = jax.ShapeDtypeStruct((T * T,), jnp.int32)
-    dst, place = call(
-        index_kernel,
-        "index",
-        (ints, ints),
-        2,
-        0,
-        [pltpu.SMEM] * 2,
-        [pltpu.SMEM((devices,), jnp.int32)],
-    )(row_owner.reshape(T * T), row_slot.reshape(T * T))
-    places = jnp.pad(
-        place.reshape(devices, capacity).astype(F32), ((0, 0), (0, L - capacity))
-    )
+    table = (T * T // L, L)
+    dst, places = call(
+        index_kernel, "index", (jax.ShapeDtypeStruct(table, jnp.int32), shape(devices, L)), 0, 2
+    )(row_owner.reshape(table), row_slot.reshape(table))
+    dst = dst.reshape(T * T)
 
     cm, cp = call(strip_kernel, "strip", (shape(4, 96, L), shape(4, 96, L)), 1, 3)(
         dst, x_lo, x_hi, places
@@ -614,8 +604,7 @@
         + [
             pltpu.VMEM((NQ, EJ, L), F32),
             pltpu.VMEM((EI, EJ, L), F32),
-            pltpu.VMEM((2, 40, L), F32),
-            pltpu.VMEM((3, 40, L), F32),
+            pltpu.VMEM((2, T, L), F32),
             pltpu.VMEM((devices * chunk + 2 * capacity + 8, L), F32),
             pltpu.VMEM((3, T, T, L), F32),
             pltpu.SemaphoreType.DMA(()),

time: 141 us -> 124 us (0.88)
  Pallas kernels: 67 us -> 50.5 us
  local copies, waits for them, and re-layouts: 13 us -> 3.08 us
  waiting for transfers between devices: 10.6 us -> 19.8 us
    pallas_call x1, Pallas kernels: 16.4 us -> 1.63 us  [body(): call(index_kernel, 'index', (jax.ShapeDtypeStruct(table, jnp.int32), shap...]
    unnamed x35 -> x21, local copies, waits for them, and re-layouts: 12 us -> 2.29 us
    ppermute x4, waiting for transfers between devices: 10.6 us -> 19.7 us  [swap(): lax.ppermute(high, axis, ring(axis, 1))]
    pallas_call x1, Pallas kernels: 37 us -> 32.5 us  [body(): call(solve_kernel, 'solve', shape(devices * chunk, L), 2, 11, pl.ANY, [pl...]
    pallas_call x1, Pallas kernels: 2.02 us -> 4.77 us  [body(): call(prep_kernel, 'prep', (shape(5, T, T, L), shape(4 * H + 2, T, L), sha...]
  transfers between devices with their start and end apart: 8 -> 8, of which waited for: 2 -> 4; matrix products, arithmetic and copies ran while one was open for 2% -> 3% of each run, Pallas kernels for 13% -> 2%
where the time goes in v3:
time: 124 us
  Pallas kernels  50.5 us (41%)
  blocking collectives  34.8 us (28%)
  waiting for transfers between devices  19.8 us (16%)
  starting transfers between devices  13.6 us (11%)
  local copies, waits for them, and re-layouts  3.08 us (2%)
  other arithmetic  1.95 us (2%)
    all_to_all x1, blocking collectives, body(): lax.all_to_all(send.reshape(devices, chunk, 1, L), AXES, split_axis=0, co...  34.8 us
    pallas_call x1, Pallas kernels, body(): call(solve_kernel, 'solve', shape(devices * chunk, L), 2, 11, pl.ANY, [pl...  32.5 us
    ppermute x4, waiting for transfers between devices, swap(): lax.ppermute(high, axis, ring(axis, 1))  19.7 us
    ppermute x4, starting transfers between devices, swap(): lax.ppermute(low, axis, ring(axis, -1))  8.56 us
    pallas_call x1, Pallas kernels, body(): call(build_kernel, 'build', (shape(4, EI, EJ + 8, L), shape(2, T + 2, EJ,...  5.7 us
    ppermute x4, starting transfers between devices, swap(): lax.ppermute(high, axis, ring(axis, 1))  5.03 us
    pallas_call x1, Pallas kernels, body(): call(prep_kernel, 'prep', (shape(5, T, T, L), shape(4 * H + 2, T, L), sha...  4.77 us
    pallas_call x1, Pallas kernels, body(): call(unpack_kernel, 'unpack', shape(3, SLOTS, L), 0, 1, pl.ANY, [pltpu.VM...  4.47 us
  transfers between devices with their start and end apart: 8, of which 4 were waited for; matrix products, arithmetic and copies ran while one was open for 3% of the time, Pallas kernels for 2%

profile of v3, /device:TPU:0, one launch (start us, length us, event | category | flops | bytes accessed | tf_op | source)
XLA Modules:
  0.0 123.8 jit_solution(10644030825596678708)
XLA Ops:
  0.0 4.8 %prep.1 = (f32[5,32,32,128]{3,2,1,0:T(8,128)}, f32[42,32,128]{2,1,0:T(8,128)}, f32[42,32,128]{2,1,0:T(8,128)}, f32[34,40,128]{2,1,0:T(8,128)}, f32[34,40,128]{2,1,0:T(8,128)}) custom-call(f32[32,32,128]{2,1,0:T(8,128)} %p.3, f32[2,32,32,128]{3,2,1,0:T(8,128)} %sat.3, f32[32,32,128]{2,1,0:T(8,128)} %perm.1, f32[32,32,128]{2,1,0:T(8,128)} %sto.3, ...), custom_call_target="tpu_custom_call" | custom-call | tf_op jit(solution)/shard_map/prep/pallas_call | solution.py:552
  4.8 2.0 %collective-permute-start = (f32[42,32,128]{2,1,0:T(8,128)}, f32[42,32,128]{2,1,0:T(8,128)S(1)}, u32[]{:S(2)}, u32[]{:S(2)}) collective-permute-start(f32[42,32,128]{2,1,0:T(8,128)} %get-tuple-element.20), channel_id=1, source_target_pairs={{0,32},{32,64},{64,96},{96,0},{1,33},{33,65},{65,97},{97,1},{2,34}... | collective-permute-start | bytes 2064392 | tf_op jit(solution)/shard_map/ppermute | solution.py:537
  6.8 2.1 %collective-permute-start.1 = (f32[42,32,128]{2,1,0:T(8,128)}, f32[42,32,128]{2,1,0:T(8,128)S(1)}, u32[]{:S(2)}, u32[]{:S(2)}) collective-permute-start(f32[42,32,128]{2,1,0:T(8,128)} %get-tuple-element.21), channel_id=1, source_target_pairs={{0,96},{32,0},{64,32},{96,64},{1,97},{33,1},{65,33},{97,65},{2,98}... | collective-permute-start | bytes 2064392 | tf_op jit(solution)/shard_map/ppermute | solution.py:537
  8.9 1.5 %collective-permute-start.2 = (f32[34,40,128]{2,1,0:T(8,128)}, f32[34,40,128]{2,1,0:T(8,128)S(1)}, u32[]{:S(2)}, u32[]{:S(2)}) collective-permute-start(f32[34,40,128]{2,1,0:T(8,128)} %get-tuple-element.22), channel_id=1, source_target_pairs={{0,8},{8,16},{16,24},{24,0},{1,9},{9,17},{17,25},{25,1},{2,10},{10... | collective-permute-start | bytes 2088968 | tf_op jit(solution)/shard_map/ppermute | solution.py:537
  10.4 1.7 %collective-permute-start.3 = (f32[34,40,128]{2,1,0:T(8,128)}, f32[34,40,128]{2,1,0:T(8,128)S(1)}, u32[]{:S(2)}, u32[]{:S(2)}) collective-permute-start(f32[34,40,128]{2,1,0:T(8,128)} %get-tuple-element.23), channel_id=1, source_target_pairs={{0,24},{8,0},{16,8},{24,16},{1,25},{9,1},{17,9},{25,17},{2,26},{10... | collective-permute-start | bytes 2088968 | tf_op jit(solution)/shard_map/ppermute | solution.py:537
  12.2 0.5 broadcast.6
  12.7 0.7 reduce.6
  13.4 0.1 reshape.15.owner
  13.4 0.7 reduce.7
  14.1 0.1 reshape.16.slot
  14.2 1.6 %index.1 = (s32[8,128]{1,0:T(8,128)S(1)}, f32[128,128]{1,0:T(8,128)S(1)}) custom-call(s32[8,128]{1,0:T(8,128)S(1)} %reshape.15.owner, s32[8,128]{1,0:T(8,128)S(1)} %reshape.16.slot), custom_call_target="tpu_custom_call" | custom-call | tf_op jit(solution)/shard_map/index/pallas_call | solution.py:570
  15.8 8.8 %collective-permute-done.x_lo = f32[42,32,128]{2,1,0:T(8,128)S(1)} collective-permute-done((f32[42,32,128]{2,1,0:T(8,128)}, f32[42,32,128]{2,1,0:T(8,128)S(1)}, u32[]{:S(2)}, u32[]{:S(2)}) %collective-permute-start) | collective-permute-done | bytes 688160 | tf_op jit(solution)/shard_map/ppermute | solution.py:537
  24.6 0.0 collective-permute-done.1.x_hi
  24.6 1.4 %strip.1 = (f32[4,96,128]{2,1,0:T(8,128)}, f32[4,96,128]{2,1,0:T(8,128)}) custom-call(s32[1024]{0:T(1024)S(1)} %bitcast.13, f32[42,32,128]{2,1,0:T(8,128)S(1)} %collective-permute-done.x_lo, f32[42,32,128]{2,1,0:T(8,128)S(1)} %collective-permute-done.1.x_hi, f32[128,128]{1,0:T(8,128)S(1)} %get-tuple-element.24.places), custom_call_target="tpu_custom_call" | custom-call | tf_op jit(solution)/shard_map/strip/pallas_call | solution.py:575
  26.0 1.5 %collective-permute-start.4 = (f32[4,96,128]{2,1,0:T(8,128)}, f32[4,96,128]{2,1,0:T(8,128)S(1)}, u32[]{:S(2)}, u32[]{:S(2)}) collective-permute-start(f32[4,96,128]{2,1,0:T(8,128)} %get-tuple-element.25), channel_id=1, source_target_pairs={{0,8},{8,16},{16,24},{24,0},{1,9},{9,17},{17,25},{25,1},{2,10},{10... | collective-permute-start | bytes 589832 | tf_op jit(solution)/shard_map/ppermute | solution.py:537
  27.5 1.7 %collective-permute-start.5 = (f32[4,96,128]{2,1,0:T(8,128)}, f32[4,96,128]{2,1,0:T(8,128)}, u32[]{:S(2)}, u32[]{:S(2)}) collective-permute-start(f32[4,96,128]{2,1,0:T(8,128)} %get-tuple-element.26), channel_id=1, source_target_pairs={{0,24},{8,0},{16,8},{24,16},{1,25},{9,1},{17,9},{25,17},{2,26},{10... | collective-permute-start | bytes 589832 | tf_op jit(solution)/shard_map/ppermute | solution.py:537
  29.2 0.6 stack.27
  29.9 0.6 convert_element_type.3.edge
  30.5 0.0 collective-permute-done.2.y_lo
  30.5 0.0 collective-permute-done.3.y_hi
  30.5 3.0 %collective-permute-done.4.c_lo = f32[4,96,128]{2,1,0:T(8,128)S(1)} collective-permute-done((f32[4,96,128]{2,1,0:T(8,128)}, f32[4,96,128]{2,1,0:T(8,128)S(1)}, u32[]{:S(2)}, u32[]{:S(2)}) %collective-permute-start.4) | collective-permute-done | bytes 196640 | tf_op jit(solution)/shard_map/ppermute | solution.py:537
  33.5 0.1 collective-permute-done.5.c_hi
  33.6 1.7 %copy-done.1 = f32[5,32,32,128]{3,2,1,0:T(8,128)S(1)} copy-done((f32[5,32,32,128]{3,2,1,0:T(8,128)S(1)}, f32[5,32,32,128]{3,2,1,0:T(8,128)}, u32[]{:S(2)}) %copy-start.1) | copy-done | bytes 2621464
  35.4 5.7 %build.1 = (f32[4,52,64,128]{3,2,1,0:T(8,128)S(1)}, f32[2,34,56,128]{3,2,1,0:T(8,128)S(1)}, f32[22,56,128]{2,1,0:T(8,128)S(1)}, f32[22,56,128]{2,1,0:T(8,128)S(1)}) custom-call(f32[6]{0:T(128)S(1)} %convert_element_type.3.edge, f32[32,32,128]{2,1,0:T(8,128)S(1)} %copy-done.2, f32[5,32,32,128]{3,2,1,0:T(8,128)S(1)} %copy-done.1, ...), custom_call_target="tpu_custom_call" | custom-call | tf_op jit(solution)/shard_map/build/pallas_call | solution.py:579
  41.1 0.0 collective-permute-start.6
  41.1 2.9 %collective-permute-start.7 = (f32[22,56,128]{2,1,0:T(8,128)S(1)}, f32[22,56,128]{2,1,0:T(8,128)S(1)}, u32[]{:S(2)}, u32[]{:S(2)}) collective-permute-start(f32[22,56,128]{2,1,0:T(8,128)S(1)} %get-tuple-element.30.z_first), channel_id=1, source_target_pairs={{0,7},{1,0},{2,1},{3,2},{4,3},{5,4},{6,5},{7,6},{8,15},{9,8},{10,9... | collective-permute-start | bytes 1892360 | tf_op jit(solution)/shard_map/ppermute | solution.py:537
  44.0 8.0 %collective-permute-done.6.z_lo = f32[22,56,128]{2,1,0:T(8,128)S(1)} collective-permute-done((f32[22,56,128]{2,1,0:T(8,128)S(1)}, f32[22,56,128]{2,1,0:T(8,128)S(1)}, u32[]{:S(2)}, u32[]{:S(2)}) %collective-permute-start.6) | collective-permute-done | bytes 630816 | tf_op jit(solution)/shard_map/ppermute | solution.py:537
  52.0 0.0 collective-permute-done.7.z_hi
  52.0 0.0 copy-done.4
  52.1 32.5 %solve.1 = f32[3200,128]{1,0:T(8,128)S(1)} custom-call(f32[6]{0:T(128)S(1)} %convert_element_type.3.edge, s32[1024]{0:T(1024)S(1)} %bitcast.14, f32[4,52,64,128]{3,2,1,0:T(8,128)S(1)} %get-tuple-element.27.ext, f32[2,34,56,128]{3,2,1,0:T(8,128)S(1)} %get-tuple-element.28.aext, f32[22,56,128]{2,1,0:T(8,128)S(1)} %collective-permute-done.6.z_lo, ...), custom_call_target="tpu_custom_call" | custom-call | tf_op jit(solution)/shard_map/solve/pallas_call | solution.py:588
  84.5 34.8 %all_to_all.5 = f32[128,25,1,128]{3,2,1,0:T(1,128)S(1)} all-to-all(f32[128,25,1,128]{3,2,1,0:T(1,128)S(1)} %bitcast.11), channel_id=1, replica_groups=mesh['gx'=4,'gy'=4,'gz'=8] {'gx','gy','gz'}, dimensions={0} | all-to-all | bytes 3276800 | tf_op jit(solution)/shard_map/all_to_all | solution.py:617
  119.3 4.5 %unpack.1 = f32[3,640,128]{2,1,0:T(8,128)} custom-call(f32[3200,128]{1,0:T(8,128)S(1)} %bitcast.12), custom_call_target="tpu_custom_call" | custom-call | tf_op jit(solution)/shard_map/unpack/pallas_call | solution.py:620
  (18 shorter events, 0.0 us)
Async XLA Ops:
  0.0 33.6 %copy-start.2 = (f32[32,32,128]{2,1,0:T(8,128)S(1)}, f32[32,32,128]{2,1,0:T(8,128)}, u32[]{:S(2)}) copy-start(f32[32,32,128]{2,1,0:T(8,128)} %p.3) | copy-start | bytes 1572868
  0.0 12.7 %copy-start.8 = (s32[32,32,1]{1,2,0:T(1,128)S(1)}, s32[32,32,1]{1,2,0:T(1,128)}, u32[]{:S(2)}) copy-start(s32[32,32,1]{1,2,0:T(1,128)} %param.14) | copy-start | bytes 12292
  0.0 13.4 %copy-start.9 = (s32[32,32,1]{1,2,0:T(1,128)S(1)}, s32[32,32,1]{1,2,0:T(1,128)}, u32[]{:S(2)}) copy-start(s32[32,32,1]{1,2,0:T(1,128)} %param.15) | copy-start | bytes 12292
  4.8 19.8 %collective-permute-start = (f32[42,32,128]{2,1,0:T(8,128)}, f32[42,32,128]{2,1,0:T(8,128)S(1)}, u32[]{:S(2)}, u32[]{:S(2)}) collective-permute-start(f32[42,32,128]{2,1,0:T(8,128)} %get-tuple-element.20), channel_id=1, source_target_pairs={{0,32},{32,64},{64,96},{96,0},{1,33},{33,65},{65,97},{97,1},{2,34}... | collective-permute-start | bytes 2064392 | tf_op jit(solution)/shard_map/ppermute | solution.py:537
  6.8 17.8 %collective-permute-start.1 = (f32[42,32,128]{2,1,0:T(8,128)}, f32[42,32,128]{2,1,0:T(8,128)S(1)}, u32[]{:S(2)}, u32[]{:S(2)}) collective-permute-start(f32[42,32,128]{2,1,0:T(8,128)} %get-tuple-element.21), channel_id=1, source_target_pairs={{0,96},{32,0},{64,32},{96,64},{1,97},{33,1},{65,33},{97,65},{2,98}... | collective-permute-start | bytes 2064392 | tf_op jit(solution)/shard_map/ppermute | solution.py:537
  8.9 21.6 %collective-permute-start.2 = (f32[34,40,128]{2,1,0:T(8,128)}, f32[34,40,128]{2,1,0:T(8,128)S(1)}, u32[]{:S(2)}, u32[]{:S(2)}) collective-permute-start(f32[34,40,128]{2,1,0:T(8,128)} %get-tuple-element.22), channel_id=1, source_target_pairs={{0,8},{8,16},{16,24},{24,0},{1,9},{9,17},{17,25},{25,1},{2,10},{10... | collective-permute-start | bytes 2088968 | tf_op jit(solution)/shard_map/ppermute | solution.py:537
  10.4 20.1 %collective-permute-start.3 = (f32[34,40,128]{2,1,0:T(8,128)}, f32[34,40,128]{2,1,0:T(8,128)S(1)}, u32[]{:S(2)}, u32[]{:S(2)}) collective-permute-start(f32[34,40,128]{2,1,0:T(8,128)} %get-tuple-element.23), channel_id=1, source_target_pairs={{0,24},{8,0},{16,8},{24,16},{1,25},{9,1},{17,9},{25,17},{2,26},{10... | collective-permute-start | bytes 2088968 | tf_op jit(solution)/shard_map/ppermute | solution.py:537
  15.8 10.2 %copy-start.6 = (s32[8,128]{1,0:T(8,128)}, s32[8,128]{1,0:T(8,128)S(1)}, u32[]{:S(2)}) copy-start(s32[8,128]{1,0:T(8,128)S(1)} %get-tuple-element.18) | copy-start | bytes 12292
  26.0 7.5 %collective-permute-start.4 = (f32[4,96,128]{2,1,0:T(8,128)}, f32[4,96,128]{2,1,0:T(8,128)S(1)}, u32[]{:S(2)}, u32[]{:S(2)}) collective-permute-start(f32[4,96,128]{2,1,0:T(8,128)} %get-tuple-element.25), channel_id=1, source_target_pairs={{0,8},{8,16},{16,24},{24,0},{1,9},{9,17},{17,25},{25,1},{2,10},{10... | collective-permute-start | bytes 589832 | tf_op jit(solution)/shard_map/ppermute | solution.py:537
  27.5 6.1 %collective-permute-start.5 = (f32[4,96,128]{2,1,0:T(8,128)}, f32[4,96,128]{2,1,0:T(8,128)}, u32[]{:S(2)}, u32[]{:S(2)}) collective-permute-start(f32[4,96,128]{2,1,0:T(8,128)} %get-tuple-element.26), channel_id=1, source_target_pairs={{0,24},{8,0},{16,8},{24,16},{1,25},{9,1},{17,9},{25,17},{2,26},{10... | collective-permute-start | bytes 589832 | tf_op jit(solution)/shard_map/ppermute | solution.py:537
  33.6 1.7 %copy-start.1 = (f32[5,32,32,128]{3,2,1,0:T(8,128)S(1)}, f32[5,32,32,128]{3,2,1,0:T(8,128)}, u32[]{:S(2)}) copy-start(f32[5,32,32,128]{3,2,1,0:T(8,128)} %get-tuple-element.19.own) | copy-start | bytes 7864324
  35.3 16.7 %copy-start = (f32[2,32,32,128]{3,2,1,0:T(8,128)S(1)}, f32[2,32,32,128]{3,2,1,0:T(8,128)}, u32[]{:S(2)}) copy-start(f32[2,32,32,128]{3,2,1,0:T(8,128)} %sat.3) | copy-start | bytes 3145732
  35.3 16.7 %copy-start.3 = (f32[32,32,128]{2,1,0:T(8,128)S(1)}, f32[32,32,128]{2,1,0:T(8,128)}, u32[]{:S(2)}) copy-start(f32[32,32,128]{2,1,0:T(8,128)} %sto.3) | copy-start | bytes 1572868
  35.3 16.7 %copy-start.4 = (s32[32,32,128]{2,1,0:T(8,128)S(1)}, s32[32,32,128]{2,1,0:T(8,128)}, u32[]{:S(2)}) copy-start(s32[32,32,128]{2,1,0:T(8,128)} %mask.3) | copy-start | bytes 1572868
  35.3 16.7 %copy-start.5 = (f32[2,32,32,128]{3,2,1,0:T(8,128)S(1)}, f32[2,32,32,128]{3,2,1,0:T(8,128)}, u32[]{:S(2)}) copy-start(f32[2,32,32,128]{3,2,1,0:T(8,128)} %old.1) | copy-start | bytes 3145732
  35.3 16.7 %copy-start.7 = (s32[8,128]{1,0:T(8,128)S(1)}, s32[8,128]{1,0:T(8,128)}, u32[]{:S(2)}) copy-start(s32[8,128]{1,0:T(8,128)} %copy-done.6) | copy-start | bytes 12292
  41.1 11.0 %collective-permute-start.6 = (f32[22,56,128]{2,1,0:T(8,128)S(1)}, f32[22,56,128]{2,1,0:T(8,128)S(1)}, u32[]{:S(2)}, u32[]{:S(2)}) collective-permute-start(f32[22,56,128]{2,1,0:T(8,128)S(1)} %get-tuple-element.29.z_last), channel_id=1, source_target_pairs={{0,1},{1,2},{2,3},{3,4},{4,5},{5,6},{6,7},{7,0},{8,9},{9,10},{10,1... | collective-permute-start | bytes 1892360 | tf_op jit(solution)/shard_map/ppermute | solution.py:537
  41.1 10.9 %collective-permute-start.7 = (f32[22,56,128]{2,1,0:T(8,128)S(1)}, f32[22,56,128]{2,1,0:T(8,128)S(1)}, u32[]{:S(2)}, u32[]{:S(2)}) collective-permute-start(f32[22,56,128]{2,1,0:T(8,128)S(1)} %get-tuple-element.30.z_first), channel_id=1, source_target_pairs={{0,7},{1,0},{2,1},{3,2},{4,3},{5,4},{6,5},{7,6},{8,15},{9,8},{10,9... | collective-permute-start | bytes 1892360 | tf_op jit(solution)/shard_map/ppermute | solution.py:537

commit v4 on v3

--- a/solution.py
+++ b/solution.py
@@ -17,7 +17,7 @@
 SLOTS = 640
 ZG = 10
 NQ = 5
-SOLVE_MIB = 34
+SOLVE_MIB = 20
 PAD = 8
 ZS = 12
 
@@ -38,7 +38,21 @@
     return H - dist if side == 0 else dist - 1
 
 
-def prep_kernel(p, sat, perm, sto, mask, own, xm, xp, ym, yp):
+def prep_kernel(
+    p_far, sat_far, perm_far, sto_far, mask_far, own, xm, xp, ym, yp, p, sat, perm, sto, mask, sems
+):
+    pieces = 4
+    many = T // pieces
+
+    def copies(n):
+        at = pl.ds(n * many, many)
+        pairs = [(p_far.at[at], p.at[at]), (perm_far.at[at], perm.at[at])]
+        pairs += [(sto_far.at[at], sto.at[at]), (mask_far.at[at], mask.at[at])]
+        pairs += [(sat_far.at[:, at], sat.at[:, at])]
+        return [
+            pltpu.make_async_copy(far, near, sems.at[n, k]) for k, (far, near) in enumerate(pairs)
+        ]
+
     def rows(q, carry):
         for u in range(4):
             i = q * 4 + u
@@ -60,7 +74,13 @@
                 yp[32 + f, pl.ds(i, 1)] = v[T - 1 :]
         return carry
 
-    lax.fori_loop(0, 8, rows, 0)
+    for n in range(pieces):
+        for copy in copies(n):
+            copy.start()
+    for n in range(pieces):
+        for copy in copies(n):
+            copy.wait()
+        lax.fori_loop(n * many // 4, (n + 1) * many // 4, rows, 0)
     for f in range(4):
         for t in range(H):
             xm[f * H + t] = p[t] if f == 0 else own[f - 1, t]
@@ -185,14 +205,55 @@
     return there, back, there * step, back * step
 
 
+def combine(diag, x, x_carry, y, z, z_back, z_bflow):
+    y_back, y_bflow = down(y[1]), down(y[3])
+    whole = diag + (x[0] + x_carry[0]) + (y[0] + y_back) + (z[0] + z_back)
+    flow = (x[2] - x_carry[1]) + (y[2] - y_bflow) + (z[2] - z_bflow)
+    inv = 1.0 / whole
+    weights = [w * inv for w in (x[0], x_carry[0], y[0], y_back, z[0], z_back)]
+    return whole, flow * inv, weights
+
+
+def assemble_kernel(ext, mat, base, total):
+    rows_all, rows_up = slice(0, EJ), slice(1, EJ + 1)
+
+    def group(g, carry):
+        for q in range(NQ):
+            i = 1 + NQ * g + q
+            here = [ext[f, i, rows_all] for f in range(3)]
+            ahead = [ext[f, i + 1, rows_all] for f in range(3)]
+            if q == NQ - 1:
+                ahead = [turn(v, -ZS) for v in ahead]
+            x = face(*here, *ahead)
+            y = face(*here, *(ext[f, i, rows_up] for f in range(3)))
+            z = face(*here, *(turn(v, -1) for v in here))
+            whole, start, weights = combine(
+                ext[3, i, rows_all], x, carry, y, z, turn(z[1], 1), turn(z[3], 1)
+            )
+            for k, w in enumerate(weights):
+                mat[k, i] = w
+            total[i] = whole
+            base[i, PAD : PAD + EJ] = start
+            carry = x[1], x[3]
+        return tuple(turn(v, ZS) for v in carry)
+
+    x = face(*(ext[f, 0, rows_all] for f in range(3)), *(ext[f, 1, rows_all] for f in range(3)))
+    lax.fori_loop(0, ZG, group, (x[1], x[3]))
+
+
 def solve_kernel(
-    edge, dst, ext, aext, z_lo, z_hi, z_first, z_last, sat, old, sto, mask, places, send,
-    side, rim, back, mat, zmat, base, one, two, zbase, zone, ztwo, border, total, share, rows, stage, sem,
+    edge, dst, ext, aext, z_lo, z_hi, z_first, z_last, sat, old, sto, mask, places,
+    mat_in, base_in, total_in, send, mat, base, total,
+    side, rim, zmat, ztotal, one, two, zbase, zone, ztwo, border, share, stage,
 ):
+    del mat_in, base_in, total_in
     lane = lanes_of(EJ)
     part = lax.rem(lane, ZS)
-    first_lane = part == 0
-    last_lane = (part == ZS - 1) & (lane < ZS * (ZG - 1)) | (lane == L - 1)
+    first_lane = (part < 2) & (lane < ZS * ZG)
+    last_lane = part >= ZS - 2
+    for late in (L - 2, L - 1):
+        last_lane = last_lane | (lane == late)
+    start_lane = part == 0
     body_rows = slice(PAD, PAD + EJ)
 
     def wrap(ref, t):
@@ -204,28 +265,16 @@
             right, left = z_hi[f * NQ + q], z_lo[f * NQ + q]
             if f == 1:
                 right, left = right * edge[5], left * edge[4]
-            if f < 3:
-                right = jnp.where(last_lane, z_last[f * NQ + q], right)
-                left = jnp.where(first_lane, z_first[f * NQ + q], left)
-                rim[f, q] = jnp.where(first_lane, z_hi[f * NQ + q], z_lo[f * NQ + q])
-                if f == 1:
-                    rim[f, q] = jnp.where(first_lane, right, left)
-            side[f, 0, 1 + q] = right
-            side[f, 1, 1 + q] = left
+            if f == 0:
+                rim[q] = jnp.where(start_lane, right, left)
+            side[f, 0, 1 + q] = jnp.where(last_lane, z_last[f * NQ + q], right)
+            side[f, 1, 1 + q] = jnp.where(first_lane, z_first[f * NQ + q], left)
         return carry
 
     lax.fori_loop(0, NQ, join, 0)
     for f in range(3):
         for t in (0, 1):
             wrap(side.at[f], t)
-
-    def combine(diag, x, x_carry, y, z, z_back, z_bflow):
-        y_back, y_bflow = down(y[1]), down(y[3])
-        whole = diag + (x[0] + x_carry[0]) + (y[0] + y_back) + (z[0] + z_back)
-        flow = (x[2] - x_carry[1]) + (y[2] - y_bflow) + (z[2] - z_bflow)
-        inv = 1.0 / whole
-        weights = [w * inv for w in (x[0], x_carry[0], y[0], y_back, z[0], z_back)]
-        return whole, flow * inv, weights
 
     for t in (0, 1):
 
@@ -234,14 +283,12 @@
             x = face(*here, *(side[f, t, q + 1] for f in range(3)))
             y = face(*here, *(up(v) for v in here))
             z = face(*here, *(turn(v, -1) for v in here))
-            if t == 1:
-                back[0, q - 1] = z[1]
-                back[1, q - 1] = z[3]
-            _, start, weights = combine(
+            whole, start, weights = combine(
                 side[3, t, q], x, carry, y, z, turn(z[1], 1), turn(z[3], 1)
             )
             for k, w in enumerate(weights):
                 zmat[k, t, q - 1] = w
+            ztotal[t, q - 1] = whole
             zbase[t, q, body_rows] = start
             return x[1], x[3]
 
@@ -255,36 +302,21 @@
         pltpu.store(ref.at[0, 1 + q, rows_at], value, mask=marks[1])
         pltpu.store(ref.at[1, 1 + q, rows_at], value, mask=marks[0])
 
-    all_rows = slice(0, EJ)
-
-    def assemble(g, carry):
-        marks = spots(g, lane)
-        for q in range(NQ):
+    def mend(q, carry):
+        ends = [jnp.where(start_lane, zmat[k, 1, q], zmat[k, 0, q]) for k in range(6)]
+        ends.append(jnp.where(start_lane, ztotal[1, q], ztotal[0, q]))
+        start = jnp.where(start_lane, zbase[1, 1 + q, body_rows], zbase[0, 1 + q, body_rows])
+        for g in range(ZG):
             i = 1 + NQ * g + q
-            here = [ext[f, i, all_rows] for f in range(3)]
-            ahead = [ext[f, i + 1, all_rows] for f in range(3)]
-            if q == NQ - 1:
-                ahead = [turn(v, -ZS) for v in ahead]
-            x = face(*here, *ahead)
-            y = face(*here, *(ext[f, i, 1 : EJ + 1] for f in range(3)))
-            z = face(
-                *here,
-                *(turn(jnp.where(marks[0], rim[f, q], v), -1) for f, v in enumerate(here)),
-            )
-            z_back, z_bflow = (
-                turn(jnp.where(marks[1], back[k, q], z[n]), 1) for k, n in ((0, 1), (1, 3))
-            )
-            whole, start, weights = combine(ext[3, i, all_rows], x, carry, y, z, z_back, z_bflow)
-            for k, w in enumerate(weights):
-                mat[k, i] = w
-            total[i] = whole
-            base[i, body_rows] = start
-            ghosts(zbase, q, start, body_rows, marks)
-            carry = x[1], x[3]
-        return tuple(turn(v, ZS) for v in carry)
-
-    x = face(*(ext[f, 0, all_rows] for f in range(3)), *(ext[f, 1, all_rows] for f in range(3)))
-    lax.fori_loop(0, ZG, assemble, (x[1], x[3]))
+            here = (lane == ZS * g) | (lane == (ZS * g + L - 1) % L)
+            for k in range(6):
+                pltpu.store(mat.at[k, i], ends[k], mask=here)
+            if 1 <= g < ZG - 1:
+                pltpu.store(total.at[i], ends[6], mask=here)
+            pltpu.store(base.at[i, body_rows], start, mask=here)
+        return carry
+
+    lax.fori_loop(0, NQ, mend, 0)
 
     def prepare(zsrc):
         for t in (0, 1):
@@ -292,11 +324,11 @@
 
         def plane(q, carry):
             border[q] = jnp.where(
-                first_lane, zsrc[0, 1 + q, body_rows], zsrc[1, 1 + q, body_rows]
+                start_lane, zsrc[0, 1 + q, body_rows], zsrc[1, 1 + q, body_rows]
             )
             return carry
 
-        lax.fori_loop(0, NQ, plane, 0)
+        lax.fori_loop(0, NQ, plane, 0, unroll=NQ)
 
     def sweep(src, zsrc, target, ztarget, depth):
         low, high = (4, 52) if depth > 4 else (8, 48)
@@ -317,7 +349,7 @@
                 ztarget[t, q, y_at] = acc + zmat[5, t, q - 1, at] * turn(y, 1)
             return carry
 
-        lax.fori_loop(1, NQ + 1, halo, 0)
+        lax.fori_loop(1, NQ + 1, halo, 0, unroll=NQ)
 
         def planes(g, carry):
             marks = spots(g, lanes)
@@ -339,7 +371,8 @@
                 ghosts(ztarget, q, acc, y_at, marks)
             return carry
 
-        lax.fori_loop(*((0, ZG) if depth > 4 else (1, ZG - 1)), planes, 0)
+        groups = (0, ZG) if depth > 4 else (1, ZG - 1)
+        lax.fori_loop(*groups, planes, 0, unroll=(groups[1] - groups[0]) // 2)
 
     src, zsrc = base, zbase
     for k in range(1, SWEEPS):
@@ -348,77 +381,110 @@
         src, zsrc = target, ztarget
     prepare(zsrc)
 
-    mid, mid_up, mid_down = (slice(k, k + T) for k in (OJ, OJ + 1, OJ - 1))
-    y_mid, y_up, y_down = (slice(PAD + k, PAD + k + T) for k in (OJ, OJ + 1, OJ - 1))
-    lanes = lanes_of(T)
-    even = lax.rem(lanes, 2) == 0
+    half = T // 2
+    lanes = lanes_of(half)
+    tile = slice(OJ, OJ + T)
+    even = lax.rem(lanes_of(T), 2) == 0
     for f in range(2):
-        share[f] = jnp.where(even, z_hi[4 * NQ + f, mid], z_lo[4 * NQ + f, mid])
-
-    def near_of(ref, lead, i, at, at_up, at_down, edge_plane, q, marks):
-        here, ahead, behind = (ref[lead + (i + k, at)] for k in (0, 1, -1))
+        share[f] = jnp.where(even, z_hi[4 * NQ + f, tile], z_lo[4 * NQ + f, tile])
+
+    def moved(ref, lead, i, first, edge_plane, q, marks):
+        at = slice(first, first + half)
+        here = ref[lead + (i, at)]
+        out = {
+            4: turn(jnp.where(marks[0], edge_plane, here), -1),
+            5: turn(jnp.where(marks[1], edge_plane, here), 1),
+        }
         if q == 0:
-            behind = turn(behind, ZS)
+            out[1] = turn(ref[lead + (i - 1, at)], ZS)
         if q == NQ - 1:
-            ahead = turn(ahead, -ZS)
-        return here, (
-            ahead,
-            behind,
-            ref[lead + (i, at_up)],
-            ref[lead + (i, at_down)],
-            turn(jnp.where(marks[0], edge_plane, here), -1),
-            turn(jnp.where(marks[1], edge_plane, here), 1),
-        )
-
-    def finish(g, q, marks):
+            out[0] = turn(ref[lead + (i + 1, at)], -ZS)
+        return out
+
+    def near_of(ref, lead, i, first, ready):
+        spots_of = ((1, 0), (-1, 0), (0, 1), (0, -1))
+        return [
+            ready[k] if k in ready else ref[lead + (i + d, slice(first + r, first + r + half))]
+            for k, (d, r) in enumerate(spots_of)
+        ] + [ready[4], ready[5]]
+
+    def prefetch(g, q, marks, part):
         e = 1 + NQ * g + q
         i = e - H
-        pa, p_near = near_of(ext, (0,), e, mid, mid_up, mid_down, rim[0, q, mid], q, marks)
-        _, s_near = near_of(src, (), e, y_mid, y_up, y_down, border[q, mid], q, marks)
+        first = OJ + half * part
+        at, own = slice(first, first + half), slice(half * part, half * part + half)
+        edges = [turn(share[f, own], ZS * g - 2 * i) for f in range(2)]
+        return [
+            moved(ext, (0,), e, first, rim[q, at], q, marks),
+            moved(src, (), e, PAD + first, border[q, at], q, marks),
+        ] + [moved(aext, (f,), i + 1, first, edges[f], q, marks) for f in range(2)]
+
+    def finish(g, q, part, ready):
+        e = 1 + NQ * g + q
+        i = e - H
+        first = OJ + half * part
+        at, y_at = slice(first, first + half), slice(PAD + first, PAD + first + half)
+        own = slice(half * part, half * part + half)
+        pa = ext[0, e, at]
+        p_near = near_of(ext, (0,), e, first, ready[0])
+        s_near = near_of(src, (), e, PAD + first, ready[1])
         shares = [
-            near_of(
-                aext, (f,), i + 1, mid, mid_up, mid_down,
-                turn(share[f], ZS * g - 2 * i), q, marks,
-            )
+            (aext[f, i + 1, at], near_of(aext, (f,), i + 1, first, ready[2 + f]))
             for f in range(2)
         ]
-        x_p = base[e, y_mid]
+        x_p = base[e, y_at]
+        column = [None, None]
+        drive = [None, None]
         for k in range(6):
-            x_p = x_p + mat[k, e, mid] * s_near[k]
-        column = [jnp.zeros((T, L), F32) for _ in range(2)]
-        drive = [jnp.zeros((T, L), F32) for _ in range(2)]
-        for k in range(6):
-            weight = mat[k, e, mid]
+            weight = mat[k, e, at]
+            x_p = x_p + weight * s_near[k]
             upstream = pa >= p_near[k]
             step = s_near[k] - (pa - p_near[k])
             for f, (a, a_near) in enumerate(shares):
                 w = weight * jnp.where(upstream, a, a_near[k])
-                column[f] = column[f] + w
-                drive[f] = drive[f] + w * step
-        scale = total[e, mid]
+                column[f] = w if k == 0 else column[f] + w
+                drive[f] = w * step if k == 0 else drive[f] + w * step
+        scale = total[e, at]
         shift = -ZS * g
         coupled = [turn((drive[f] - column[f] * x_p) * scale, shift) for f in range(2)]
-        x_p = turn(x_p, shift)
-        act = mask[i].astype(F32)
-        held = act * sto[i]
+        return turn(x_p, shift), coupled
+
+    def settle(g, q, part, result):
+        i = 1 + NQ * g + q - H
+        own = slice(half * part, half * part + half)
+        x_p, coupled = result
+        act = mask[i, own].astype(F32)
+        held = act * sto[i, own]
         idle = 1.0 - act
         inverse = 1.0 / (held + idle)
-        stage[0, i] = x_p
+        stage[0, i, own] = x_p
         for f, compress in ((0, 0.5), (1, 2.0)):
-            s_now = sat[f, i]
+            s_now = sat[f, i, own]
             local = (held * (compress * s_now) + idle) * x_p
-            change = held * (s_now - old[f, i])
-            stage[1 + f, i] = (coupled[f] - change - local) * inverse
+            change = held * (s_now - old[f, i, own])
+            stage[1 + f, i, own] = (coupled[f] - change - local) * inverse
+
+    def chain(items):
+        ready, result = prefetch(*items[0]), None
+        for n, (g, q, marks, part) in enumerate(items):
+            later = prefetch(*items[n + 1]) if n + 1 < len(items) else None
+            now = finish(g, q, part, ready)
+            if n:
+                settle(items[n - 1][0], items[n - 1][1], items[n - 1][3], result)
+            ready, result = later, now
+        settle(items[-1][0], items[-1][1], items[-1][3], result)
 
     def group(g, carry):
         marks = spots(g, lanes)
-        for q in range(NQ):
-            finish(g, q, marks)
+        chain([(g, q, marks, part) for q in range(NQ) for part in (0, 1)])
         return carry
 
     lax.fori_loop(2, 8, group, 0)
-    finish(jnp.int32(1), NQ - 1, spots(1, lanes))
-    finish(jnp.int32(8), 0, spots(8, lanes))
+    chain([
+        (jnp.int32(g), q, spots(g, lanes), part)
+        for g, q in ((1, NQ - 1), (8, 0))
+        for part in (0, 1)
+    ])
 
     devices = places.shape[0]
     capacity = T * T // devices
@@ -428,19 +494,16 @@
         for j in range(T):
             d = dst[i * T + j]
             for f in range(3):
-                rows[pl.ds(d + f * capacity, 1)] = stage[f, i, j : j + 1]
-        return carry
-
-    lax.fori_loop(0, T, place, 0)
+                send[pl.ds(d + f * capacity, 1)] = stage[f, i, j : j + 1]
+        return carry
+
+    lax.fori_loop(0, T, place, 0, unroll=4)
 
     def tail(d, carry):
-        rows[pl.ds(d * chunk + 3 * capacity, 1)] = places[pl.ds(d, 1)]
+        send[pl.ds(d * chunk + 3 * capacity, 1)] = places[pl.ds(d, 1)]
         return carry
 
     lax.fori_loop(0, devices, tail, 0, unroll=8)
-    copy = pltpu.make_async_copy(rows.at[: devices * chunk], send, sem)
-    copy.start()
-    copy.wait()
 
 
 def index_kernel(owner, slot, dst, places):
@@ -460,7 +523,7 @@
         ahead = jnp.dot(hit.astype(bf16), earlier, preferred_element_type=F32) + count
         count = count + jnp.sum(hit, axis=1, keepdims=True)
         rank = jnp.sum(hit * ahead, axis=0, keepdims=True).astype(jnp.int32)
-        dst[c : c + 1] = jnp.where(own >= 0, own * chunk + rank, devices * chunk)
+        dst[c : c + 1] = jnp.where(own >= 0, own * chunk + rank, -1)
         place = slot[c : c + 1]
         high = lax.div(place, 32)
         here = spot == rank
@@ -473,6 +536,9 @@
                 coarse = coarse + found
             else:
                 fine = fine + found
+    free = jnp.where(count < capacity, lax.broadcasted_iota(jnp.int32, (devices, 1), 0).astype(F32), 0.0)
+    spare = jnp.max(free, axis=0, keepdims=True).astype(jnp.int32) * chunk + capacity - 1
+    dst[...] = jnp.where(dst[...] < 0, spare, dst[...])
     lane = lax.broadcasted_iota(jnp.int32, (devices, L), 1).astype(F32)
     places[...] = jnp.where(lane < count, 32.0 * coarse + fine, -1.0)
 
@@ -500,7 +566,7 @@
                 held[f, pl.ds(s, 1)] = got[pl.ds(d * chunk + f * capacity + k, 1)]
         return carry
 
-    lax.fori_loop(0, devices, scatter, 0)
+    lax.fori_loop(0, devices, scatter, 0, unroll=8)
     copy = pltpu.make_async_copy(held.at[:, :SLOTS], update, sem)
     copy.start()
     copy.wait()
@@ -514,16 +580,17 @@
     return jax.ShapeDtypeStruct(dims, F32)
 
 
-def call(kernel, name, out_shape, smem, count, out_spaces=None, scratch=(), limit=16):
+def call(kernel, name, out_shape, smem, count, out_spaces=None, scratch=(), limit=16, alias=None, space=pltpu.VMEM):
     many = isinstance(out_shape, (tuple, list))
     spaces = out_spaces or ([pltpu.VMEM] * len(out_shape) if many else pltpu.VMEM)
     return pl.pallas_call(
         kernel,
         name=name,
         out_shape=out_shape,
-        in_specs=[spec(pltpu.SMEM)] * smem + [spec(pltpu.VMEM)] * count,
+        in_specs=[spec(pltpu.SMEM)] * smem + [spec(space)] * count,
         out_specs=[spec(s) for s in spaces] if many else spec(spaces),
         scratch_shapes=list(scratch),
+        input_output_aliases=alias or {},
         compiler_params=pltpu.CompilerParams(vmem_limit_bytes=limit << 20),
     )
 
@@ -561,7 +628,12 @@
         ),
         0,
         5,
-        limit=60,
+        None,
+        [pltpu.VMEM((T, T, L), F32), pltpu.VMEM((2, T, T, L), F32)]
+        + [pltpu.VMEM((T, T, L), F32)] * 2
+        + [pltpu.VMEM((T, T, L), jnp.int32), pltpu.SemaphoreType.DMA((4, 5))],
+        60,
+        space=pltpu.HBM,
     )(pressure, saturation, permeability, storage, cell_mask)
     x_lo, x_hi = swap(xm, xp, "gx")
     y_lo, y_hi = swap(ym, yp, "gy")
@@ -585,34 +657,34 @@
         limit=24,
     )(edge, pressure, own, x_lo, x_hi, y_lo, y_hi, c_lo, c_hi)
     z_lo, z_hi = swap(zm, zp, "gz")
-    send = call(
+    grid, tall = (EI, EJ, L), (EI, EJ + 2 * PAD, L)
+    rows_of = (shape(6, *grid), shape(*tall), shape(*grid))
+    mat, base, total = call(assemble_kernel, "assemble", rows_of, 0, 1)(ext)
+    send, *_ = call(
         solve_kernel,
         "solve",
-        shape(devices * chunk, L),
+        (shape(devices * chunk, L),) + rows_of,
         2,
-        11,
-        pl.ANY,
+        14,
+        None,
         [
             pltpu.VMEM((4, 2, NQ + 2, EJ, L), F32),
-            pltpu.VMEM((3, NQ, EJ, L), F32),
+            pltpu.VMEM((NQ, EJ, L), F32),
+            pltpu.VMEM((6, 2, NQ, EJ, L), F32),
             pltpu.VMEM((2, NQ, EJ, L), F32),
-            pltpu.VMEM((6, EI, EJ, L), F32),
-            pltpu.VMEM((6, 2, NQ, EJ, L), F32),
         ]
-        + [pltpu.VMEM((EI, EJ + 2 * PAD, L), F32)] * 3
+        + [pltpu.VMEM(tall, F32)] * 2
         + [pltpu.VMEM((2, NQ + 2, EJ + 2 * PAD, L), F32)] * 3
         + [
             pltpu.VMEM((NQ, EJ, L), F32),
-            pltpu.VMEM((EI, EJ, L), F32),
             pltpu.VMEM((2, T, L), F32),
-            pltpu.VMEM((devices * chunk + 2 * capacity + 8, L), F32),
             pltpu.VMEM((3, T, T, L), F32),
-            pltpu.SemaphoreType.DMA(()),
         ],
         SOLVE_MIB,
+        {13: 1, 14: 2, 15: 3},
     )(
         edge, dst, ext, aext, z_lo, z_hi, zm, zp,
-        saturation, old_saturation, storage, cell_mask, places,
+        saturation, old_saturation, storage, cell_mask, places, mat, base, total,
     )
     got = lax.all_to_all(
         send.reshape(devices, chunk, 1, L), AXES, split_axis=0, concat_axis=0, tiled=True

time: 124 us -> 111 us (0.90)
  Pallas kernels: 50.5 us -> 42.9 us
  waiting for transfers between devices: 19.8 us -> 14.1 us
    pallas_call x1 -> x2, Pallas kernels: 32.5 us -> 25.6 us  [the longest x1 19.8 us: body(): call(solve_kernel, 'solve', (shape(devices * chunk, L),) + rows_of, 2, 14...]
    ppermute x4, waiting for transfers between devices: 19.7 us -> 14 us  [swap(): lax.ppermute(high, axis, ring(axis, 1))]
  transfers between devices with their start and end apart: 8 -> 8, of which waited for: 4 -> 4; matrix products, arithmetic and copies ran while one was open for 3% -> 3% of each run, Pallas kernels for 2% -> 8%
where the time goes in v4:
time: 111 us
  Pallas kernels  42.9 us (39%)
  blocking collectives  34.9 us (31%)
  waiting for transfers between devices  14.1 us (13%)
  starting transfers between devices  13.7 us (12%)
  local copies, waits for them, and re-layouts  3.07 us (3%)
  other arithmetic  1.84 us (2%)
    all_to_all x1, blocking collectives, body(): lax.all_to_all(send.reshape(devices, chunk, 1, L), AXES, split_axis=0, co...  34.9 us
    pallas_call x1, Pallas kernels, body(): call(solve_kernel, 'solve', (shape(devices * chunk, L),) + rows_of, 2, 14...  19.8 us
    ppermute x4, waiting for transfers between devices, swap(): lax.ppermute(high, axis, ring(axis, 1))  14 us
    ppermute x4, starting transfers between devices, swap(): lax.ppermute(low, axis, ring(axis, -1))  8.63 us
    pallas_call x1, Pallas kernels, body(): mat, base, total = call(assemble_kernel, 'assemble', rows_of, 0, 1)(ext)  5.73 us
    pallas_call x1, Pallas kernels, body(): call(build_kernel, 'build', (shape(4, EI, EJ + 8, L), shape(2, T + 2, EJ,...  5.54 us
    ppermute x4, starting transfers between devices, swap(): lax.ppermute(high, axis, ring(axis, 1))  5.1 us
    pallas_call x1, Pallas kernels, body(): call(prep_kernel, 'prep', (shape(5, T, T, L), shape(4 * H + 2, T, L), sha...  4.66 us
  transfers between devices with their start and end apart: 8, of which 4 were waited for; matrix products, arithmetic and copies ran while one was open for 3% of the time, Pallas kernels for 8%

profile of v4, /device:TPU:0, one launch (start us, length us, event | category | flops | bytes accessed | tf_op | source)
XLA Modules:
  0.0 110.7 jit_solution(4217280362690138310)
XLA Ops:
  0.0 4.7 %prep.1 = (f32[5,32,32,128]{3,2,1,0:T(8,128)}, f32[42,32,128]{2,1,0:T(8,128)}, f32[42,32,128]{2,1,0:T(8,128)}, f32[34,40,128]{2,1,0:T(8,128)}, f32[34,40,128]{2,1,0:T(8,128)}) custom-call(f32[32,32,128]{2,1,0:T(8,128)} %p.1, f32[2,32,32,128]{3,2,1,0:T(8,128)} %sat.1, f32[32,32,128]{2,1,0:T(8,128)} %perm_far.1, f32[32,32,128]{2,1,0:T(8,128)} %sto.1, ...), custom_call_target="tpu_custom_call" | custom-call | tf_op jit(solution)/shard_map/prep/pallas_call | solution.py:619
  4.7 2.1 %collective-permute-start = (f32[42,32,128]{2,1,0:T(8,128)}, f32[42,32,128]{2,1,0:T(8,128)S(1)}, u32[]{:S(2)}, u32[]{:S(2)}) collective-permute-start(f32[42,32,128]{2,1,0:T(8,128)} %get-tuple-element.24), channel_id=1, source_target_pairs={{0,32},{32,64},{64,96},{96,0},{1,33},{33,65},{65,97},{97,1},{2,34}... | collective-permute-start | bytes 2064392 | tf_op jit(solution)/shard_map/ppermute | solution.py:604
  6.8 2.2 %collective-permute-start.1 = (f32[42,32,128]{2,1,0:T(8,128)}, f32[42,32,128]{2,1,0:T(8,128)S(1)}, u32[]{:S(2)}, u32[]{:S(2)}) collective-permute-start(f32[42,32,128]{2,1,0:T(8,128)} %get-tuple-element.25), channel_id=1, source_target_pairs={{0,96},{32,0},{64,32},{96,64},{1,97},{33,1},{65,33},{97,65},{2,98}... | collective-permute-start | bytes 2064392 | tf_op jit(solution)/shard_map/ppermute | solution.py:604
  9.0 1.5 %collective-permute-start.2 = (f32[34,40,128]{2,1,0:T(8,128)}, f32[34,40,128]{2,1,0:T(8,128)S(1)}, u32[]{:S(2)}, u32[]{:S(2)}) collective-permute-start(f32[34,40,128]{2,1,0:T(8,128)} %get-tuple-element.26), channel_id=1, source_target_pairs={{0,8},{8,16},{16,24},{24,0},{1,9},{9,17},{17,25},{25,1},{2,10},{10... | collective-permute-start | bytes 2088968 | tf_op jit(solution)/shard_map/ppermute | solution.py:604
  10.5 1.7 %collective-permute-start.3 = (f32[34,40,128]{2,1,0:T(8,128)}, f32[34,40,128]{2,1,0:T(8,128)S(1)}, u32[]{:S(2)}, u32[]{:S(2)}) collective-permute-start(f32[34,40,128]{2,1,0:T(8,128)} %get-tuple-element.27), channel_id=1, source_target_pairs={{0,24},{8,0},{16,8},{24,16},{1,25},{9,1},{17,9},{25,17},{2,26},{10... | collective-permute-start | bytes 2088968 | tf_op jit(solution)/shard_map/ppermute | solution.py:604
  12.2 0.5 broadcast.6
  12.7 0.6 reduce.6
  13.3 0.1 reshape.15.owner
  13.4 0.6 reduce.7
  14.0 0.1 reshape.16.slot
  14.1 1.6 %index.1 = (s32[8,128]{1,0:T(8,128)S(1)}, f32[128,128]{1,0:T(8,128)S(1)}) custom-call(s32[8,128]{1,0:T(8,128)S(1)} %reshape.15.owner, s32[8,128]{1,0:T(8,128)S(1)} %reshape.16.slot), custom_call_target="tpu_custom_call" | custom-call | tf_op jit(solution)/shard_map/index/pallas_call | solution.py:642
  15.7 8.8 %collective-permute-done.x_lo = f32[42,32,128]{2,1,0:T(8,128)S(1)} collective-permute-done((f32[42,32,128]{2,1,0:T(8,128)}, f32[42,32,128]{2,1,0:T(8,128)S(1)}, u32[]{:S(2)}, u32[]{:S(2)}) %collective-permute-start) | collective-permute-done | bytes 688160 | tf_op jit(solution)/shard_map/ppermute | solution.py:604
  24.5 0.0 collective-permute-done.1.x_hi
  24.5 1.4 %strip.1 = (f32[4,96,128]{2,1,0:T(8,128)}, f32[4,96,128]{2,1,0:T(8,128)}) custom-call(s32[1024]{0:T(1024)S(1)} %bitcast.13, f32[42,32,128]{2,1,0:T(8,128)S(1)} %collective-permute-done.x_lo, f32[42,32,128]{2,1,0:T(8,128)S(1)} %collective-permute-done.1.x_hi, f32[128,128]{1,0:T(8,128)S(1)} %get-tuple-element.28.places), custom_call_target="tpu_custom_call" | custom-call | tf_op jit(solution)/shard_map/strip/pallas_call | solution.py:647
  26.0 1.5 %collective-permute-start.4 = (f32[4,96,128]{2,1,0:T(8,128)}, f32[4,96,128]{2,1,0:T(8,128)S(1)}, u32[]{:S(2)}, u32[]{:S(2)}) collective-permute-start(f32[4,96,128]{2,1,0:T(8,128)} %get-tuple-element.29), channel_id=1, source_target_pairs={{0,8},{8,16},{16,24},{24,0},{1,9},{9,17},{17,25},{25,1},{2,10},{10... | collective-permute-start | bytes 589832 | tf_op jit(solution)/shard_map/ppermute | solution.py:604
  27.4 1.7 %collective-permute-start.5 = (f32[4,96,128]{2,1,0:T(8,128)}, f32[4,96,128]{2,1,0:T(8,128)}, u32[]{:S(2)}, u32[]{:S(2)}) collective-permute-start(f32[4,96,128]{2,1,0:T(8,128)} %get-tuple-element.30), channel_id=1, source_target_pairs={{0,24},{8,0},{16,8},{24,16},{1,25},{9,1},{17,9},{25,17},{2,26},{10... | collective-permute-start | bytes 589832 | tf_op jit(solution)/shard_map/ppermute | solution.py:604
  29.2 0.6 stack.27
  29.8 0.6 convert_element_type.3.edge
  30.5 0.0 collective-permute-done.2.y_lo
  30.5 0.0 collective-permute-done.3.y_hi
  30.5 3.0 %collective-permute-done.4.c_lo = f32[4,96,128]{2,1,0:T(8,128)S(1)} collective-permute-done((f32[4,96,128]{2,1,0:T(8,128)}, f32[4,96,128]{2,1,0:T(8,128)S(1)}, u32[]{:S(2)}, u32[]{:S(2)}) %collective-permute-start.4) | collective-permute-done | bytes 196640 | tf_op jit(solution)/shard_map/ppermute | solution.py:604
  33.4 0.1 collective-permute-done.5.c_hi
  33.5 1.7 %copy-done.1 = f32[5,32,32,128]{3,2,1,0:T(8,128)S(1)} copy-done((f32[5,32,32,128]{3,2,1,0:T(8,128)S(1)}, f32[5,32,32,128]{3,2,1,0:T(8,128)}, u32[]{:S(2)}) %copy-start.1) | copy-done | bytes 2621464
  35.3 5.5 %build.1 = (f32[4,52,64,128]{3,2,1,0:T(8,128)S(1)}, f32[2,34,56,128]{3,2,1,0:T(8,128)S(1)}, f32[22,56,128]{2,1,0:T(8,128)S(1)}, f32[22,56,128]{2,1,0:T(8,128)S(1)}) custom-call(f32[6]{0:T(128)S(1)} %convert_element_type.3.edge, f32[32,32,128]{2,1,0:T(8,128)S(1)} %copy-done.2, f32[5,32,32,128]{3,2,1,0:T(8,128)S(1)} %copy-done.1, ...), custom_call_target="tpu_custom_call" | custom-call | tf_op jit(solution)/shard_map/build/pallas_call | solution.py:651
  40.8 0.0 collective-permute-start.6
  40.9 2.9 %collective-permute-start.7 = (f32[22,56,128]{2,1,0:T(8,128)S(1)}, f32[22,56,128]{2,1,0:T(8,128)S(1)}, u32[]{:S(2)}, u32[]{:S(2)}) collective-permute-start(f32[22,56,128]{2,1,0:T(8,128)S(1)} %get-tuple-element.34.z_first), channel_id=1, source_target_pairs={{0,7},{1,0},{2,1},{3,2},{4,3},{5,4},{6,5},{7,6},{8,15},{9,8},{10,9... | collective-permute-start | bytes 1892360 | tf_op jit(solution)/shard_map/ppermute | solution.py:604
  43.8 5.7 %assemble.1 = (f32[6,52,56,128]{3,2,1,0:T(8,128)S(1)}, f32[52,72,128]{2,1,0:T(8,128)S(1)}, f32[52,56,128]{2,1,0:T(8,128)S(1)}) custom-call(f32[4,52,64,128]{3,2,1,0:T(8,128)S(1)} %get-tuple-element.31.ext), custom_call_target="tpu_custom_call" | custom-call | tf_op jit(solution)/shard_map/assemble/pallas_call | solution.py:662
  49.6 2.2 %collective-permute-done.6.z_lo = f32[22,56,128]{2,1,0:T(8,128)S(1)} collective-permute-done((f32[22,56,128]{2,1,0:T(8,128)S(1)}, f32[22,56,128]{2,1,0:T(8,128)S(1)}, u32[]{:S(2)}, u32[]{:S(2)}) %collective-permute-start.6) | collective-permute-done | bytes 630816 | tf_op jit(solution)/shard_map/ppermute | solution.py:604
  51.8 0.0 collective-permute-done.7.z_hi
  51.8 19.8 %solve.1 = (f32[3200,128]{1,0:T(8,128)S(1)}, f32[6,52,56,128]{3,2,1,0:T(8,128)S(1)}, f32[52,72,128]{2,1,0:T(8,128)S(1)}, f32[52,56,128]{2,1,0:T(8,128)S(1)}) custom-call(f32[6]{0:T(128)S(1)} %convert_element_type.3.edge, s32[1024]{0:T(1024)S(1)} %bitcast.14, ...), custom_call_target="tpu_custom_call", output_to_operand_aliasing={{1}: (13, {}), {2}: (14, {}), {3}: (15, {})} | custom-call | tf_op jit(solution)/shard_map/solve/pallas_call | solution.py:663
  71.7 34.9 %all_to_all.5 = f32[128,25,1,128]{3,2,1,0:T(1,128)S(1)} all-to-all(f32[128,25,1,128]{3,2,1,0:T(1,128)S(1)} %bitcast.12), channel_id=1, replica_groups=mesh['gx'=4,'gy'=4,'gz'=8] {'gx','gy','gz'}, dimensions={0} | all-to-all | bytes 3276800 | tf_op jit(solution)/shard_map/all_to_all | solution.py:689
  106.6 4.1 %unpack.1 = f32[3,640,128]{2,1,0:T(8,128)} custom-call(f32[3200,128]{1,0:T(8,128)S(1)} %bitcast.11), custom_call_target="tpu_custom_call" | custom-call | tf_op jit(solution)/shard_map/unpack/pallas_call | solution.py:692
  (19 shorter events, 0.0 us)
Async XLA Ops:
  0.0 33.5 %copy-start.2 = (f32[32,32,128]{2,1,0:T(8,128)S(1)}, f32[32,32,128]{2,1,0:T(8,128)}, u32[]{:S(2)}) copy-start(f32[32,32,128]{2,1,0:T(8,128)} %p.1) | copy-start | bytes 1572868
  0.0 12.7 %copy-start.8 = (s32[32,32,1]{1,2,0:T(1,128)S(1)}, s32[32,32,1]{1,2,0:T(1,128)}, u32[]{:S(2)}) copy-start(s32[32,32,1]{1,2,0:T(1,128)} %param.14) | copy-start | bytes 12292
  0.0 13.4 %copy-start.9 = (s32[32,32,1]{1,2,0:T(1,128)S(1)}, s32[32,32,1]{1,2,0:T(1,128)}, u32[]{:S(2)}) copy-start(s32[32,32,1]{1,2,0:T(1,128)} %param.15) | copy-start | bytes 12292
  4.7 19.9 %collective-permute-start = (f32[42,32,128]{2,1,0:T(8,128)}, f32[42,32,128]{2,1,0:T(8,128)S(1)}, u32[]{:S(2)}, u32[]{:S(2)}) collective-permute-start(f32[42,32,128]{2,1,0:T(8,128)} %get-tuple-element.24), channel_id=1, source_target_pairs={{0,32},{32,64},{64,96},{96,0},{1,33},{33,65},{65,97},{97,1},{2,34}... | collective-permute-start | bytes 2064392 | tf_op jit(solution)/shard_map/ppermute | solution.py:604
  6.8 17.8 %collective-permute-start.1 = (f32[42,32,128]{2,1,0:T(8,128)}, f32[42,32,128]{2,1,0:T(8,128)S(1)}, u32[]{:S(2)}, u32[]{:S(2)}) collective-permute-start(f32[42,32,128]{2,1,0:T(8,128)} %get-tuple-element.25), channel_id=1, source_target_pairs={{0,96},{32,0},{64,32},{96,64},{1,97},{33,1},{65,33},{97,65},{2,98}... | collective-permute-start | bytes 2064392 | tf_op jit(solution)/shard_map/ppermute | solution.py:604
  9.0 21.5 %collective-permute-start.2 = (f32[34,40,128]{2,1,0:T(8,128)}, f32[34,40,128]{2,1,0:T(8,128)S(1)}, u32[]{:S(2)}, u32[]{:S(2)}) collective-permute-start(f32[34,40,128]{2,1,0:T(8,128)} %get-tuple-element.26), channel_id=1, source_target_pairs={{0,8},{8,16},{16,24},{24,0},{1,9},{9,17},{17,25},{25,1},{2,10},{10... | collective-permute-start | bytes 2088968 | tf_op jit(solution)/shard_map/ppermute | solution.py:604
  10.5 20.0 %collective-permute-start.3 = (f32[34,40,128]{2,1,0:T(8,128)}, f32[34,40,128]{2,1,0:T(8,128)S(1)}, u32[]{:S(2)}, u32[]{:S(2)}) collective-permute-start(f32[34,40,128]{2,1,0:T(8,128)} %get-tuple-element.27), channel_id=1, source_target_pairs={{0,24},{8,0},{16,8},{24,16},{1,25},{9,1},{17,9},{25,17},{2,26},{10... | collective-permute-start | bytes 2088968 | tf_op jit(solution)/shard_map/ppermute | solution.py:604
  15.7 10.2 %copy-start.6 = (s32[8,128]{1,0:T(8,128)}, s32[8,128]{1,0:T(8,128)S(1)}, u32[]{:S(2)}) copy-start(s32[8,128]{1,0:T(8,128)S(1)} %get-tuple-element.22) | copy-start | bytes 12292
  26.0 7.5 %collective-permute-start.4 = (f32[4,96,128]{2,1,0:T(8,128)}, f32[4,96,128]{2,1,0:T(8,128)S(1)}, u32[]{:S(2)}, u32[]{:S(2)}) collective-permute-start(f32[4,96,128]{2,1,0:T(8,128)} %get-tuple-element.29), channel_id=1, source_target_pairs={{0,8},{8,16},{16,24},{24,0},{1,9},{9,17},{17,25},{25,1},{2,10},{10... | collective-permute-start | bytes 589832 | tf_op jit(solution)/shard_map/ppermute | solution.py:604
  27.4 6.1 %collective-permute-start.5 = (f32[4,96,128]{2,1,0:T(8,128)}, f32[4,96,128]{2,1,0:T(8,128)}, u32[]{:S(2)}, u32[]{:S(2)}) collective-permute-start(f32[4,96,128]{2,1,0:T(8,128)} %get-tuple-element.30), channel_id=1, source_target_pairs={{0,24},{8,0},{16,8},{24,16},{1,25},{9,1},{17,9},{25,17},{2,26},{10... | collective-permute-start | bytes 589832 | tf_op jit(solution)/shard_map/ppermute | solution.py:604
  33.5 1.7 %copy-start.1 = (f32[5,32,32,128]{3,2,1,0:T(8,128)S(1)}, f32[5,32,32,128]{3,2,1,0:T(8,128)}, u32[]{:S(2)}) copy-start(f32[5,32,32,128]{3,2,1,0:T(8,128)} %get-tuple-element.23.own) | copy-start | bytes 7864324
  40.8 11.0 %collective-permute-start.6 = (f32[22,56,128]{2,1,0:T(8,128)S(1)}, f32[22,56,128]{2,1,0:T(8,128)S(1)}, u32[]{:S(2)}, u32[]{:S(2)}) collective-permute-start(f32[22,56,128]{2,1,0:T(8,128)S(1)} %get-tuple-element.33.z_last), channel_id=1, source_target_pairs={{0,1},{1,2},{2,3},{3,4},{4,5},{5,6},{6,7},{7,0},{8,9},{9,10},{10,1... | collective-permute-start | bytes 1892360 | tf_op jit(solution)/shard_map/ppermute | solution.py:604
  40.9 10.9 %collective-permute-start.7 = (f32[22,56,128]{2,1,0:T(8,128)S(1)}, f32[22,56,128]{2,1,0:T(8,128)S(1)}, u32[]{:S(2)}, u32[]{:S(2)}) collective-permute-start(f32[22,56,128]{2,1,0:T(8,128)S(1)} %get-tuple-element.34.z_first), channel_id=1, source_target_pairs={{0,7},{1,0},{2,1},{3,2},{4,3},{5,4},{6,5},{7,6},{8,15},{9,8},{10,9... | collective-permute-start | bytes 1892360 | tf_op jit(solution)/shard_map/ppermute | solution.py:604
  43.8 8.0 %copy-start = (f32[2,32,32,128]{3,2,1,0:T(8,128)S(1)}, f32[2,32,32,128]{3,2,1,0:T(8,128)}, u32[]{:S(2)}) copy-start(f32[2,32,32,128]{3,2,1,0:T(8,128)} %sat.1) | copy-start | bytes 3145732
  43.8 8.0 %copy-start.3 = (f32[32,32,128]{2,1,0:T(8,128)S(1)}, f32[32,32,128]{2,1,0:T(8,128)}, u32[]{:S(2)}) copy-start(f32[32,32,128]{2,1,0:T(8,128)} %sto.1) | copy-start | bytes 1572868
  43.8 8.0 %copy-start.4 = (s32[32,32,128]{2,1,0:T(8,128)S(1)}, s32[32,32,128]{2,1,0:T(8,128)}, u32[]{:S(2)}) copy-start(s32[32,32,128]{2,1,0:T(8,128)} %mask.1) | copy-start | bytes 1572868
  43.8 8.0 %copy-start.5 = (f32[2,32,32,128]{3,2,1,0:T(8,128)S(1)}, f32[2,32,32,128]{3,2,1,0:T(8,128)}, u32[]{:S(2)}) copy-start(f32[2,32,32,128]{3,2,1,0:T(8,128)} %old.1) | copy-start | bytes 3145732
  43.8 8.0 %copy-start.7 = (s32[8,128]{1,0:T(8,128)S(1)}, s32[8,128]{1,0:T(8,128)}, u32[]{:S(2)}) copy-start(s32[8,128]{1,0:T(8,128)} %copy-done.6) | copy-start | bytes 12292

commit v5 on v4

--- a/solution.py
+++ b/solution.py
@@ -18,6 +18,7 @@
 ZG = 10
 NQ = 5
 SOLVE_MIB = 20
+LIMITS = {"index": 4, "strip": 6, "seed": 12, "flank": 16, "corner": 20, "assemble": 16, "unpack": 8}
 PAD = 8
 ZS = 12
 
@@ -90,8 +91,8 @@
         xp[4 * H + f] = own[3 + f, T - 1]
 
 
-def strip_kernel(dst, x_lo, x_hi, places, cm, cp):
-    del dst, places
+def strip_kernel(dst, x_lo, x_hi, places, zm, cm, cp):
+    del dst, places, zm
     for f in range(4):
         for side, src in ((0, x_lo), (1, x_hi)):
             for dist in range(1, H):
@@ -114,87 +115,126 @@
 
 
 def turn(v, by):
-    return pltpu.roll(v, by % L if isinstance(by, int) else lax.rem(by + 2 * L, L), 1)
-
-
-def build_kernel(edge, p, own, x_lo, x_hi, y_lo, y_hi, c_lo, c_hi, ext, aext, zm, zp):
-    def cells(q, carry):
+    if isinstance(by, int):
+        return pltpu.roll(v, by % L, 1) if by % L else v
+    return pltpu.roll(v, lax.rem(by + 2 * L, L), 1)
+
+
+MID = slice(OJ, OJ + T)
+
+
+def packing(g, rows):
+    lane = lanes_of(rows)
+    first = lane - ZS * g
+    last = lane - (ZS * g - H) % L if isinstance(g, int) else lane - lax.rem(ZS * g + L - H, L)
+    return (first >= 0) & (first < H), (last >= 0) & (last < H)
+
+
+def put(ext, zm, zp, f, i, rows, value, masks):
+    if isinstance(i, int):
+        q, g = (i - 1) % NQ, (i - 1) // NQ
+    else:
+        q, g = lax.rem(i - 1, NQ), lax.div(i - 1, NQ)
+    r = turn(value, ZS * g)
+    ext[f, i, rows] = r
+    pltpu.store(zm.at[f * NQ + q, rows], r, mask=masks[0])
+    pltpu.store(zp.at[f * NQ + q, rows], r, mask=masks[1])
+
+
+def seed_kernel(p, own, turned, aext, zm, zp):
+    lane = lanes_of(T)
+
+    def plane(i, carry):
+        e = i + H
+        g = lax.div(e - 1, NQ)
+        masks = packing(g, T)
+        for f in range(4):
+            r = turn(p[i] if f == 0 else own[f - 1, i], ZS * g)
+            turned[f, i] = r
+            s = f * NQ + lax.rem(e - 1, NQ)
+            pltpu.store(zm.at[s, MID], r, mask=masks[0])
+            pltpu.store(zp.at[s, MID], r, mask=masks[1])
+        spot = 2 * i
+        for f in range(2):
+            v = own[3 + f, i]
+            aext[f, i] = turn(v, ZS * g)
+            r = turn(v, spot)
+            pltpu.store(zm.at[4 * NQ + f, MID], r, mask=lane == spot)
+            pltpu.store(zp.at[4 * NQ + f, MID], r, mask=lane == lax.rem(spot + L - 1, L))
+        return carry
+
+    lax.fori_loop(0, T, plane, 0, unroll=4)
+
+
+def flank_kernel(
+    edge, y_lo, y_hi, x_lo, x_hi, turned, aext_in, zm_in, zp_in, ext, aext, zm, zp
+):
+    zm[...] = zm_in[...]
+    zp[...] = zp_in[...]
+
+    def planes(block, carry):
         for u in range(4):
-            i = q * 4 + u
+            i = block * 4 + u
+            e = i + H
+            masks = packing(lax.div(e - 1, NQ), H)
+            shift = ZS * lax.div(e - 1, NQ)
+            for src, rows, k in (
+                (y_lo, slice(OJ - H, OJ), 2),
+                (y_hi, slice(OJ + T, OJ + T + H), 3),
+            ):
+                for f in range(4):
+                    v = src[f * 8 + block, 10 * u : 10 * u + 10]
+                    put(ext, zm, zp, f, e, rows, v * edge[k] if f == 1 else v, masks)
             for f in range(4):
-                lo = y_lo[f * 8 + q, 10 * u : 10 * u + 10]
-                hi = y_hi[f * 8 + q, 10 * u : 10 * u + 10]
-                if f == 1:
-                    lo, hi = lo * edge[2], hi * edge[3]
-                ext[f, H + i, OJ - H : OJ] = lo
-                ext[f, H + i, OJ : OJ + T] = p[i] if f == 0 else own[f - 1, i]
-                ext[f, H + i, OJ + T : OJ + T + H] = hi
+                ext[f, e, MID] = turned[f, i]
             for f in range(2):
-                aext[f, 1 + i, OJ - 1 : OJ] = y_lo[32 + f, pl.ds(i, 1)]
-                aext[f, 1 + i, OJ : OJ + T] = own[3 + f, i]
-                aext[f, 1 + i, OJ + T : OJ + T + 1] = y_hi[32 + f, pl.ds(i, 1)]
-        return carry
-
-    lax.fori_loop(0, 8, cells, 0)
-    for f in range(4):
-        for side, src in ((0, x_lo), (1, x_hi)):
-            for dist in range(1, H + 1):
-                t = plane_of(side, dist)
-                i = t if side == 0 else H + T + t
+                aext[f, 1 + i, MID] = aext_in[f, i]
+                aext[f, 1 + i, OJ - 1 : OJ] = turn(y_lo[32 + f, pl.ds(i, 1)], shift)
+                aext[f, 1 + i, OJ + T : OJ + T + 1] = turn(y_hi[32 + f, pl.ds(i, 1)], shift)
+        return carry
+
+    lax.fori_loop(0, 8, planes, 0)
+    for side, src in ((0, x_lo), (1, x_hi)):
+        for dist in range(1, H + 1):
+            t = plane_of(side, dist)
+            i = t if side == 0 else H + T + t
+            for f in range(4 if dist < H else 3):
                 v = src[f * H + t]
                 if f == 1:
                     v = v * edge[side]
-                ext[f, i, OJ : OJ + T] = v
-                n = H - dist
-                if n:
-                    at = STRIPS[side, dist]
-                    lo, hi = c_lo[f, at : at + n], c_hi[f, at : at + n]
-                    if f == 1:
-                        lo, hi = lo * (edge[side] * edge[2]), hi * (edge[side] * edge[3])
-                    ext[f, i, OJ - n : OJ] = lo
-                    ext[f, i, OJ + T : OJ + T + n] = hi
-    for f in range(2):
-        aext[f, 0, OJ : OJ + T] = x_lo[4 * H + f]
-        aext[f, T + 1, OJ : OJ + T] = x_hi[4 * H + f]
-    lane = lanes_of(EJ)
-
-    def pack(s, carry):
-        f, q = s // NQ, s % NQ
-        low = jnp.zeros((EJ, L), F32)
-        high = low
-        for g in range(ZG):
-            i = 1 + q + NQ * g
-            r = ext[f, i, :EJ]
-            if g:
-                r = turn(r, ZS * g)
-                ext[f, i, :EJ] = r
-            low = jnp.where((lane >= ZS * g) & (lane < ZS * g + H), r, low)
-            first = (ZS * g - H) % L
-            high = jnp.where((lane >= first) & (lane < first + H), r, high)
-        zm[s] = low
-        zp[s] = high
-        return carry
-
-    lax.fori_loop(0, 4 * NQ, pack, 0)
-    for f in range(3):
-        ext[f, EI - 1, :EJ] = turn(ext[f, EI - 1, :EJ], ZS * ZG)
-
-    def pack_share(f, carry):
-        low = jnp.zeros((EJ, L), F32)
-        high = low
-        for i in range(T + 2):
-            v = aext[f, i]
-            if 1 <= i <= T:
-                spot = 2 * (i - 1)
-                r = turn(v, spot) if spot else v
-                low = jnp.where(lane == spot, r, low)
-                high = jnp.where(lane == (spot + L - 1) % L, r, high)
-            aext[f, i] = turn(v, ZS * ((i + H - 2) // NQ))
-        zm[4 * NQ + f] = low
-        zp[4 * NQ + f] = high
-        return carry
-
-    lax.fori_loop(0, 2, pack_share, 0)
+                if dist < H:
+                    put(ext, zm, zp, f, i, MID, v, packing((i - 1) // NQ, T))
+                else:
+                    ext[f, i, MID] = turn(v, 0 if side == 0 else ZS * ZG)
+        for f in range(2):
+            i = 0 if side == 0 else T + 1
+            aext[f, i, MID] = turn(src[4 * H + f], ZS * ((i + H - 2) // NQ))
+
+
+def corner_kernel(
+    edge, c_lo, c_hi, ext_in, zm_in, zp_in, ext, zm, zp
+):
+    zm[...] = zm_in[...]
+    zp[...] = zp_in[...]
+
+    def carry_over(i, carry):
+        for f in range(4):
+            ext[f, i, :EJ] = ext_in[f, i, :EJ]
+        return carry
+
+    lax.fori_loop(0, EI, carry_over, 0)
+    for side in (0, 1):
+        for dist in range(1, H):
+            t = plane_of(side, dist)
+            i = t if side == 0 else H + T + t
+            n, at = H - dist, STRIPS[side, dist]
+            masks = packing((i - 1) // NQ, n)
+            for f in range(4):
+                lo, hi = c_lo[f, at : at + n], c_hi[f, at : at + n]
+                if f == 1:
+                    lo, hi = lo * (edge[side] * edge[2]), hi * (edge[side] * edge[3])
+                put(ext, zm, zp, f, i, slice(OJ - n, OJ), lo, masks)
+                put(ext, zm, zp, f, i, slice(OJ + T, OJ + T + n), hi, masks)
 
 
 def face(p, c, m, pn, cn, mn):
@@ -591,7 +631,7 @@
         out_specs=[spec(s) for s in spaces] if many else spec(spaces),
         scratch_shapes=list(scratch),
         input_output_aliases=alias or {},
-        compiler_params=pltpu.CompilerParams(vmem_limit_bytes=limit << 20),
+        compiler_params=pltpu.CompilerParams(vmem_limit_bytes=LIMITS.get(name, limit) << 20),
     )
 
 
@@ -644,18 +684,25 @@
     )(row_owner.reshape(table), row_slot.reshape(table))
     dst = dst.reshape(T * T)
 
-    cm, cp = call(strip_kernel, "strip", (shape(4, 96, L), shape(4, 96, L)), 1, 3)(
-        dst, x_lo, x_hi, places
+    planes = (
+        shape(4, EI, EJ + 8, L),
+        shape(2, T + 2, EJ, L),
+        shape(22, EJ, L),
+        shape(22, EJ, L),
+    )
+    turned, tile_share, zm, zp = call(
+        seed_kernel, "seed", (shape(4, T, T, L), shape(2, T, T, L)) + planes[2:], 0, 2
+    )(pressure, own)
+    cm, cp = call(strip_kernel, "strip", (shape(4, 96, L), shape(4, 96, L)), 1, 4)(
+        dst, x_lo, x_hi, places, zm
     )
     c_lo, c_hi = swap(cm, cp, "gy")
-    ext, aext, zm, zp = call(
-        build_kernel,
-        "build",
-        (shape(4, EI, EJ + 8, L), shape(2, T + 2, EJ, L), shape(22, EJ, L), shape(22, EJ, L)),
-        1,
-        8,
-        limit=24,
-    )(edge, pressure, own, x_lo, x_hi, y_lo, y_hi, c_lo, c_hi)
+    ext, aext, zm, zp = call(flank_kernel, "flank", planes, 1, 8)(
+        edge, y_lo, y_hi, x_lo, x_hi, turned, tile_share, zm, zp
+    )
+    ext, zm, zp = call(corner_kernel, "corner", (planes[0], planes[2], planes[3]), 1, 5)(
+        edge, c_lo, c_hi, ext, zm, zp
+    )
     z_lo, z_hi = swap(zm, zp, "gz")
     grid, tall = (EI, EJ, L), (EI, EJ + 2 * PAD, L)
     rows_of = (shape(6, *grid), shape(*tall), shape(*grid))

time: 111 us -> 106 us (0.955)
  waiting for transfers between devices: 14.1 us -> 4.35 us
  local copies, waits for them, and re-layouts: 3.07 us -> 8.34 us
    ppermute x4, waiting for transfers between devices: 14 us -> 4.34 us  [swap(): lax.ppermute(high, axis, ring(axis, 1))]
    unnamed x21 -> x29, local copies, waits for them, and re-layouts: 2.28 us -> 8.1 us
    pallas_call x2 -> x4, Pallas kernels: 6.95 us -> 7.46 us  [the longest x1 3.08 us: body(): call(flank_kernel, 'flank', planes, 1, 8)]
  transfers between devices with their start and end apart: 8 -> 8, of which waited for: 4 -> 2; matrix products, arithmetic and copies ran while one was open for 3% -> 2% of each run, Pallas kernels for 8% -> 13%
where the time goes in v5:
time: 106 us; the launch traced here: 105 us
  Pallas kernels  43.7 us (41%)
  blocking collectives  33.8 us (32%)
  starting transfers between devices  13.7 us (13%)
  local copies, waits for them, and re-layouts  8.34 us (8%)
  waiting for transfers between devices  4.35 us (4%)
  other arithmetic  1.34 us (1%)
    all_to_all x1, blocking collectives, body(): lax.all_to_all(send.reshape(devices, chunk, 1, L), AXES, split_axis=0, co...  33.8 us
    pallas_call x1, Pallas kernels, body(): call(solve_kernel, 'solve', (shape(devices * chunk, L),) + rows_of, 2, 14...  20.1 us
    ppermute x4, starting transfers between devices, swap(): lax.ppermute(low, axis, ring(axis, -1))  8.63 us
    unnamed x29, local copies, waits for them, and re-layouts  8.1 us
    pallas_call x1, Pallas kernels, body(): mat, base, total = call(assemble_kernel, 'assemble', rows_of, 0, 1)(ext)  5.76 us
    ppermute x4, starting transfers between devices, swap(): lax.ppermute(high, axis, ring(axis, 1))  5.1 us
    pallas_call x1, Pallas kernels, body(): call(prep_kernel, 'prep', (shape(5, T, T, L), shape(4 * H + 2, T, L), sha...  4.66 us
    ppermute x4, waiting for transfers between devices, swap(): lax.ppermute(high, axis, ring(axis, 1))  4.34 us
  transfers between devices with their start and end apart: 8, of which 2 were waited for; matrix products, arithmetic and copies ran while one was open for 2% of the time, Pallas kernels for 13%

profile of v5, /device:TPU:0, one launch (start us, length us, event | category | flops | bytes accessed | tf_op | source)
XLA Modules:
  0.0 105.5 jit_solution(9232306202894524114)
XLA Ops:
  0.0 4.7 %prep.1 = (f32[5,32,32,128]{3,2,1,0:T(8,128)}, f32[42,32,128]{2,1,0:T(8,128)}, f32[42,32,128]{2,1,0:T(8,128)}, f32[34,40,128]{2,1,0:T(8,128)}, f32[34,40,128]{2,1,0:T(8,128)}) custom-call(f32[32,32,128]{2,1,0:T(8,128)} %p.1, f32[2,32,32,128]{3,2,1,0:T(8,128)} %sat.1, f32[32,32,128]{2,1,0:T(8,128)} %perm_far.1, f32[32,32,128]{2,1,0:T(8,128)} %sto.1, ...), custom_call_target="tpu_custom_call" | custom-call | tf_op jit(solution)/shard_map/prep/pallas_call | solution.py:659
  4.7 2.1 %collective-permute-start = (f32[42,32,128]{2,1,0:T(8,128)}, f32[42,32,128]{2,1,0:T(8,128)S(1)}, u32[]{:S(2)}, u32[]{:S(2)}) collective-permute-start(f32[42,32,128]{2,1,0:T(8,128)} %get-tuple-element.30), channel_id=1, source_target_pairs={{0,32},{32,64},{64,96},{96,0},{1,33},{33,65},{65,97},{97,1},{2,34}... | collective-permute-start | bytes 2064392 | tf_op jit(solution)/shard_map/ppermute | solution.py:644
  6.8 2.2 %collective-permute-start.1 = (f32[42,32,128]{2,1,0:T(8,128)}, f32[42,32,128]{2,1,0:T(8,128)S(1)}, u32[]{:S(2)}, u32[]{:S(2)}) collective-permute-start(f32[42,32,128]{2,1,0:T(8,128)} %get-tuple-element.31), channel_id=1, source_target_pairs={{0,96},{32,0},{64,32},{96,64},{1,97},{33,1},{65,33},{97,65},{2,98}... | collective-permute-start | bytes 2064392 | tf_op jit(solution)/shard_map/ppermute | solution.py:644
  9.0 1.5 %collective-permute-start.4 = (f32[34,40,128]{2,1,0:T(8,128)}, f32[34,40,128]{2,1,0:T(8,128)}, u32[]{:S(2)}, u32[]{:S(2)}) collective-permute-start(f32[34,40,128]{2,1,0:T(8,128)} %get-tuple-element.37), channel_id=1, source_target_pairs={{0,8},{8,16},{16,24},{24,0},{1,9},{9,17},{17,25},{25,1},{2,10},{10... | collective-permute-start | bytes 2088968 | tf_op jit(solution)/shard_map/ppermute | solution.py:644
  10.5 1.7 %collective-permute-start.5 = (f32[34,40,128]{2,1,0:T(8,128)}, f32[34,40,128]{2,1,0:T(8,128)}, u32[]{:S(2)}, u32[]{:S(2)}) collective-permute-start(f32[34,40,128]{2,1,0:T(8,128)} %get-tuple-element.38), channel_id=1, source_target_pairs={{0,24},{8,0},{16,8},{24,16},{1,25},{9,1},{17,9},{25,17},{2,26},{10... | collective-permute-start | bytes 2088968 | tf_op jit(solution)/shard_map/ppermute | solution.py:644
  12.2 0.5 broadcast.6
  12.7 0.7 reduce.6
  13.4 0.1 reshape.15.owner
  13.5 0.7 reduce.7
  14.2 0.1 reshape.16.slot
  14.2 1.7 %copy-done.1 = f32[5,32,32,128]{3,2,1,0:T(8,128)S(1)} copy-done((f32[5,32,32,128]{3,2,1,0:T(8,128)S(1)}, f32[5,32,32,128]{3,2,1,0:T(8,128)}, u32[]{:S(2)}) %copy-start.1) | copy-done | bytes 2621464
  16.0 1.6 %seed.1 = (f32[4,32,32,128]{3,2,1,0:T(8,128)S(1)}, f32[2,32,32,128]{3,2,1,0:T(8,128)S(1)}, f32[22,56,128]{2,1,0:T(8,128)S(1)}, f32[22,56,128]{2,1,0:T(8,128)S(1)}) custom-call(f32[32,32,128]{2,1,0:T(8,128)S(1)} %copy-done.6, f32[5,32,32,128]{3,2,1,0:T(8,128)S(1)} %copy-done.1), custom_call_target="tpu_custom_call" | custom-call | tf_op jit(solution)/shard_map/seed/pallas_call | solution.py:693
  17.6 1.3 %copy-done.2 = f32[4,32,32,128]{3,2,1,0:T(8,128)} copy-done((f32[4,32,32,128]{3,2,1,0:T(8,128)}, f32[4,32,32,128]{3,2,1,0:T(8,128)S(1)}, u32[]{:S(2)}) %copy-start.2) | copy-done | bytes 2097176
  19.0 1.0 copy-done.8
  20.0 0.8 copy-done.10
  20.8 1.6 %index.1 = (s32[8,128]{1,0:T(8,128)S(1)}, f32[128,128]{1,0:T(8,128)S(1)}) custom-call(s32[8,128]{1,0:T(8,128)S(1)} %reshape.15.owner, s32[8,128]{1,0:T(8,128)S(1)} %reshape.16.slot), custom_call_target="tpu_custom_call" | custom-call | tf_op jit(solution)/shard_map/index/pallas_call | solution.py:682
  22.4 2.1 %collective-permute-done.x_lo = f32[42,32,128]{2,1,0:T(8,128)S(1)} collective-permute-done((f32[42,32,128]{2,1,0:T(8,128)}, f32[42,32,128]{2,1,0:T(8,128)S(1)}, u32[]{:S(2)}, u32[]{:S(2)}) %collective-permute-start) | collective-permute-done | bytes 688160 | tf_op jit(solution)/shard_map/ppermute | solution.py:644
  24.5 1.4 %strip.1 = (f32[4,96,128]{2,1,0:T(8,128)}, f32[4,96,128]{2,1,0:T(8,128)}) custom-call(s32[1024]{0:T(1024)S(1)} %bitcast.13, f32[42,32,128]{2,1,0:T(8,128)S(1)} %collective-permute-done.x_lo, f32[42,32,128]{2,1,0:T(8,128)S(1)} %collective-permute-done.1.x_hi, f32[128,128]{1,0:T(8,128)S(1)} %get-tuple-element.32.places, ...), custom_call_target="tpu_custom_call" | custom-call | tf_op jit(solution)/shard_map/strip/pallas_call | solution.py:696
  26.0 1.5 %collective-permute-start.2 = (f32[4,96,128]{2,1,0:T(8,128)}, f32[4,96,128]{2,1,0:T(8,128)S(1)}, u32[]{:S(2)}, u32[]{:S(2)}) collective-permute-start(f32[4,96,128]{2,1,0:T(8,128)} %get-tuple-element.35), channel_id=1, source_target_pairs={{0,8},{8,16},{16,24},{24,0},{1,9},{9,17},{17,25},{25,1},{2,10},{10... | collective-permute-start | bytes 589832 | tf_op jit(solution)/shard_map/ppermute | solution.py:644
  27.4 1.7 %collective-permute-start.3 = (f32[4,96,128]{2,1,0:T(8,128)}, f32[4,96,128]{2,1,0:T(8,128)S(1)}, u32[]{:S(2)}, u32[]{:S(2)}) collective-permute-start(f32[4,96,128]{2,1,0:T(8,128)} %get-tuple-element.36), channel_id=1, source_target_pairs={{0,24},{8,0},{16,8},{24,16},{1,25},{9,1},{17,9},{25,17},{2,26},{10... | collective-permute-start | bytes 589832 | tf_op jit(solution)/shard_map/ppermute | solution.py:644
  29.2 0.1 stack.27
  29.3 1.6 %copy-done.3 = f32[4,32,32,128]{3,2,1,0:T(8,128)S(1)} copy-done((f32[4,32,32,128]{3,2,1,0:T(8,128)S(1)}, f32[4,32,32,128]{3,2,1,0:T(8,128)}, u32[]{:S(2)}) %copy-start.3) | copy-done | bytes 2097176
  30.9 1.1 %copy-done.11 = f32[22,56,128]{2,1,0:T(8,128)S(1)} copy-done((f32[22,56,128]{2,1,0:T(8,128)S(1)}, f32[22,56,128]{2,1,0:T(8,128)}, u32[]{:S(2)}) %copy-start.11) | copy-done | bytes 630808
  32.0 3.1 %flank.1 = (f32[4,52,64,128]{3,2,1,0:T(8,128)S(1)}, f32[2,34,56,128]{3,2,1,0:T(8,128)S(1)}, f32[22,56,128]{2,1,0:T(8,128)S(1)}, f32[22,56,128]{2,1,0:T(8,128)S(1)}) custom-call(f32[6]{0:T(128)S(1)} %convert_element_type.3.edge, f32[34,40,128]{2,1,0:T(8,128)} %collective-permute-done.4.y_lo, f32[34,40,128]{2,1,0:T(8,128)} %collective-permute-done.5.y_hi, ...), custom_call_target="tpu_custom_call" | custom-call | tf_op jit(solution)/shard_map/flank/pallas_call | solution.py:700
  35.1 1.3 %corner.1 = (f32[4,52,64,128]{3,2,1,0:T(8,128)S(1)}, f32[22,56,128]{2,1,0:T(8,128)S(1)}, f32[22,56,128]{2,1,0:T(8,128)S(1)}) custom-call(f32[6]{0:T(128)S(1)} %convert_element_type.3.edge, f32[4,96,128]{2,1,0:T(8,128)S(1)} %collective-permute-done.2.c_lo, f32[4,96,128]{2,1,0:T(8,128)S(1)} %collective-permute-done.3.c_hi, ...), custom_call_target="tpu_custom_call" | custom-call | tf_op jit(solution)/shard_map/corner/pallas_call | solution.py:703
  36.4 0.0 collective-permute-start.6
  36.4 2.9 %collective-permute-start.7 = (f32[22,56,128]{2,1,0:T(8,128)S(1)}, f32[22,56,128]{2,1,0:T(8,128)S(1)}, u32[]{:S(2)}, u32[]{:S(2)}) collective-permute-start(f32[22,56,128]{2,1,0:T(8,128)S(1)} %get-tuple-element.48.z_first), channel_id=1, source_target_pairs={{0,7},{1,0},{2,1},{3,2},{4,3},{5,4},{6,5},{7,6},{8,15},{9,8},{10,9... | collective-permute-start | bytes 1892360 | tf_op jit(solution)/shard_map/ppermute | solution.py:644
  39.4 5.8 %assemble.1 = (f32[6,52,56,128]{3,2,1,0:T(8,128)S(1)}, f32[52,72,128]{2,1,0:T(8,128)S(1)}, f32[52,56,128]{2,1,0:T(8,128)S(1)}) custom-call(f32[4,52,64,128]{3,2,1,0:T(8,128)S(1)} %get-tuple-element.45.ext), custom_call_target="tpu_custom_call" | custom-call | tf_op jit(solution)/shard_map/assemble/pallas_call | solution.py:709
  45.2 2.2 %collective-permute-done.6.z_lo = f32[22,56,128]{2,1,0:T(8,128)S(1)} collective-permute-done((f32[22,56,128]{2,1,0:T(8,128)S(1)}, f32[22,56,128]{2,1,0:T(8,128)S(1)}, u32[]{:S(2)}, u32[]{:S(2)}) %collective-permute-start.6) | collective-permute-done | bytes 630816 | tf_op jit(solution)/shard_map/ppermute | solution.py:644
  47.4 20.1 %solve.1 = (f32[3200,128]{1,0:T(8,128)S(1)}, f32[6,52,56,128]{3,2,1,0:T(8,128)S(1)}, f32[52,72,128]{2,1,0:T(8,128)S(1)}, f32[52,56,128]{2,1,0:T(8,128)S(1)}) custom-call(f32[6]{0:T(128)S(1)} %convert_element_type.3.edge, s32[1024]{0:T(1024)S(1)} %bitcast.14, ...), custom_call_target="tpu_custom_call", output_to_operand_aliasing={{1}: (13, {}), {2}: (14, {}), {3}: (15, {})} | custom-call | tf_op jit(solution)/shard_map/solve/pallas_call | solution.py:710
  67.5 33.8 %all_to_all.5 = f32[128,25,1,128]{3,2,1,0:T(1,128)S(1)} all-to-all(f32[128,25,1,128]{3,2,1,0:T(1,128)S(1)} %bitcast.12), channel_id=1, replica_groups=mesh['gx'=4,'gy'=4,'gz'=8] {'gx','gy','gz'}, dimensions={0} | all-to-all | bytes 3276800 | tf_op jit(solution)/shard_map/all_to_all | solution.py:736
  101.4 4.1 %unpack.1 = f32[3,640,128]{2,1,0:T(8,128)} custom-call(f32[3200,128]{1,0:T(8,128)S(1)} %bitcast.11), custom_call_target="tpu_custom_call" | custom-call | tf_op jit(solution)/shard_map/unpack/pallas_call | solution.py:739
  (29 shorter events, 0.1 us)
Async XLA Ops:
  0.0 14.2 %copy-start.6 = (f32[32,32,128]{2,1,0:T(8,128)S(1)}, f32[32,32,128]{2,1,0:T(8,128)}, u32[]{:S(2)}) copy-start(f32[32,32,128]{2,1,0:T(8,128)} %p.1) | copy-start | bytes 1572868
  0.0 12.7 %copy-start.12 = (s32[32,32,1]{1,2,0:T(1,128)S(1)}, s32[32,32,1]{1,2,0:T(1,128)}, u32[]{:S(2)}) copy-start(s32[32,32,1]{1,2,0:T(1,128)} %param.14) | copy-start | bytes 12292
  0.0 13.5 %copy-start.13 = (s32[32,32,1]{1,2,0:T(1,128)S(1)}, s32[32,32,1]{1,2,0:T(1,128)}, u32[]{:S(2)}) copy-start(s32[32,32,1]{1,2,0:T(1,128)} %param.15) | copy-start | bytes 12292
  4.7 19.9 %collective-permute-start = (f32[42,32,128]{2,1,0:T(8,128)}, f32[42,32,128]{2,1,0:T(8,128)S(1)}, u32[]{:S(2)}, u32[]{:S(2)}) collective-permute-start(f32[42,32,128]{2,1,0:T(8,128)} %get-tuple-element.30), channel_id=1, source_target_pairs={{0,32},{32,64},{64,96},{96,0},{1,33},{33,65},{65,97},{97,1},{2,34}... | collective-permute-start | bytes 2064392 | tf_op jit(solution)/shard_map/ppermute | solution.py:644
  6.8 17.8 %collective-permute-start.1 = (f32[42,32,128]{2,1,0:T(8,128)}, f32[42,32,128]{2,1,0:T(8,128)S(1)}, u32[]{:S(2)}, u32[]{:S(2)}) collective-permute-start(f32[42,32,128]{2,1,0:T(8,128)} %get-tuple-element.31), channel_id=1, source_target_pairs={{0,96},{32,0},{64,32},{96,64},{1,97},{33,1},{65,33},{97,65},{2,98}... | collective-permute-start | bytes 2064392 | tf_op jit(solution)/shard_map/ppermute | solution.py:644
  9.0 20.3 %collective-permute-start.4 = (f32[34,40,128]{2,1,0:T(8,128)}, f32[34,40,128]{2,1,0:T(8,128)}, u32[]{:S(2)}, u32[]{:S(2)}) collective-permute-start(f32[34,40,128]{2,1,0:T(8,128)} %get-tuple-element.37), channel_id=1, source_target_pairs={{0,8},{8,16},{16,24},{24,0},{1,9},{9,17},{17,25},{25,1},{2,10},{10... | collective-permute-start | bytes 2088968 | tf_op jit(solution)/shard_map/ppermute | solution.py:644
  10.5 18.8 %collective-permute-start.5 = (f32[34,40,128]{2,1,0:T(8,128)}, f32[34,40,128]{2,1,0:T(8,128)}, u32[]{:S(2)}, u32[]{:S(2)}) collective-permute-start(f32[34,40,128]{2,1,0:T(8,128)} %get-tuple-element.38), channel_id=1, source_target_pairs={{0,24},{8,0},{16,8},{24,16},{1,25},{9,1},{17,9},{25,17},{2,26},{10... | collective-permute-start | bytes 2088968 | tf_op jit(solution)/shard_map/ppermute | solution.py:644
  14.2 1.7 %copy-start.1 = (f32[5,32,32,128]{3,2,1,0:T(8,128)S(1)}, f32[5,32,32,128]{3,2,1,0:T(8,128)}, u32[]{:S(2)}) copy-start(f32[5,32,32,128]{3,2,1,0:T(8,128)} %get-tuple-element.33.own) | copy-start | bytes 7864324
  17.6 1.3 %copy-start.2 = (f32[4,32,32,128]{3,2,1,0:T(8,128)}, f32[4,32,32,128]{3,2,1,0:T(8,128)S(1)}, u32[]{:S(2)}) copy-start(f32[4,32,32,128]{3,2,1,0:T(8,128)S(1)} %get-tuple-element.39.turned) | copy-start | bytes 6291460
  19.0 1.0 copy-start.8
  20.0 0.8 copy-start.10
  22.4 6.9 %copy-start.9 = (f32[2,32,32,128]{3,2,1,0:T(8,128)S(1)}, f32[2,32,32,128]{3,2,1,0:T(8,128)}, u32[]{:S(2)}) copy-start(f32[2,32,32,128]{3,2,1,0:T(8,128)} %copy-done.8) | copy-start | bytes 3145732
  26.0 9.1 %collective-permute-start.2 = (f32[4,96,128]{2,1,0:T(8,128)}, f32[4,96,128]{2,1,0:T(8,128)S(1)}, u32[]{:S(2)}, u32[]{:S(2)}) collective-permute-start(f32[4,96,128]{2,1,0:T(8,128)} %get-tuple-element.35), channel_id=1, source_target_pairs={{0,8},{8,16},{16,24},{24,0},{1,9},{9,17},{17,25},{25,1},{2,10},{10... | collective-permute-start | bytes 589832 | tf_op jit(solution)/shard_map/ppermute | solution.py:644
  27.4 7.6 %collective-permute-start.3 = (f32[4,96,128]{2,1,0:T(8,128)}, f32[4,96,128]{2,1,0:T(8,128)S(1)}, u32[]{:S(2)}, u32[]{:S(2)}) collective-permute-start(f32[4,96,128]{2,1,0:T(8,128)} %get-tuple-element.36), channel_id=1, source_target_pairs={{0,24},{8,0},{16,8},{24,16},{1,25},{9,1},{17,9},{25,17},{2,26},{10... | collective-permute-start | bytes 589832 | tf_op jit(solution)/shard_map/ppermute | solution.py:644
  29.3 1.6 %copy-start.3 = (f32[4,32,32,128]{3,2,1,0:T(8,128)S(1)}, f32[4,32,32,128]{3,2,1,0:T(8,128)}, u32[]{:S(2)}) copy-start(f32[4,32,32,128]{3,2,1,0:T(8,128)} %copy-done.2) | copy-start | bytes 6291460
  30.9 1.1 %copy-start.11 = (f32[22,56,128]{2,1,0:T(8,128)S(1)}, f32[22,56,128]{2,1,0:T(8,128)}, u32[]{:S(2)}) copy-start(f32[22,56,128]{2,1,0:T(8,128)} %copy-done.10) | copy-start | bytes 1892356
  36.4 11.0 %collective-permute-start.6 = (f32[22,56,128]{2,1,0:T(8,128)S(1)}, f32[22,56,128]{2,1,0:T(8,128)S(1)}, u32[]{:S(2)}, u32[]{:S(2)}) collective-permute-start(f32[22,56,128]{2,1,0:T(8,128)S(1)} %get-tuple-element.47.z_last), channel_id=1, source_target_pairs={{0,1},{1,2},{2,3},{3,4},{4,5},{5,6},{6,7},{7,0},{8,9},{9,10},{10,1... | collective-permute-start | bytes 1892360 | tf_op jit(solution)/shard_map/ppermute | solution.py:644
  36.4 10.9 %collective-permute-start.7 = (f32[22,56,128]{2,1,0:T(8,128)S(1)}, f32[22,56,128]{2,1,0:T(8,128)S(1)}, u32[]{:S(2)}, u32[]{:S(2)}) collective-permute-start(f32[22,56,128]{2,1,0:T(8,128)S(1)} %get-tuple-element.48.z_first), channel_id=1, source_target_pairs={{0,7},{1,0},{2,1},{3,2},{4,3},{5,4},{6,5},{7,6},{8,15},{9,8},{10,9... | collective-permute-start | bytes 1892360 | tf_op jit(solution)/shard_map/ppermute | solution.py:644
  39.4 8.0 %copy-start = (f32[2,32,32,128]{3,2,1,0:T(8,128)S(1)}, f32[2,32,32,128]{3,2,1,0:T(8,128)}, u32[]{:S(2)}) copy-start(f32[2,32,32,128]{3,2,1,0:T(8,128)} %sat.1) | copy-start | bytes 3145732
  39.4 8.0 %copy-start.4 = (f32[32,32,128]{2,1,0:T(8,128)S(1)}, f32[32,32,128]{2,1,0:T(8,128)}, u32[]{:S(2)}) copy-start(f32[32,32,128]{2,1,0:T(8,128)} %sto.1) | copy-start | bytes 1572868
  39.4 8.0 %copy-start.5 = (s32[32,32,128]{2,1,0:T(8,128)S(1)}, s32[32,32,128]{2,1,0:T(8,128)}, u32[]{:S(2)}) copy-start(s32[32,32,128]{2,1,0:T(8,128)} %mask.1) | copy-start | bytes 1572868
  39.4 8.0 %copy-start.7 = (f32[2,32,32,128]{3,2,1,0:T(8,128)S(1)}, f32[2,32,32,128]{3,2,1,0:T(8,128)}, u32[]{:S(2)}) copy-start(f32[2,32,32,128]{3,2,1,0:T(8,128)} %old.1) | copy-start | bytes 3145732
